TPU v7x, 32 devices: a whole 2x2x4 slice. The times are simulated.
32 devices in a mesh: req: 8 (over z, x), head: 4 (over y, core).
Axes of the slice: x: 2, y: 2, z: 4, core: 2. Of those that a mesh axis runs over, the one named last changes fastest.
Arguments:
- hidden: bfloat16 [56, 2048], P('req'), may hold values from -6 to 6
- queries: bfloat16 [56, 16, 576], P('req', 'head'), may hold values from -48 to 48
- latent_cache: bfloat16 [64, 128, 576], P(('req', 'head')), may hold values from -6 to 6
- page_table: int32 [56, 2], P('req'), may hold values from 0 to 7, as said below
- seq_lens: int32 [56], P('req'), may hold values from 2 to 256, as said below
- value_up: bfloat16 [16, 512, 128], P('head'), may hold values from -0.25 to 0.25
- out_proj: bfloat16 [2048, 2048], P('head'), may hold values from -0.125 to 0.125
- norm_gain: float32 [2048], replicated, may hold values from 0.25 to 1.75
- expert_ids: int32 [56, 6], P('req'), may hold values from 0 to 63, all different within a row; in each aligned block of 7 rows (0 to 6, 7 to 13, ...) at most 2 rows name the same one
- expert_mix: float32 [56, 6], P('req'), may hold values from 0.2 to 1
- gate_weight: bfloat16 [128, 2048, 704], P('req', None, 'head'), may hold values from -0.125 to 0.125
- up_weight: bfloat16 [128, 2048, 704], P('req', None, 'head'), may hold values from -0.125 to 0.125
- down_weight: bfloat16 [128, 704, 2048], P('req', 'head'), may hold values from -0.15625 to 0.15625
Outputs:
- layer_out: bfloat16 [56, 2048], P('req', 'head')
Inputs may be any that keep to these rules, and one draw needn't show every extreme that they name: `page_table`: rows g * 7 to g * 7 + 6 form group g. The first ceil(seq_lens / 128) entries of a row are distinct pages, no page serves two requests of a group, and the remaining entries repeat the row's first page. `seq_lens`: the pages that the requests of one group need sum to at most 8. `expert_ids`: among the 7 rows of one device, at most 2 name the same expert.
All inputs are finite; a program needn't handle non-finite values.
Results may differ from a plain program's by a relative error of at most 0.02.
Values may be sent and summed in bfloat16 or wider, within the bound.
No kernel may reach another device: no remote copies, remote signals or barrier semaphores. Data moves between devices by JAX's collectives and lax.ppermute only.
A program may use at most 64 MiB of HBM per device.

v0:
```python
import math

import jax
import jax.numpy as jnp
from jax import lax
from jax.sharding import PartitionSpec as P

RANK = 512
ROPE = 64
NOPE = 128
VHEAD = 128
EXPERTS = 64
TOP = 6
PAGE = 128
CAP = 2


norm_eps = 1e-06
masked_low = -1e30


def joined(value, axis, join):
    pieces = jax.tree.map(lambda part: lax.all_gather(part, axis), value)
    head = jax.tree.map(lambda part: part[0], pieces)
    tail = jax.tree.map(lambda part: part[1:], pieces)
    total, _ = lax.scan(lambda total, share: (join(total, share), None), head, tail)
    return total


def combine_parts(earlier_part, later_part):
    high_a, total_a, summed_a = earlier_part
    high_b, total_b, summed_b = later_part
    highest = jnp.maximum(high_a, high_b)
    factor_a = jnp.exp(high_a - highest)
    factor_b = jnp.exp(high_b - highest)
    return (
        highest,
        total_a * factor_a + total_b * factor_b,
        summed_a * factor_a[..., None] + summed_b * factor_b[..., None],
    )


def per_device(
    hidden,
    queries,
    latent_cache,
    page_table,
    seq_lens,
    value_up,
    out_proj,
    norm_gain,
    expert_ids,
    expert_mix,
    gate_weight,
    up_weight,
    down_weight,
):
    head_count = lax.axis_size("head")
    head_at = lax.axis_index("head")
    req_count = lax.axis_size("req")
    requests = hidden.shape[0]
    local_heads = queries.shape[1]
    pages_here = latent_cache.shape[0]
    table_width = page_table.shape[1]
    quarter = hidden.shape[1] // head_count
    everyone = lax.all_gather(queries, "head", axis=1, tiled=True)
    page_ids = head_at * pages_here + jnp.arange(pages_here)
    needed = (seq_lens + PAGE - 1) // PAGE
    entries = jnp.arange(table_width)
    in_use = entries[None, :] < needed[:, None]
    matches = (page_table[:, :, None] == page_ids[None, None, :]) & in_use[:, :, None]
    page_slot = jnp.sum(jnp.where(matches, entries[None, :, None], 0), axis=1)
    present = jnp.any(matches, axis=1)
    within = jnp.arange(PAGE)
    valid = present[:, :, None] & (
        page_slot[:, :, None] * PAGE + within[None, None, :] < seq_lens[:, None, None]
    )
    valid = valid.reshape(requests, pages_here * PAGE)
    flat_cache = latent_cache.reshape(pages_here * PAGE, latent_cache.shape[2])
    scale = 1.0 / math.sqrt(NOPE + ROPE)
    scores = (
        jnp.einsum("rhc,tc->rht", everyone, flat_cache, preferred_element_type=jnp.float32) * scale
    )
    masked = jnp.where(valid[:, None, :], scores, masked_low)
    highest = jnp.max(masked, axis=-1)
    weights = jnp.where(valid[:, None, :], jnp.exp(masked - highest[..., None]), 0.0)
    totals = jnp.sum(weights, axis=-1)
    latent = flat_cache[:, :RANK].astype(jnp.float32)
    summed = jnp.einsum("rht,tc->rhc", weights, latent, precision=lax.Precision.HIGHEST)
    merged = joined((highest, totals, summed), "head", combine_parts)
    lower = head_at * local_heads
    mine_total = lax.dynamic_slice_in_dim(merged[1], lower, local_heads, 1)
    mine_summed = lax.dynamic_slice_in_dim(merged[2], lower, local_heads, 1)
    attended = (mine_summed / mine_total[..., None]).astype(jnp.bfloat16)
    head_out = jnp.einsum(
        "rhc,hcv->rhv", attended, value_up, preferred_element_type=jnp.float32
    ).astype(jnp.bfloat16)
    head_out = head_out.reshape(requests, local_heads * VHEAD)
    partial_out = jnp.dot(head_out, out_proj, preferred_element_type=jnp.float32)
    attn_out = lax.psum(partial_out.astype(jnp.bfloat16), "head").astype(jnp.float32)
    mixed = hidden.astype(jnp.float32) + attn_out
    spread = jnp.mean(mixed * mixed, axis=-1, keepdims=True)
    normed = (mixed * lax.rsqrt(spread + norm_eps) * norm_gain).astype(jnp.bfloat16)
    slots_here = gate_weight.shape[0]
    pair_count = requests * TOP
    flat_experts = expert_ids.reshape(pair_count)
    pair_index = jnp.arange(pair_count)
    earlier = (flat_experts[:, None] == flat_experts[None, :]) & (
        pair_index[None, :] < pair_index[:, None]
    )
    position = jnp.sum(earlier.astype(jnp.int32), axis=1)
    slot_total = 2 * EXPERTS * CAP
    slot_ids = jnp.arange(slot_total)
    target_low = 2 * flat_experts * CAP + position
    target_high = (2 * flat_experts + 1) * CAP + position
    slot_hits = (
        (slot_ids[:, None] == target_low[None, :]) | (slot_ids[:, None] == target_high[None, :])
    ).astype(jnp.float32)
    owner = pair_index // TOP
    token_hits = (owner[:, None] == jnp.arange(requests)[None, :]).astype(jnp.float32)
    route = jnp.dot(slot_hits, token_hits, precision=lax.Precision.HIGHEST)
    mix_route = jnp.dot(
        slot_hits,
        token_hits * expert_mix.reshape(pair_count)[:, None],
        precision=lax.Precision.HIGHEST,
    )
    own_mixed = lax.dynamic_slice_in_dim(mixed, head_at * quarter, quarter, 1)
    packed = jnp.dot(route.astype(jnp.bfloat16), normed, preferred_element_type=jnp.float32).astype(
        jnp.bfloat16
    )
    packed = packed.reshape(req_count, slots_here, CAP, normed.shape[1])
    full_rows = lax.all_to_all(packed, "req", split_axis=0, concat_axis=0, tiled=True)
    gate_part = jnp.einsum(
        "nsid,sdf->nsif", full_rows, gate_weight, preferred_element_type=jnp.float32
    )
    up_part = jnp.einsum("nsid,sdf->nsif", full_rows, up_weight, preferred_element_type=jnp.float32)
    active = (jax.nn.silu(gate_part) * up_part).astype(jnp.bfloat16)
    summed_out = lax.psum(
        jnp.einsum(
            "nsif,sfd->nsid", active, down_weight, preferred_element_type=jnp.float32
        ).astype(jnp.bfloat16),
        "head",
    )
    returned = lax.all_to_all(summed_out, "req", split_axis=0, concat_axis=0, tiled=True)
    returned = returned.reshape(slot_total, normed.shape[1]).astype(jnp.float32)
    routed_full = jnp.dot(mix_route.T, returned, precision=lax.Precision.HIGHEST)
    routed = lax.dynamic_slice_in_dim(routed_full, head_at * quarter, quarter, 1)
    return (own_mixed + routed).astype(jnp.bfloat16)


def solution(mesh):
    return jax.shard_map(
        per_device,
        mesh=mesh,
        in_specs=(
            P("req", None),
            P("req", "head", None),
            P(("req", "head"), None, None),
            P("req", None),
            P("req"),
            P("head", None, None),
            P("head", None),
            P(),
            P("req", None),
            P("req", None),
            P("req", None, "head"),
            P("req", None, "head"),
            P("req", "head", None),
        ),
        out_specs=P("req", "head"),
        check_vma=False,
    )
```

profile of v0, /device:TPU:0, one launch (start us, length us, event | category | flops | bytes accessed | tf_op | source)
XLA Modules:
  0.0 187.4 jit_solution(17942914670669561649)
XLA Ops:
  6.6 0.8 and_select_fusion.1
  7.4 0.8 fusion.70
  8.2 0.8 fusion.69
  9.1 1.2 copy.36
  10.3 0.8 copy.35
  11.1 6.7 %all_gather.21 = bf16[7,16,576]{2,0,1:T(8,128)(2,1)S(1)} all-gather(bf16[7,4,576]{2,0,1:T(8,128)(2,1)S(1)} %copy.35), channel_id=1, replica_groups=mesh['req'=8,'head'=4] {'head'}, dimensions={1}, use_global_device_ids=true | all-gather | bytes 161280 | tf_op jit(solution)/shard_map/all_gather | solution.py:66
  17.7 0.7 fusion.67
  19.1 9.6 %all-gather.2 = f32[28,16,512]{2,1,0:T(8,128)S(1)} all-gather(f32[7,16,512]{2,1,0:T(8,128)S(1)} %fusion.35), channel_id=4, replica_groups=mesh['req'=8,'head'=4] {'head'}, dimensions={0}, use_global_device_ids=true | all-gather | bytes 1146880 | tf_op jit(solution)/shard_map/all_gather | solution.py:23
  29.0 5.2 %all-gather.4 = f32[4,7,16]{2,1,0:T(8,128)S(1)} all-gather(f32[1,7,16]{2,1,0:T(8,128)S(1)} %bitcast.101), channel_id=3, replica_groups=mesh['req'=8,'head'=4] {'head'}, dimensions={0}, use_global_device_ids=true | all-gather | bytes 2240 | tf_op jit(solution)/shard_map/all_gather | solution.py:23
  34.2 5.2 %all-gather.3 = f32[4,7,16]{2,1,0:T(8,128)S(1)} all-gather(f32[1,7,16]{2,1,0:T(8,128)S(1)} %bitcast.100), channel_id=2, replica_groups=mesh['req'=8,'head'=4] {'head'}, dimensions={0}, use_global_device_ids=true | all-gather | bytes 2240 | tf_op jit(solution)/shard_map/all_gather | solution.py:23
  40.0 1.5 convolution_convert_fusion.1
  41.6 11.7 %psum.14 = bf16[7,2048]{1,0:T(8,128)(2,1)S(1)} all-reduce(bf16[7,2048]{1,0:T(8,128)(2,1)S(1)} %convolution_convert_fusion.1), channel_id=1, replica_groups=mesh['req'=8,'head'=4] {'head'}, use_global_device_ids=true, to_apply=%region_6.7 | all-reduce | flops 14336 | bytes 57344 | tf_op jit(solution)/shard_map/psum | solution.py:100
  53.9 0.5 convolution_convert_fusion
  54.4 1.5 reshape.124
  56.0 30.7 %all_to_all.10 = bf16[8,16,2,2048]{3,2,1,0:T(2,128)(2,1)S(1)} all-to-all(bf16[8,16,2,2048]{3,2,1,0:T(2,128)(2,1)} %reshape.124), channel_id=1, replica_groups=mesh['req'=8,'head'=4] {'req'}, dimensions={0} | all-to-all | bytes 2097152 | tf_op jit(solution)/shard_map/all_to_all | solution.py:132
  86.6 7.3 %fusion.15 = f32[8,16,2,176]{3,0,2,1:T(8,128)S(1)} fusion(bf16[16,2048,176]{1,2,0:T(8,128)(2,1)} %param.25, bf16[8,16,2,2048]{3,2,1,0:T(2,128)(2,1)S(1)} %all_to_all.10), kind=kOutput, calls=%fused_computation.18 | convolution fusion | flops 184549376 | bytes 12763136 | tf_op jit(solution)/shard_map/nsid,sdf->nsif/dot_general | solution.py:133
  94.0 13.2 %fusion.12 = bf16[8,16,2,2048]{3,0,2,1:T(8,128)(2,1)} fusion(bf16[16,176,2048]{2,1,0:T(8,128)(2,1)} %param.27, bf16[16,2048,176]{1,2,0:T(8,128)(2,1)} %param.26, bf16[8,16,2,2048]{3,2,1,0:T(2,128)(2,1)S(1)} %all_to_all.10, f32[8,16,2,176]{3,0,2,1:T(8,128)S(1)} %fusion.15), kind=kOutput, calls=%fused_computation.16 | convolution fusion | flops 369893376 | bytes 25346048 | tf_op jit(solution)/shard_map/nsif,sfd->nsid/dot_general | solution.py:139
  107.2 35.4 %all-reduce.2.cloned.1.call-done = bf16[8,16,2,2048]{3,0,2,1:T(8,128)(2,1)} async-done(((bf16[8,16,2,2048]{3,0,2,1:T(8,128)(2,1)}), bf16[8,16,2,2048]{3,0,2,1:T(8,128)(2,1)}) %all-reduce.2.cloned.1.call-update) | async-done | bytes 1048592 | tf_op jit(solution)/shard_map/psum | solution.py:138
  142.6 3.3 %copy.42 = bf16[8,16,2,2048]{3,2,1,0:T(2,128)(2,1)} copy(bf16[8,16,2,2048]{3,0,2,1:T(8,128)(2,1)} %all-reduce.2.cloned.1.call-done) | data formatting | bytes 2097152 | tf_op jit(solution)/shard_map/psum | solution.py:138
  145.9 5.5 %all-to-all-start.1 = ((bf16[8,16,2,2048]{3,2,1,0:T(2,128)(2,1)}), bf16[8,16,2,2048]{3,2,1,0:T(2,128)(2,1)S(1)}, u32[]{:S(2)}, u32[]{:S(2)}) async-start(bf16[8,16,2,2048]{3,2,1,0:T(2,128)(2,1)} %copy.42), calls=%async_computation.1 | async-start | bytes 2097152 | tf_op jit(solution)/shard_map/all_to_all | solution.py:144
  151.8 25.2 %all-to-all-done.1 = bf16[8,16,2,2048]{3,2,1,0:T(2,128)(2,1)S(1)} async-done(((bf16[8,16,2,2048]{3,2,1,0:T(2,128)(2,1)}), bf16[8,16,2,2048]{3,2,1,0:T(2,128)(2,1)S(1)}, u32[]{:S(2)}, u32[]{:S(2)}) %all-to-all-start.1) | async-done | bytes 1048608 | tf_op jit(solution)/shard_map/all_to_all | solution.py:144
  177.0 1.2 reshape.125
  178.2 1.7 fusion.76
  179.9 0.6 add_convert_fusion
  (45 shorter events, 3.2 us)
Async XLA Ops:
  6.5 33.5 %copy-start = (bf16[512,2048]{1,0:T(8,128)(2,1)S(1)}, bf16[512,2048]{1,0:T(8,128)(2,1)}, u32[]{:S(2)}) copy-start(bf16[512,2048]{1,0:T(8,128)(2,1)} %param.21) | copy-start | bytes 6291460
  6.5 46.7 %copy-start.1 = (bf16[7,2048]{1,0:T(8,128)(2,1)S(1)}, bf16[7,2048]{1,0:T(8,128)(2,1)}, u32[]{:S(2)}) copy-start(bf16[7,2048]{1,0:T(8,128)(2,1)} %param.15) | copy-start | bytes 86020
  6.5 46.9 %copy-start.3 = (s32[7,6]{1,0:T(8,128)S(1)}, s32[7,6]{1,0:T(8,128)}, u32[]{:S(2)}) copy-start(s32[7,6]{1,0:T(8,128)} %param.23) | copy-start | bytes 508
  6.5 47.4 %copy-start.2 = (f32[2048]{0:T(1024)S(1)}, f32[2048]{0:T(1024)}, u32[]{:S(2)}) copy-start(f32[2048]{0:T(1024)} %param.22) | copy-start | bytes 24580
  6.5 136.1 %all-reduce.2.cloned.1.call-start = ((), (), s32[]{:S(2)}) async-start(), calls=%async_computation.2 | async-start | bytes 2097152 | tf_op jit(solution)/shard_map/psum | solution.py:138
  94.0 57.5 %copy-start.4 = (f32[7,6]{1,0:T(8,128)S(1)}, f32[7,6]{1,0:T(8,128)}, u32[]{:S(2)}) copy-start(f32[7,6]{1,0:T(8,128)} %param.24) | copy-start | bytes 508
  145.9 31.0 %all-to-all-start.1 = ((bf16[8,16,2,2048]{3,2,1,0:T(2,128)(2,1)}), bf16[8,16,2,2048]{3,2,1,0:T(2,128)(2,1)S(1)}, u32[]{:S(2)}, u32[]{:S(2)}) async-start(bf16[8,16,2,2048]{3,2,1,0:T(2,128)(2,1)} %copy.42), calls=%async_computation.1 | async-start | bytes 2097152 | tf_op jit(solution)/shard_map/all_to_all | solution.py:144
Sparse Core Ops, SparseCore 0:
  107.3 35.2 all-reduce.1
where the time goes:
time: 188 us; the launch traced here: 187 us
  blocking collectives  69 us (37%)
  waiting for transfers between devices  60.6 us (32%)
  matrix products  25.5 us (14%)
  between operations  13.5 us (7%)
  local copies, waits for them, and re-layouts  8.51 us (5%)
  starting transfers between devices  5.54 us (3%)
  other arithmetic  4.66 us (2%)
    psum x1, waiting for transfers between devices, per_device(): lax.psum(jnp.einsum('nsif,sfd->nsid', active, down_weight, preferred_elem...  35.4 us
    all_to_all x1, blocking collectives, per_device(): lax.all_to_all(packed, 'req', split_axis=0, concat_axis=0, tiled=True)  30.7 us
    all_to_all x1, waiting for transfers between devices, per_device(): lax.all_to_all(summed_out, 'req', split_axis=0, concat_axis=0, tiled=True)  25.2 us
    all_gather x3, blocking collectives, joined(): pieces = jax.tree.map(lambda part: lax.all_gather(part, axis), value)  20 us
    dot_general x1, matrix products, per_device(): jnp.einsum('nsif,sfd->nsid', active, down_weight, preferred_element_type=...  13.2 us
    psum x1, blocking collectives, per_device(): lax.psum(partial_out.astype(jnp.bfloat16), 'head').astype(jnp.float32)  11.7 us
    dot_general x1, matrix products, per_device(): jnp.einsum('nsid,sdf->nsif', full_rows, gate_weight, preferred_element_ty...  7.35 us
    all_gather x1, blocking collectives, per_device(): everyone = lax.all_gather(queries, 'head', axis=1, tiled=True)  6.67 us
  transfers between devices with their start and end apart: 2, of which 2 were waited for; matrix products, arithmetic and copies ran while one was open for 0% of the time, Pallas kernels for 0%

commit v1 on v0

v1 whole, which is shorter than its diff:
```python
import functools
import math

import jax
import jax.numpy as jnp
from jax import lax
from jax.experimental import pallas as pl
from jax.experimental.pallas import tpu as pltpu
from jax.sharding import PartitionSpec as P

RANK = 512
ROPE = 64
NOPE = 128
VHEAD = 128
EXPERTS = 64
TOP = 6
PAGE = 128
LANES = 128
ROWS = 8

norm_eps = 1e-06
masked_low = -1e30

f32 = jnp.float32
bf16 = jnp.bfloat16
NT = (((1,), (1,)), ((), ()))
VMEM = pl.BlockSpec(memory_space=pltpu.VMEM)
SMEM = pl.BlockSpec(memory_space=pltpu.SMEM)
ANY = pl.BlockSpec(memory_space=pl.ANY)


def split3(value):
    high = value.astype(bf16).astype(f32)
    rest = value - high
    middle = rest.astype(bf16).astype(f32)
    return high, middle, (rest - middle).astype(bf16).astype(f32)


def attend_kernel(
    table,
    lens,
    ids,
    mix,
    q_own,
    q_far,
    cache_own,
    cache_near,
    own_out,
    own_lse,
    far_out,
    route_out,
    q_all,
    weighted,
    lse_all,
):
    head_at = lax.axis_index("head")
    requests, heads, width = q_own.shape
    pages_here = cache_own.shape[0]
    q_all[...] = jnp.zeros_like(q_all)
    for r in range(requests):
        q_all[r * ROWS : r * ROWS + heads, :] = q_own[r].astype(f32)
        q_all[r * ROWS + heads : r * ROWS + 2 * heads, :] = q_far[r].astype(f32)
    q_rows = q_all[...].astype(bf16)
    total_rows = q_all.shape[0]
    row_request = lax.broadcasted_iota(jnp.int32, (total_rows, PAGE), 0) // ROWS
    within = lax.broadcasted_iota(jnp.int32, (total_rows, PAGE), 1)
    scale = 1.0 / math.sqrt(NOPE + ROPE)
    keys, valids, scores = [], [], []
    for side, cache in ((0, cache_own), (1, cache_near)):
        holder = head_at if side == 0 else head_at ^ 1
        for p in range(pages_here):
            page = holder * pages_here + p
            owner = jnp.int32(-1)
            count = jnp.int32(0)
            for r in range(requests):
                for m in range(table.shape[1]):
                    left = lens[r] - m * PAGE
                    hit = jnp.logical_and(table[r, m] == page, left > 0)
                    owner = jnp.where(hit, r, owner)
                    count = jnp.where(hit, left, count)
            valid = (row_request == owner) & (within < count)
            keys.append(cache.at[p])
            valids.append(valid)
            score = jnp.dot(q_rows, cache[p], preferred_element_type=f32) * scale
            scores.append(jnp.where(valid, score, masked_low))
    highest = functools.reduce(jnp.maximum, scores).max(axis=-1, keepdims=True)
    total = jnp.zeros((total_rows, 1), f32)
    summed = jnp.zeros((total_rows, RANK), f32)
    for key, valid, score in zip(keys, valids, scores):
        weight = jnp.where(valid, jnp.exp(score - highest), 0.0)
        total = total + jnp.sum(weight, axis=-1, keepdims=True)
        high = weight.astype(bf16)
        low = (weight - high.astype(f32)).astype(bf16)
        latent = key[:RANK, :]
        summed = summed + lax.dot_general(high, latent, NT, preferred_element_type=f32)
        summed = summed + lax.dot_general(low, latent, NT, preferred_element_type=f32)
    some = total > 0.0
    safe = jnp.where(some, total, 1.0)
    summed = summed * (1.0 / safe)
    for c in range(RANK // LANES):
        weighted[c] = summed[:, c * LANES : (c + 1) * LANES]
    lse = jnp.where(some, highest + jnp.log(safe), masked_low)
    lse_all[...] = jnp.broadcast_to(lse, lse_all.shape)
    lane = lax.broadcasted_iota(jnp.int32, (ROWS, 128), 1)
    for h in range(heads):
        own_lse[h] = lse_all[pl.ds(h, ROWS, stride=ROWS), :]
        for c in range(RANK // LANES):
            span = slice(c * LANES, (c + 1) * LANES)
            own_out[h, :, span] = weighted[c, pl.ds(h, ROWS, stride=ROWS), :]
            far_out[h, :, span] = weighted[c, pl.ds(heads + h, ROWS, stride=ROWS), :].astype(bf16)
        high, middle, low = split3(lse_all[pl.ds(heads + h, ROWS, stride=ROWS), :])
        far_out[h, :, RANK:] = jnp.where(
            lane == 0, high, jnp.where(lane == 1, middle, jnp.where(lane == 2, low, 0.0))
        ).astype(bf16)
    lanes = lax.broadcasted_iota(jnp.int32, route_out.shape, 1)
    row = jnp.zeros(route_out.shape, f32)
    for r in range(requests):
        for i in range(TOP):
            row = jnp.where(lanes == r * EXPERTS + ids[r, i], mix[r, i], row)
    high, middle, low = split3(row)
    route_out[...] = jnp.where(
        head_at == 0, high, jnp.where(head_at == 1, middle, jnp.where(head_at == 2, low, 0.0))
    )


def project_kernel(own, own_lse, far, value_up, out_proj, mine, near, far_y, far_both, whole):
    heads = own.shape[0]
    head_at = lax.axis_index("head")
    parts = []
    for h in range(heads):
        stats = far[h, :, RANK:].astype(f32)
        lse_far = stats[:, 0:1] + stats[:, 1:2] + stats[:, 2:3]
        lse_own = own_lse[h][:, 0:1]
        highest = jnp.maximum(lse_own, lse_far)
        weight_own = jnp.exp(lse_own - highest)
        weight_far = jnp.exp(lse_far - highest)
        merged = weight_own * own[h] + weight_far * far[h, :, :RANK].astype(f32)
        attended = (merged * (1.0 / (weight_own + weight_far))).astype(bf16)
        parts.append(jnp.dot(attended, value_up[h], preferred_element_type=f32))
    head_out = jnp.concatenate(parts, axis=1).astype(bf16)
    whole[...] = jnp.dot(head_out, out_proj[...], preferred_element_type=f32)
    quarter = mine.shape[1]
    mine[...] = whole[:, pl.ds(pl.multiple_of(head_at * quarter, quarter), quarter)]
    for out, flip in ((near, 1), (far_y, 2), (far_both, 3)):
        start = pl.multiple_of((head_at ^ flip) * quarter, quarter)
        out[...] = whole[:, pl.ds(start, quarter)].astype(bf16)


def mix_kernel(mine, near, far_y, far_both, hidden, route, mixed_out, spread_out):
    head_at = lax.axis_index("head")
    requests = hidden.shape[0]
    quarter = mine.shape[1]
    start = pl.multiple_of(head_at * quarter, quarter)
    attn = mine[...] + near[...].astype(f32) + far_y[...].astype(f32) + far_both[...].astype(f32)
    residual = hidden[:, pl.ds(start, quarter)].astype(f32)
    mixed_out[...] = attn[:requests] + residual
    row = lax.broadcasted_iota(jnp.int32, (ROWS, quarter), 0)
    padded = jnp.concatenate(
        [residual, jnp.zeros((ROWS - requests, quarter), f32)], axis=0
    )
    block = jnp.where(row < requests, attn + padded, route[...]).astype(bf16)
    for n in range(spread_out.shape[0]):
        spread_out[n] = block


def expert_kernel(
    chunk,
    tokens,
    gain,
    gate,
    up,
    down,
    out,
    rows_all,
    mix_all,
    total,
    gate_buf,
    up_buf,
    down_buf,
    sems,
):
    req_count = lax.axis_size("req")
    head_count = lax.axis_size("head")
    req_at = lax.axis_index("req")
    slots, depth, model = gate.shape
    quarter = tokens.shape[2]
    requests = ROWS - 1
    live = requests * req_count
    units = slots * depth
    steps = units // chunk
    flat = [w.reshape(units, model) for w in (gate, up, down)]

    def copies(step):
        slot = step % 2
        return [
            pltpu.make_async_copy(
                w.at[pl.ds(step * chunk, chunk), :], buf.at[slot], sems.at[n, slot]
            )
            for n, (w, buf) in enumerate(zip(flat, (gate_buf, up_buf, down_buf)))
        ]

    for copy in copies(0):
        copy.start()
    for i in range(req_count):
        for j in range(head_count):
            block = tokens[i * head_count + j].astype(f32)
            for c in range(quarter // LANES):
                rows_all[j * quarter // LANES + c, pl.ds(i, ROWS, stride=req_count), :] = block[
                    :, c * LANES : (c + 1) * LANES
                ]
    for r in range(requests):
        for k in range(3):
            start = k * quarter + r * EXPERTS
            lane = start % LANES
            mix_all[r * req_count : (r + 1) * req_count, k * EXPERTS : (k + 1) * EXPERTS] = rows_all[
                start // LANES, live : live + req_count, lane : lane + EXPERTS
            ]
    mixed = jnp.concatenate([rows_all[c, :live, :] for c in range(model // LANES)], axis=1)
    spread = jnp.mean(mixed * mixed, axis=-1, keepdims=True)
    normed = (mixed * lax.rsqrt(spread + norm_eps) * gain[...]).astype(bf16)
    mix_rows = mix_all[...].astype(bf16)
    for step in range(steps):
        slot = step % 2
        if step + 1 < steps:
            for copy in copies(step + 1):
                copy.start()
        for copy in copies(step):
            copy.wait()
        unit = step * chunk + lax.broadcasted_iota(jnp.int32, (3 * EXPERTS, chunk), 1)
        expert = lax.broadcasted_iota(jnp.int32, (3 * EXPERTS, chunk), 0) % EXPERTS
        here = expert == (req_at * slots + unit // depth) // 2
        weight = jnp.dot(
            mix_rows, jnp.where(here, 1.0, 0.0).astype(bf16), preferred_element_type=f32
        )
        gate_part = lax.dot_general(normed, gate_buf[slot], NT, preferred_element_type=f32)
        up_part = lax.dot_general(normed, up_buf[slot], NT, preferred_element_type=f32)
        active = gate_part / (1.0 + jnp.exp(-gate_part)) * up_part * weight
        product = jnp.dot(active.astype(bf16), down_buf[slot], preferred_element_type=f32)
        for c in range(model // LANES):
            share = product[:, c * LANES : (c + 1) * LANES]
            total[c, :live, :] = share if step == 0 else total[c, :live, :] + share
    for c in range(model // LANES):
        total[c, live:, :] = jnp.zeros((req_count, LANES), f32)
    for i in range(req_count):
        for j in range(head_count):
            for c in range(quarter // LANES):
                out[i * head_count + j, :, c * LANES : (c + 1) * LANES] = total[
                    j * quarter // LANES + c, pl.ds(i, ROWS, stride=req_count), :
                ].astype(bf16)


def final_kernel(parts, mixed, out):
    total = jnp.sum(parts[...].astype(f32), axis=0)
    out[...] = (mixed[...] + total[: mixed.shape[0]]).astype(bf16)


def limit(mebibytes):
    return pltpu.CompilerParams(vmem_limit_bytes=mebibytes * 2**20)


def per_device(
    hidden,
    queries,
    latent_cache,
    page_table,
    seq_lens,
    value_up,
    out_proj,
    norm_gain,
    expert_ids,
    expert_mix,
    gate_weight,
    up_weight,
    down_weight,
):
    head_count = lax.axis_size("head")
    req_count = lax.axis_size("req")
    both = ("req", "head")
    requests, heads, width = queries.shape
    model = hidden.shape[1]
    quarter = model // head_count
    devices = req_count * head_count
    assert head_count == 4 and requests == ROWS - 1 and requests * EXPERTS <= quarter

    def swap(value, flip):
        return lax.ppermute(value, "head", [(n, n ^ flip) for n in range(head_count)])

    cache = jnp.swapaxes(latent_cache, 1, 2)
    q_far = swap(queries, 2)
    cache_near = swap(cache, 1)
    rows = ROWS * ROWS
    own, own_lse, far, route = pl.pallas_call(
        attend_kernel,
        out_shape=(
            jax.ShapeDtypeStruct((heads, ROWS, RANK), f32),
            jax.ShapeDtypeStruct((heads, ROWS, 128), f32),
            jax.ShapeDtypeStruct((heads, ROWS, RANK + 128), bf16),
            jax.ShapeDtypeStruct((1, quarter), f32),
        ),
        in_specs=[SMEM] * 4 + [VMEM] * 4,
        out_specs=[VMEM] * 4,
        scratch_shapes=[
            pltpu.VMEM((rows, width), f32),
            pltpu.VMEM((RANK // LANES, rows, LANES), f32),
            pltpu.VMEM((rows, LANES), f32),
        ],
        compiler_params=limit(8),
        name="attend",
    )(page_table, seq_lens, expert_ids, expert_mix, queries, q_far, cache, cache_near)
    far = swap(far, 2)
    piece = jax.ShapeDtypeStruct((ROWS, quarter), bf16)
    mine, near, far_y, far_both = pl.pallas_call(
        project_kernel,
        out_shape=(jax.ShapeDtypeStruct((ROWS, quarter), f32), piece, piece, piece),
        in_specs=[VMEM] * 5,
        out_specs=[VMEM] * 4,
        scratch_shapes=[pltpu.VMEM((ROWS, model), f32)],
        compiler_params=limit(8),
        name="project",
    )(own, own_lse, far, value_up, out_proj)
    near, far_y, far_both = swap(near, 1), swap(far_y, 2), swap(far_both, 3)
    mixed, spread = pl.pallas_call(
        mix_kernel,
        out_shape=(
            jax.ShapeDtypeStruct((requests, quarter), f32),
            jax.ShapeDtypeStruct((devices, ROWS, quarter), bf16),
        ),
        in_specs=[VMEM] * 6,
        out_specs=[VMEM] * 2,
        compiler_params=limit(12),
        name="mix",
    )(mine, near, far_y, far_both, hidden, route)
    tokens = lax.all_to_all(spread, both, split_axis=0, concat_axis=0, tiled=True)
    slots, _, depth = gate_weight.shape
    chunk = 256 if (slots * depth) % 256 == 0 else depth
    parts = pl.pallas_call(
        functools.partial(expert_kernel, chunk),
        out_shape=jax.ShapeDtypeStruct((devices, ROWS, quarter), bf16),
        in_specs=[VMEM, VMEM, ANY, ANY, ANY],
        out_specs=VMEM,
        scratch_shapes=[
            pltpu.VMEM((model // LANES, ROWS * req_count, LANES), f32),
            pltpu.VMEM((requests * req_count, 3 * EXPERTS), f32),
            pltpu.VMEM((model // LANES, ROWS * req_count, LANES), f32),
            pltpu.VMEM((2, chunk, model), bf16),
            pltpu.VMEM((2, chunk, model), bf16),
            pltpu.VMEM((2, chunk, model), bf16),
            pltpu.SemaphoreType.DMA((3, 2)),
        ],
        compiler_params=limit(50),
        name="experts",
    )(
        tokens,
        norm_gain.reshape(1, model),
        jnp.swapaxes(gate_weight, 1, 2),
        jnp.swapaxes(up_weight, 1, 2),
        down_weight,
    )
    parts = lax.all_to_all(parts, both, split_axis=0, concat_axis=0, tiled=True)
    return pl.pallas_call(
        final_kernel,
        out_shape=jax.ShapeDtypeStruct((requests, quarter), bf16),
        in_specs=[VMEM] * 2,
        out_specs=VMEM,
        compiler_params=limit(24),
        name="final",
    )(parts, mixed)


def solution(mesh):
    return jax.shard_map(
        per_device,
        mesh=mesh,
        in_specs=(
            P("req", None),
            P("req", "head", None),
            P(("req", "head"), None, None),
            P("req", None),
            P("req"),
            P("head", None, None),
            P("head", None),
            P(),
            P("req", None),
            P("req", None),
            P("req", None, "head"),
            P("req", None, "head"),
            P("req", "head", None),
        ),
        out_specs=P("req", "head"),
        check_vma=False,
    )
```

time: 188 us -> 69.5 us (0.37)
  waiting for transfers between devices: 60.6 us -> 6.76 us
  blocking collectives: 69 us -> 28.2 us
  matrix products: 25.5 us -> 0 us
  Pallas kernels: 0 us -> 18.6 us
  between operations: 13.5 us -> 0.05 us
  other arithmetic: 4.66 us -> 0 us
    psum x1 -> x0, waiting for transfers between devices: 35.4 us -> none  [per_device(): lax.psum(jnp.einsum('nsif,sfd->nsid', active, down_weight, preferred_elem...]
    all_gather x4 -> x0, blocking collectives: 26.6 us -> none  [the longest x3 20 us: joined(): pieces = jax.tree.map(lambda part: lax.all_gather(part, axis), value)]
    dot_general x9 -> x0, matrix products: 25.5 us -> none  [the longest x1 13.2 us: per_device(): jnp.einsum('nsif,sfd->nsid', active, down_weight, preferred_element_type=...]
    all_to_all x1 -> x0, waiting for transfers between devices: 25.2 us -> none  [per_device(): lax.all_to_all(summed_out, 'req', split_axis=0, concat_axis=0, tiled=True)]
    pallas_call x0 -> x5, Pallas kernels: none -> 18.6 us  [the longest x1 15.7 us: per_device(): pl.pallas_call(functools.partial(expert_kernel, chunk), out_shape=jax.Sha...]
    psum x1 -> x0, blocking collectives: 11.7 us -> none  [per_device(): lax.psum(partial_out.astype(jnp.bfloat16), 'head').astype(jnp.float32)]
    ppermute x0 -> x6, starting transfers between devices: none -> 6.83 us  [swap(): lax.ppermute(value, 'head', [(n, n ^ flip) for n in range(head_count)])]
    ppermute x0 -> x6, waiting for transfers between devices: none -> 6.76 us  [swap(): lax.ppermute(value, 'head', [(n, n ^ flip) for n in range(head_count)])]
  transfers between devices with their start and end apart: 2 -> 6, of which waited for: 2 -> 4; matrix products, arithmetic and copies ran while one was open for 0% -> 1% of each run, Pallas kernels for 0% -> 0%
where the time goes in v1:
time: 69.5 us; the launch traced here: 69 us
  blocking collectives  28.2 us (41%)
  Pallas kernels  18.6 us (27%)
  local copies, waits for them, and re-layouts  8.61 us (12%)
  starting transfers between devices  6.83 us (10%)
  waiting for transfers between devices  6.76 us (10%)
    pallas_call x1, Pallas kernels, per_device(): pl.pallas_call(functools.partial(expert_kernel, chunk), out_shape=jax.Sha...  15.7 us
    all_to_all x1, blocking collectives, per_device(): lax.all_to_all(spread, both, split_axis=0, concat_axis=0, tiled=True)  15.3 us
    all_to_all x1, blocking collectives, per_device(): parts = lax.all_to_all(parts, both, split_axis=0, concat_axis=0, tiled=True)  12.8 us
    unnamed x19, local copies, waits for them, and re-layouts  8.61 us
    ppermute x6, starting transfers between devices, swap(): lax.ppermute(value, 'head', [(n, n ^ flip) for n in range(head_count)])  6.83 us
    ppermute x6, waiting for transfers between devices, swap(): lax.ppermute(value, 'head', [(n, n ^ flip) for n in range(head_count)])  6.76 us
    pallas_call x1, Pallas kernels, per_device(): pl.pallas_call(attend_kernel, out_shape=(jax.ShapeDtypeStruct((heads, ROW...  1.55 us
  transfers between devices with their start and end apart: 6, of which 4 were waited for; matrix products, arithmetic and copies ran while one was open for 1% of the time, Pallas kernels for 0%

profile of v1, /device:TPU:0, one launch (start us, length us, event | category | flops | bytes accessed | tf_op | source)
XLA Modules:
  0.0 69.0 jit_solution(7757270832476552772)
XLA Ops:
  0.0 0.5 collective-permute-start.1
  0.5 2.5 %collective-permute-start = (bf16[7,4,576]{2,1,0:T(4,128)(2,1)}, bf16[7,4,576]{2,1,0:T(4,128)(2,1)S(1)}, u32[]{:S(2)}, u32[]{:S(2)}) collective-permute-start(bf16[7,4,576]{2,1,0:T(4,128)(2,1)} %q_own.1), channel_id=1, source_target_pairs={{0,2},{1,3},{2,0},{3,1},{4,6},{5,7},{6,4},{7,5},{8,10},{9,11},{10,... | collective-permute-start | bytes 96776 | tf_op jit(solution)/shard_map/ppermute | solution.py:286
  3.0 0.8 %copy.14.table = s32[7,2]{1,0:T(8,128)S(1)} copy(s32[7,2]{0,1:T(2,128)} %param.16) | data formatting | bytes 112 | tf_op args[3]
  3.7 1.6 %collective-permute-done.q_far = bf16[7,4,576]{2,1,0:T(4,128)(2,1)S(1)} collective-permute-done((bf16[7,4,576]{2,1,0:T(4,128)(2,1)}, bf16[7,4,576]{2,1,0:T(4,128)(2,1)S(1)}, u32[]{:S(2)}, u32[]{:S(2)}) %collective-permute-start) | collective-permute-done | bytes 32288 | tf_op jit(solution)/shard_map/ppermute | solution.py:286
  5.3 1.0 %copy-done.2 = bf16[2,128,576]{1,2,0:T(8,128)(2,1)S(1)} copy-done((bf16[2,128,576]{1,2,0:T(8,128)(2,1)S(1)}, bf16[2,128,576]{1,2,0:T(8,128)(2,1)}, u32[]{:S(2)}) %copy-start.2) | copy-done | bytes 294936
  6.3 0.8 %copy-done.3 = bf16[7,4,576]{2,1,0:T(4,128)(2,1)S(1)} copy-done((bf16[7,4,576]{2,1,0:T(4,128)(2,1)S(1)}, bf16[7,4,576]{2,1,0:T(4,128)(2,1)}, u32[]{:S(2)}) %copy-start.3) | copy-done | bytes 32280
  7.0 0.7 copy-done.6
  7.7 0.7 copy-done.7
  8.4 0.7 copy-done.8
  9.1 1.5 %attend.1 = (f32[4,8,512]{2,1,0:T(8,128)S(1)}, f32[4,8,128]{2,1,0:T(8,128)S(1)}, bf16[4,8,640]{2,1,0:T(8,128)(2,1)S(1)}, f32[1,512]{1,0:T(1,128)S(1)}) custom-call(s32[7,2]{1,0:T(8,128)S(1)} %copy.14.table, s32[7]{0:T(128)S(1)} %copy-done.8, s32[7,6]{1,0:T(8,128)S(1)} %copy-done.6, f32[7,6]{1,0:T(8,128)S(1)} %copy-done.7, bf16[7,4,576]{2,1,0:T(4,128)(2,1)S(1)} %copy-done.3, ...), custom_call_target="tpu_custom_call" | custom-call | tf_op jit(solution)/shard_map/attend/pallas_call | solution.py:292
  10.6 1.9 %collective-permute-start.2 = (bf16[4,8,640]{2,1,0:T(8,128)(2,1)S(1)}, bf16[4,8,640]{2,1,0:T(8,128)(2,1)S(1)}, u32[]{:S(2)}, u32[]{:S(2)}) collective-permute-start(bf16[4,8,640]{2,1,0:T(8,128)(2,1)S(1)} %get-tuple-element.17), channel_id=1, source_target_pairs={{0,2},{1,3},{2,0},{3,1},{4,6},{5,7},{6,4},{7,5},{8,10},{9,11},{10,... | collective-permute-start | bytes 122888 | tf_op jit(solution)/shard_map/ppermute | solution.py:286
  12.5 2.2 %collective-permute-done.2.far = bf16[4,8,640]{2,1,0:T(8,128)(2,1)S(1)} collective-permute-done((bf16[4,8,640]{2,1,0:T(8,128)(2,1)S(1)}, bf16[4,8,640]{2,1,0:T(8,128)(2,1)S(1)}, u32[]{:S(2)}, u32[]{:S(2)}) %collective-permute-start.2) | collective-permute-done | bytes 40992 | tf_op jit(solution)/shard_map/ppermute | solution.py:286
  14.7 1.6 %copy-done = bf16[512,2048]{1,0:T(8,128)(2,1)S(1)} copy-done((bf16[512,2048]{1,0:T(8,128)(2,1)S(1)}, bf16[512,2048]{1,0:T(8,128)(2,1)}, u32[]{:S(2)}) %copy-start) | copy-done | bytes 2097176
  16.3 1.0 %copy-done.1 = bf16[4,512,128]{2,1,0:T(8,128)(2,1)S(1)} copy-done((bf16[4,512,128]{2,1,0:T(8,128)(2,1)S(1)}, bf16[4,512,128]{2,1,0:T(8,128)(2,1)}, u32[]{:S(2)}) %copy-start.1) | copy-done | bytes 524312
  17.3 0.7 project.1
  18.0 1.9 %collective-permute-start.4 = (bf16[8,512]{1,0:T(8,128)(2,1)S(1)}, bf16[8,512]{1,0:T(8,128)(2,1)S(1)}, u32[]{:S(2)}, u32[]{:S(2)}) collective-permute-start(bf16[8,512]{1,0:T(8,128)(2,1)S(1)} %get-tuple-element.20), channel_id=1, source_target_pairs={{0,2},{1,3},{2,0},{3,1},{4,6},{5,7},{6,4},{7,5},{8,10},{9,11},{10,... | collective-permute-start | bytes 24584 | tf_op jit(solution)/shard_map/ppermute | solution.py:286
  20.0 1.8 %collective-permute-done.4.far_y = bf16[8,512]{1,0:T(8,128)(2,1)S(1)} collective-permute-done((bf16[8,512]{1,0:T(8,128)(2,1)S(1)}, bf16[8,512]{1,0:T(8,128)(2,1)S(1)}, u32[]{:S(2)}, u32[]{:S(2)}) %collective-permute-start.4) | collective-permute-done | bytes 8224 | tf_op jit(solution)/shard_map/ppermute | solution.py:286
  21.7 1.2 %collective-permute-done.5.far_both = bf16[8,512]{1,0:T(8,128)(2,1)S(1)} collective-permute-done((bf16[8,512]{1,0:T(8,128)(2,1)S(1)}, bf16[8,512]{1,0:T(8,128)(2,1)S(1)}, u32[]{:S(2)}, u32[]{:S(2)}) %collective-permute-start.5) | collective-permute-done | bytes 8224 | tf_op jit(solution)/shard_map/ppermute | solution.py:286
  23.0 0.8 %copy-done.4 = bf16[7,2048]{1,0:T(8,128)(2,1)S(1)} copy-done((bf16[7,2048]{1,0:T(8,128)(2,1)S(1)}, bf16[7,2048]{1,0:T(8,128)(2,1)}, u32[]{:S(2)}) %copy-start.4) | copy-done | bytes 28696
  23.8 15.3 %all_to_all.10.tokens = bf16[32,8,512]{2,1,0:T(8,128)(2,1)S(1)} all-to-all(bf16[32,8,512]{2,1,0:T(8,128)(2,1)S(1)} %get-tuple-element.23), channel_id=1, replica_groups=mesh['req'=8,'head'=4] {'req','head'}, dimensions={0} | all-to-all | bytes 524288 | tf_op jit(solution)/shard_map/all_to_all | solution.py:333
  39.1 0.7 %copy-done.5 = f32[2048]{0:T(1024)S(1)} copy-done((f32[2048]{0:T(1024)S(1)}, f32[2048]{0:T(1024)}, u32[]{:S(2)}) %copy-start.5) | copy-done | bytes 8216
  39.8 15.7 %experts.1 = bf16[32,8,512]{2,1,0:T(8,128)(2,1)S(1)} custom-call(bf16[32,8,512]{2,1,0:T(8,128)(2,1)S(1)} %all_to_all.10.tokens, f32[1,2048]{1,0:T(1,128)S(1)} %bitcast.6, bf16[16,176,2048]{2,1,0:T(8,128)(2,1)} %bitcast.7, bf16[16,176,2048]{2,1,0:T(8,128)(2,1)} %bitcast.8, bf16[16,176,2048]{2,1,0:T(8,128)(2,1)} %down.1), custom_call_target="tpu_custom_call" | custom-call | tf_op jit(solution)/shard_map/experts/pallas_call | solution.py:336
  55.5 12.8 %all_to_all.11.parts = bf16[32,8,512]{2,1,0:T(8,128)(2,1)S(1)} all-to-all(bf16[32,8,512]{2,1,0:T(8,128)(2,1)S(1)} %experts.1), channel_id=1, replica_groups=mesh['req'=8,'head'=4] {'req','head'}, dimensions={0} | all-to-all | bytes 524288 | tf_op jit(solution)/shard_map/all_to_all | solution.py:359
  68.3 0.6 final.1
  (14 shorter events, 0.1 us)
Async XLA Ops:
  0.0 5.3 %collective-permute-start.1 = (bf16[2,576,128]{2,1,0:T(8,128)(2,1)}, bf16[2,576,128]{2,1,0:T(8,128)(2,1)S(1)}, u32[]{:S(2)}, u32[]{:S(2)}) collective-permute-start(bf16[2,576,128]{2,1,0:T(8,128)(2,1)} %bitcast.4), channel_id=1, source_target_pairs={{0,1},{1,0},{2,3},{3,2},{4,5},{5,4},{6,7},{7,6},{8,9},{9,8},{10,11... | collective-permute-start | bytes 884744 | tf_op jit(solution)/shard_map/ppermute | solution.py:286
  0.5 4.9 %collective-permute-start = (bf16[7,4,576]{2,1,0:T(4,128)(2,1)}, bf16[7,4,576]{2,1,0:T(4,128)(2,1)S(1)}, u32[]{:S(2)}, u32[]{:S(2)}) collective-permute-start(bf16[7,4,576]{2,1,0:T(4,128)(2,1)} %q_own.1), channel_id=1, source_target_pairs={{0,2},{1,3},{2,0},{3,1},{4,6},{5,7},{6,4},{7,5},{8,10},{9,11},{10,... | collective-permute-start | bytes 96776 | tf_op jit(solution)/shard_map/ppermute | solution.py:286
  5.3 1.0 %copy-start.2 = (bf16[2,128,576]{1,2,0:T(8,128)(2,1)S(1)}, bf16[2,128,576]{1,2,0:T(8,128)(2,1)}, u32[]{:S(2)}) copy-start(bf16[2,128,576]{1,2,0:T(8,128)(2,1)} %param.15) | copy-start | bytes 884740
  6.3 0.8 %copy-start.3 = (bf16[7,4,576]{2,1,0:T(4,128)(2,1)S(1)}, bf16[7,4,576]{2,1,0:T(4,128)(2,1)}, u32[]{:S(2)}) copy-start(bf16[7,4,576]{2,1,0:T(4,128)(2,1)} %q_own.1) | copy-start | bytes 96772
  7.0 0.7 copy-start.6
  7.7 0.7 copy-start.7
  8.4 0.7 copy-start.8
  10.6 4.1 %collective-permute-start.2 = (bf16[4,8,640]{2,1,0:T(8,128)(2,1)S(1)}, bf16[4,8,640]{2,1,0:T(8,128)(2,1)S(1)}, u32[]{:S(2)}, u32[]{:S(2)}) collective-permute-start(bf16[4,8,640]{2,1,0:T(8,128)(2,1)S(1)} %get-tuple-element.17), channel_id=1, source_target_pairs={{0,2},{1,3},{2,0},{3,1},{4,6},{5,7},{6,4},{7,5},{8,10},{9,11},{10,... | collective-permute-start | bytes 122888 | tf_op jit(solution)/shard_map/ppermute | solution.py:286
  14.7 1.6 %copy-start = (bf16[512,2048]{1,0:T(8,128)(2,1)S(1)}, bf16[512,2048]{1,0:T(8,128)(2,1)}, u32[]{:S(2)}) copy-start(bf16[512,2048]{1,0:T(8,128)(2,1)} %out_proj.1) | copy-start | bytes 6291460
  16.3 1.0 %copy-start.1 = (bf16[4,512,128]{2,1,0:T(8,128)(2,1)S(1)}, bf16[4,512,128]{2,1,0:T(8,128)(2,1)}, u32[]{:S(2)}) copy-start(bf16[4,512,128]{2,1,0:T(8,128)(2,1)} %value_up.1) | copy-start | bytes 1572868
  18.0 2.0 %collective-permute-start.3 = (bf16[8,512]{1,0:T(8,128)(2,1)S(1)}, bf16[8,512]{1,0:T(8,128)(2,1)S(1)}, u32[]{:S(2)}, u32[]{:S(2)}) collective-permute-start(bf16[8,512]{1,0:T(8,128)(2,1)S(1)} %get-tuple-element.19), channel_id=1, source_target_pairs={{0,1},{1,0},{2,3},{3,2},{4,5},{5,4},{6,7},{7,6},{8,9},{9,8},{10,11... | collective-permute-start | bytes 24584 | tf_op jit(solution)/shard_map/ppermute | solution.py:286
  18.0 3.7 %collective-permute-start.4 = (bf16[8,512]{1,0:T(8,128)(2,1)S(1)}, bf16[8,512]{1,0:T(8,128)(2,1)S(1)}, u32[]{:S(2)}, u32[]{:S(2)}) collective-permute-start(bf16[8,512]{1,0:T(8,128)(2,1)S(1)} %get-tuple-element.20), channel_id=1, source_target_pairs={{0,2},{1,3},{2,0},{3,1},{4,6},{5,7},{6,4},{7,5},{8,10},{9,11},{10,... | collective-permute-start | bytes 24584 | tf_op jit(solution)/shard_map/ppermute | solution.py:286
  19.9 3.1 %collective-permute-start.5 = (bf16[8,512]{1,0:T(8,128)(2,1)S(1)}, bf16[8,512]{1,0:T(8,128)(2,1)S(1)}, u32[]{:S(2)}, u32[]{:S(2)}) collective-permute-start(bf16[8,512]{1,0:T(8,128)(2,1)S(1)} %get-tuple-element.21), channel_id=1, source_target_pairs={{0,3},{1,2},{2,1},{3,0},{4,7},{5,6},{6,5},{7,4},{8,11},{9,10},{10,... | collective-permute-start | bytes 24584 | tf_op jit(solution)/shard_map/ppermute | solution.py:286
  23.0 0.8 %copy-start.4 = (bf16[7,2048]{1,0:T(8,128)(2,1)S(1)}, bf16[7,2048]{1,0:T(8,128)(2,1)}, u32[]{:S(2)}) copy-start(bf16[7,2048]{1,0:T(8,128)(2,1)} %hidden.1) | copy-start | bytes 86020
  39.1 0.7 %copy-start.5 = (f32[2048]{0:T(1024)S(1)}, f32[2048]{0:T(1024)}, u32[]{:S(2)}) copy-start(f32[2048]{0:T(1024)} %param.20) | copy-start | bytes 24580

commit v2 on v1

--- a/solution.py
+++ b/solution.py
@@ -36,11 +36,69 @@
     return high, middle, (rest - middle).astype(bf16).astype(f32)
 
 
+def start_all(pairs, sems):
+    copies = [
+        pltpu.make_async_copy(src, dst, sems.at[n]) for n, (src, dst) in enumerate(pairs)
+    ]
+    for copy in copies:
+        copy.start()
+    return copies
+
+
+def stage_kernel(*refs):
+    table_in, lens_in, ids_in, mix_in = refs[:4]
+    bias_out, route_out = refs[10:12]
+    table, lens, ids, mix, small_sems, sems = refs[18:]
+    small = start_all(
+        ((table_in, table), (lens_in, lens), (ids_in, ids), (mix_in, mix)), small_sems
+    )
+    large = start_all(tuple(zip(refs[4:10], refs[12:18])), sems)
+    for copy in small:
+        copy.wait()
+    head_at = lax.axis_index("head")
+    width, requests = table.shape
+    pages_here = bias_out.shape[0] // 2
+    row_request = lax.broadcasted_iota(jnp.int32, bias_out.shape[1:], 0) // ROWS
+    within = lax.broadcasted_iota(jnp.int32, bias_out.shape[1:], 1)
+    for side in range(2):
+        for p in range(pages_here):
+            page = (head_at ^ side) * pages_here + p
+            owner = jnp.int32(-1)
+            count = jnp.int32(0)
+            for r in range(requests):
+                for m in range(width):
+                    left = lens[r] - m * PAGE
+                    hit = jnp.logical_and(table[m, r] == page, left > 0)
+                    owner = jnp.where(hit, r, owner)
+                    count = jnp.where(hit, left, count)
+            valid = (row_request == owner) & (within < count)
+            bias_out[side * pages_here + p] = jnp.where(valid, 1.0, 0.0)
+    lanes = lax.broadcasted_iota(jnp.int32, route_out.shape, 1)
+    row = jnp.zeros(route_out.shape, f32)
+    for r in range(requests):
+        for i in range(TOP):
+            row = jnp.where(lanes == r * EXPERTS + ids[r, i], mix[r, i], row)
+    high, middle, low = split3(row)
+    route_out[...] = jnp.where(
+        head_at == 0, high, jnp.where(head_at == 1, middle, jnp.where(head_at == 2, low, 0.0))
+    )
+    for copy in large:
+        copy.wait()
+
+
+def fetch_kernel(spans, *refs):
+    count = len(spans)
+    sources, outs, sems = refs[:count], refs[count + 1 : 2 * count + 1], refs[2 * count + 1]
+    pairs = []
+    for source, out, (first, last) in zip(sources, outs, spans):
+        flat = source.reshape(source.shape[0] * source.shape[1], source.shape[2])
+        pairs.append((flat.at[pl.ds(first, last - first), :], out))
+    for copy in start_all(tuple(pairs), sems):
+        copy.wait()
+
+
 def attend_kernel(
-    table,
-    lens,
-    ids,
-    mix,
+    usable,
     q_own,
     q_far,
     cache_own,
@@ -48,41 +106,25 @@
     own_out,
     own_lse,
     far_out,
-    route_out,
     q_all,
     weighted,
     lse_all,
 ):
-    head_at = lax.axis_index("head")
     requests, heads, width = q_own.shape
     pages_here = cache_own.shape[0]
-    q_all[...] = jnp.zeros_like(q_all)
+    q_all[requests * ROWS :, :] = jnp.zeros((ROWS * (ROWS - requests), width), f32)
     for r in range(requests):
         q_all[r * ROWS : r * ROWS + heads, :] = q_own[r].astype(f32)
         q_all[r * ROWS + heads : r * ROWS + 2 * heads, :] = q_far[r].astype(f32)
     q_rows = q_all[...].astype(bf16)
     total_rows = q_all.shape[0]
-    row_request = lax.broadcasted_iota(jnp.int32, (total_rows, PAGE), 0) // ROWS
-    within = lax.broadcasted_iota(jnp.int32, (total_rows, PAGE), 1)
     scale = 1.0 / math.sqrt(NOPE + ROPE)
-    keys, valids, scores = [], [], []
-    for side, cache in ((0, cache_own), (1, cache_near)):
-        holder = head_at if side == 0 else head_at ^ 1
-        for p in range(pages_here):
-            page = holder * pages_here + p
-            owner = jnp.int32(-1)
-            count = jnp.int32(0)
-            for r in range(requests):
-                for m in range(table.shape[1]):
-                    left = lens[r] - m * PAGE
-                    hit = jnp.logical_and(table[r, m] == page, left > 0)
-                    owner = jnp.where(hit, r, owner)
-                    count = jnp.where(hit, left, count)
-            valid = (row_request == owner) & (within < count)
-            keys.append(cache.at[p])
-            valids.append(valid)
-            score = jnp.dot(q_rows, cache[p], preferred_element_type=f32) * scale
-            scores.append(jnp.where(valid, score, masked_low))
+    keys = [cache.at[p] for cache in (cache_own, cache_near) for p in range(pages_here)]
+    valids = [usable[n] > 0.0 for n in range(2 * pages_here)]
+    scores = []
+    for key, valid in zip(keys, valids):
+        score = jnp.dot(q_rows, key[...], preferred_element_type=f32) * scale
+        scores.append(jnp.where(valid, score, masked_low))
     highest = functools.reduce(jnp.maximum, scores).max(axis=-1, keepdims=True)
     total = jnp.zeros((total_rows, 1), f32)
     summed = jnp.zeros((total_rows, RANK), f32)
@@ -101,7 +143,7 @@
         weighted[c] = summed[:, c * LANES : (c + 1) * LANES]
     lse = jnp.where(some, highest + jnp.log(safe), masked_low)
     lse_all[...] = jnp.broadcast_to(lse, lse_all.shape)
-    lane = lax.broadcasted_iota(jnp.int32, (ROWS, 128), 1)
+    lane = lax.broadcasted_iota(jnp.int32, (ROWS, LANES), 1)
     for h in range(heads):
         own_lse[h] = lse_all[pl.ds(h, ROWS, stride=ROWS), :]
         for c in range(RANK // LANES):
@@ -112,18 +154,9 @@
         far_out[h, :, RANK:] = jnp.where(
             lane == 0, high, jnp.where(lane == 1, middle, jnp.where(lane == 2, low, 0.0))
         ).astype(bf16)
-    lanes = lax.broadcasted_iota(jnp.int32, route_out.shape, 1)
-    row = jnp.zeros(route_out.shape, f32)
-    for r in range(requests):
-        for i in range(TOP):
-            row = jnp.where(lanes == r * EXPERTS + ids[r, i], mix[r, i], row)
-    high, middle, low = split3(row)
-    route_out[...] = jnp.where(
-        head_at == 0, high, jnp.where(head_at == 1, middle, jnp.where(head_at == 2, low, 0.0))
-    )
-
-
-def project_kernel(own, own_lse, far, value_up, out_proj, mine, near, far_y, far_both, whole):
+
+
+def project_kernel(own, own_lse, far, value_up, out_proj, _, mine, near, far_y, far_both, whole):
     heads = own.shape[0]
     head_at = lax.axis_index("head")
     parts = []
@@ -146,7 +179,7 @@
         out[...] = whole[:, pl.ds(start, quarter)].astype(bf16)
 
 
-def mix_kernel(mine, near, far_y, far_both, hidden, route, mixed_out, spread_out):
+def mix_kernel(mine, near, far_y, far_both, hidden, route, _, mixed_out, spread_out):
     head_at = lax.axis_index("head")
     requests = hidden.shape[0]
     quarter = mine.shape[1]
@@ -167,40 +200,44 @@
     chunk,
     tokens,
     gain,
+    gate_a,
+    up_a,
+    gate_b,
+    up_b,
     gate,
     up,
     down,
     out,
     rows_all,
     mix_all,
+    active_all,
     total,
-    gate_buf,
-    up_buf,
-    down_buf,
+    gate_c,
+    up_c,
+    down_all,
     sems,
 ):
     req_count = lax.axis_size("req")
     head_count = lax.axis_size("head")
     req_at = lax.axis_index("req")
-    slots, depth, model = gate.shape
+    slots, depth, model = down.shape
     quarter = tokens.shape[2]
     requests = ROWS - 1
     live = requests * req_count
     units = slots * depth
-    steps = units // chunk
-    flat = [w.reshape(units, model) for w in (gate, up, down)]
-
-    def copies(step):
-        slot = step % 2
-        return [
-            pltpu.make_async_copy(
-                w.at[pl.ds(step * chunk, chunk), :], buf.at[slot], sems.at[n, slot]
-            )
-            for n, (w, buf) in enumerate(zip(flat, (gate_buf, up_buf, down_buf)))
-        ]
-
-    for copy in copies(0):
-        copy.start()
+    ready = gate_a.shape[0] + gate_b.shape[0]
+    pairs = []
+    for first in range(ready, units, chunk):
+        for source, buffer in ((gate, gate_c), (up, up_c)):
+            flat = source.reshape(units, model)
+            pairs.append((flat.at[pl.ds(first, chunk), :], buffer.at[pl.ds(first - ready, chunk), :]))
+    chunks = units // chunk
+    edges = [chunks * n // 3 * chunk for n in range(4)]
+    groups = list(zip(edges, edges[1:]))
+    for first, last in groups:
+        span = pl.ds(first, last - first)
+        pairs.append((down.reshape(units, model).at[span, :], down_all.at[span, :]))
+    loads = start_all(tuple(pairs), sems)
     for i in range(req_count):
         for j in range(head_count):
             block = tokens[i * head_count + j].astype(f32)
@@ -219,28 +256,38 @@
     spread = jnp.mean(mixed * mixed, axis=-1, keepdims=True)
     normed = (mixed * lax.rsqrt(spread + norm_eps) * gain[...]).astype(bf16)
     mix_rows = mix_all[...].astype(bf16)
-    for step in range(steps):
-        slot = step % 2
-        if step + 1 < steps:
-            for copy in copies(step + 1):
-                copy.start()
-        for copy in copies(step):
-            copy.wait()
-        unit = step * chunk + lax.broadcasted_iota(jnp.int32, (3 * EXPERTS, chunk), 1)
-        expert = lax.broadcasted_iota(jnp.int32, (3 * EXPERTS, chunk), 0) % EXPERTS
-        here = expert == (req_at * slots + unit // depth) // 2
-        weight = jnp.dot(
-            mix_rows, jnp.where(here, 1.0, 0.0).astype(bf16), preferred_element_type=f32
+    split = gate_a.shape[0]
+    for first in range(0, units, chunk):
+        if first < split:
+            gate_at, up_at, offset = gate_a, up_a, first
+        elif first < ready:
+            gate_at, up_at, offset = gate_b, up_b, first - split
+        else:
+            gate_at, up_at, offset = gate_c, up_c, first - ready
+            for _ in range(2):
+                loads.pop(0).wait()
+        unit = first + lax.broadcasted_iota(jnp.int32, (chunk, 3 * EXPERTS), 0)
+        expert = lax.broadcasted_iota(jnp.int32, (chunk, 3 * EXPERTS), 1) % EXPERTS
+        here = jnp.where(expert == (req_at * slots + unit // depth) // 2, 1.0, 0.0).astype(bf16)
+        weight = lax.dot_general(here, mix_rows, NT, preferred_element_type=f32)
+        gate_part = lax.dot_general(
+            gate_at[offset : offset + chunk, :], normed, NT, preferred_element_type=f32
         )
-        gate_part = lax.dot_general(normed, gate_buf[slot], NT, preferred_element_type=f32)
-        up_part = lax.dot_general(normed, up_buf[slot], NT, preferred_element_type=f32)
+        up_part = lax.dot_general(
+            up_at[offset : offset + chunk, :], normed, NT, preferred_element_type=f32
+        )
         active = gate_part / (1.0 + jnp.exp(-gate_part)) * up_part * weight
-        product = jnp.dot(active.astype(bf16), down_buf[slot], preferred_element_type=f32)
+        active_all[:, first : first + chunk] = active.T.astype(bf16)
+    for c in range(model // LANES):
+        total[c, live:, :] = jnp.zeros((req_count, LANES), f32)
+    for n, (first, last) in enumerate(groups):
+        loads.pop(0).wait()
+        product = jnp.dot(
+            active_all[:, first:last], down_all[first:last, :], preferred_element_type=f32
+        )
         for c in range(model // LANES):
             share = product[:, c * LANES : (c + 1) * LANES]
-            total[c, :live, :] = share if step == 0 else total[c, :live, :] + share
-    for c in range(model // LANES):
-        total[c, live:, :] = jnp.zeros((req_count, LANES), f32)
+            total[c, :live, :] = share if n == 0 else total[c, :live, :] + share
     for i in range(req_count):
         for j in range(head_count):
             for c in range(quarter // LANES):
@@ -285,20 +332,66 @@
     def swap(value, flip):
         return lax.ppermute(value, "head", [(n, n ^ flip) for n in range(head_count)])
 
+    def on_hbm(*values):
+        return [pltpu.with_memory_space_constraint(value, pltpu.HBM) for value in values]
+
+    def fetch(after, *pieces):
+        spans = tuple(span for _, span in pieces)
+        shapes = tuple(pltpu.VMEM((last - first, model), bf16) for first, last in spans)
+        size = sum(last - first for first, last in spans) * model * 2
+        return pl.pallas_call(
+            functools.partial(fetch_kernel, spans),
+            out_shape=shapes,
+            in_specs=[ANY] * (len(pieces) + 1),
+            out_specs=[VMEM] * len(pieces),
+            scratch_shapes=[pltpu.SemaphoreType.DMA((len(pieces),))],
+            compiler_params=limit(4),
+            cost_estimate=pl.CostEstimate(flops=0, bytes_accessed=size, transcendentals=0),
+            name="fetch",
+        )(*on_hbm(*(weight for weight, _ in pieces)), after)
+
+    slots, _, depth = gate_weight.shape
+    units = slots * depth
+    chunk = units // 11
+    split_a, split_b = 3 * chunk, 6 * chunk
+    gate = jnp.swapaxes(gate_weight, 1, 2)
+    up = jnp.swapaxes(up_weight, 1, 2)
     cache = jnp.swapaxes(latent_cache, 1, 2)
+    pages_here = cache.shape[0]
+    rows = ROWS * ROWS
     q_far = swap(queries, 2)
     cache_near = swap(cache, 1)
-    rows = ROWS * ROWS
-    own, own_lse, far, route = pl.pallas_call(
+    large = (queries, cache, value_up, out_proj, hidden, norm_gain.reshape(1, model))
+    usable, route, q_own, cache_own, value_up, out_proj, hidden, gain = pl.pallas_call(
+        stage_kernel,
+        out_shape=(
+            pltpu.VMEM((2 * pages_here, rows, PAGE), f32),
+            pltpu.VMEM((1, quarter), f32),
+            *(pltpu.VMEM(value.shape, value.dtype) for value in large),
+        ),
+        in_specs=[ANY] * 10,
+        out_specs=[VMEM] * 8,
+        scratch_shapes=[
+            pltpu.SMEM(page_table.shape[::-1], jnp.int32),
+            pltpu.SMEM(seq_lens.shape, jnp.int32),
+            pltpu.SMEM(expert_ids.shape, jnp.int32),
+            pltpu.SMEM(expert_mix.shape, f32),
+            pltpu.SemaphoreType.DMA((4,)),
+            pltpu.SemaphoreType.DMA((6,)),
+        ],
+        compiler_params=limit(4),
+        cost_estimate=pl.CostEstimate(flops=0, bytes_accessed=3 * 2**20, transcendentals=0),
+        name="stage",
+    )(*on_hbm(page_table.T, seq_lens, expert_ids, expert_mix, *large))
+    own, own_lse, far = pl.pallas_call(
         attend_kernel,
         out_shape=(
             jax.ShapeDtypeStruct((heads, ROWS, RANK), f32),
-            jax.ShapeDtypeStruct((heads, ROWS, 128), f32),
-            jax.ShapeDtypeStruct((heads, ROWS, RANK + 128), bf16),
-            jax.ShapeDtypeStruct((1, quarter), f32),
+            jax.ShapeDtypeStruct((heads, ROWS, LANES), f32),
+            jax.ShapeDtypeStruct((heads, ROWS, RANK + LANES), bf16),
         ),
-        in_specs=[SMEM] * 4 + [VMEM] * 4,
-        out_specs=[VMEM] * 4,
+        in_specs=[VMEM] * 5,
+        out_specs=[VMEM] * 3,
         scratch_shapes=[
             pltpu.VMEM((rows, width), f32),
             pltpu.VMEM((RANK // LANES, rows, LANES), f32),
@@ -306,18 +399,20 @@
         ],
         compiler_params=limit(8),
         name="attend",
-    )(page_table, seq_lens, expert_ids, expert_mix, queries, q_far, cache, cache_near)
+    )(usable, q_own, q_far, cache_own, cache_near)
+    gate_a, up_a = fetch(far, (gate, (0, split_a)), (up, (0, split_a)))
     far = swap(far, 2)
     piece = jax.ShapeDtypeStruct((ROWS, quarter), bf16)
     mine, near, far_y, far_both = pl.pallas_call(
         project_kernel,
         out_shape=(jax.ShapeDtypeStruct((ROWS, quarter), f32), piece, piece, piece),
-        in_specs=[VMEM] * 5,
+        in_specs=[VMEM] * 6,
         out_specs=[VMEM] * 4,
         scratch_shapes=[pltpu.VMEM((ROWS, model), f32)],
         compiler_params=limit(8),
         name="project",
-    )(own, own_lse, far, value_up, out_proj)
+    )(own, own_lse, far, value_up, out_proj, gate_a)
+    gate_b, up_b = fetch(near, (gate, (split_a, split_b)), (up, (split_a, split_b)))
     near, far_y, far_both = swap(near, 1), swap(far_y, 2), swap(far_both, 3)
     mixed, spread = pl.pallas_call(
         mix_kernel,
@@ -325,37 +420,30 @@
             jax.ShapeDtypeStruct((requests, quarter), f32),
             jax.ShapeDtypeStruct((devices, ROWS, quarter), bf16),
         ),
-        in_specs=[VMEM] * 6,
+        in_specs=[VMEM] * 7,
         out_specs=[VMEM] * 2,
         compiler_params=limit(12),
         name="mix",
-    )(mine, near, far_y, far_both, hidden, route)
+    )(mine, near, far_y, far_both, hidden, route, gate_b)
     tokens = lax.all_to_all(spread, both, split_axis=0, concat_axis=0, tiled=True)
-    slots, _, depth = gate_weight.shape
-    chunk = 256 if (slots * depth) % 256 == 0 else depth
     parts = pl.pallas_call(
         functools.partial(expert_kernel, chunk),
         out_shape=jax.ShapeDtypeStruct((devices, ROWS, quarter), bf16),
-        in_specs=[VMEM, VMEM, ANY, ANY, ANY],
+        in_specs=[VMEM] * 6 + [ANY] * 3,
         out_specs=VMEM,
         scratch_shapes=[
             pltpu.VMEM((model // LANES, ROWS * req_count, LANES), f32),
             pltpu.VMEM((requests * req_count, 3 * EXPERTS), f32),
+            pltpu.VMEM((requests * req_count, units), bf16),
             pltpu.VMEM((model // LANES, ROWS * req_count, LANES), f32),
-            pltpu.VMEM((2, chunk, model), bf16),
-            pltpu.VMEM((2, chunk, model), bf16),
-            pltpu.VMEM((2, chunk, model), bf16),
-            pltpu.SemaphoreType.DMA((3, 2)),
+            pltpu.VMEM((units - split_b, model), bf16),
+            pltpu.VMEM((units - split_b, model), bf16),
+            pltpu.VMEM((units, model), bf16),
+            pltpu.SemaphoreType.DMA((2 * (units - split_b) // chunk + 3,)),
         ],
-        compiler_params=limit(50),
+        compiler_params=limit(32),
         name="experts",
-    )(
-        tokens,
-        norm_gain.reshape(1, model),
-        jnp.swapaxes(gate_weight, 1, 2),
-        jnp.swapaxes(up_weight, 1, 2),
-        down_weight,
-    )
+    )(tokens, gain, gate_a, up_a, gate_b, up_b, *on_hbm(gate, up, down_weight))
     parts = lax.all_to_all(parts, both, split_axis=0, concat_axis=0, tiled=True)
     return pl.pallas_call(
         final_kernel,

time: 69.5 us -> 56.9 us (0.82)
  local copies, waits for them, and re-layouts: 8.61 us -> 0 us
  waiting for transfers between devices: 6.76 us -> 0.37 us
  Pallas kernels: 18.6 us -> 20.6 us
    unnamed x19 -> x0, local copies, waits for them, and re-layouts: 8.61 us -> none
    pallas_call x0 -> x3, Pallas kernels: none -> 7.69 us  [the longest x2 5.72 us: fetch(): pl.pallas_call(functools.partial(fetch_kernel, spans), out_shape=shapes,...]
    ppermute x6, waiting for transfers between devices: 6.76 us -> 0.37 us  [swap(): lax.ppermute(value, 'head', [(n, n ^ flip) for n in range(head_count)])]
    pallas_call x1, Pallas kernels: 15.7 us -> 10.7 us  [per_device(): pl.pallas_call(functools.partial(expert_kernel, chunk), out_shape=jax.Sha...]
    pallas_call x1, Pallas kernels: 1.55 us -> 0.81 us  [per_device(): pl.pallas_call(attend_kernel, out_shape=(jax.ShapeDtypeStruct((heads, ROW...]
  transfers between devices with their start and end apart: 6 -> 6, of which waited for: 4 -> 1; matrix products, arithmetic and copies ran while one was open for 1% -> 0% of each run, Pallas kernels for 0% -> 14%
where the time goes in v2:
time: 56.9 us; the launch traced here: 56.7 us
  blocking collectives  28.7 us (50%)
  Pallas kernels  20.6 us (36%)
  starting transfers between devices  7.01 us (12%)
    all_to_all x1, blocking collectives, per_device(): lax.all_to_all(spread, both, split_axis=0, concat_axis=0, tiled=True)  15.9 us
    all_to_all x1, blocking collectives, per_device(): parts = lax.all_to_all(parts, both, split_axis=0, concat_axis=0, tiled=True)  12.8 us
    pallas_call x1, Pallas kernels, per_device(): pl.pallas_call(functools.partial(expert_kernel, chunk), out_shape=jax.Sha...  10.7 us
    ppermute x6, starting transfers between devices, swap(): lax.ppermute(value, 'head', [(n, n ^ flip) for n in range(head_count)])  7.01 us
    pallas_call x2, Pallas kernels, fetch(): pl.pallas_call(functools.partial(fetch_kernel, spans), out_shape=shapes,...  5.72 us
    pallas_call x1, Pallas kernels, per_device(): pl.pallas_call(stage_kernel, out_shape=(pltpu.VMEM((2 * pages_here, rows,...  1.97 us
  transfers between devices with their start and end apart: 6, of which 1 were waited for; matrix products, arithmetic and copies ran while one was open for 0% of the time, Pallas kernels for 14%

profile of v2, /device:TPU:0, one launch (start us, length us, event | category | flops | bytes accessed | tf_op | source)
XLA Modules:
  0.0 56.7 jit_solution(654744917287034849)
XLA Ops:
  0.0 0.5 collective-permute-start.1
  0.5 2.5 %collective-permute-start = (bf16[7,4,576]{2,1,0:T(4,128)(2,1)}, bf16[7,4,576]{2,1,0:T(4,128)(2,1)S(1)}, u32[]{:S(2)}, u32[]{:S(2)}) collective-permute-start(bf16[7,4,576]{2,1,0:T(4,128)(2,1)} %refs_4_.1), channel_id=1, source_target_pairs={{0,2},{1,3},{2,0},{3,1},{4,6},{5,7},{6,4},{7,5},{8,10},{9,11},{10,... | collective-permute-start | bytes 96776 | tf_op jit(solution)/shard_map/ppermute | solution.py:333
  3.0 2.0 %stage.1 = (f32[4,64,128]{2,1,0:T(8,128)S(1)}, f32[1,512]{1,0:T(1,128)S(1)}, bf16[7,4,576]{2,1,0:T(4,128)(2,1)S(1)}, bf16[2,576,128]{2,1,0:T(8,128)(2,1)S(1)}, b...) custom-call(s32[2,7]{1,0:T(2,128)} %bitcast.14, ...), custom_call_target="tpu_custom_call" | custom-call | bytes 3145728 | tf_op jit(solution)/shard_map/stage/pallas_call | solution.py:365
  4.9 0.4 collective-permute-done.q_far
  5.3 0.0 collective-permute-done.1.cache_near
  5.3 0.8 %attend.1 = (f32[4,8,512]{2,1,0:T(8,128)S(1)}, f32[4,8,128]{2,1,0:T(8,128)S(1)}, bf16[4,8,640]{2,1,0:T(8,128)(2,1)S(1)}) custom-call(f32[4,64,128]{2,1,0:T(8,128)S(1)} %get-tuple-element.26.usable, bf16[7,4,576]{2,1,0:T(4,128)(2,1)S(1)} %get-tuple-element.27.q_own, bf16[7,4,576]{2,1,0:T(4,128)(2,1)S(1)} %collective-permute-done.q_far, ...), custom_call_target="tpu_custom_call" | custom-call | tf_op jit(solution)/shard_map/attend/pallas_call | solution.py:386
  6.1 1.9 %collective-permute-start.2 = (bf16[4,8,640]{2,1,0:T(8,128)(2,1)S(1)}, bf16[4,8,640]{2,1,0:T(8,128)(2,1)S(1)}, u32[]{:S(2)}, u32[]{:S(2)}) collective-permute-start(bf16[4,8,640]{2,1,0:T(8,128)(2,1)S(1)} %get-tuple-element.31.refs_2_), channel_id=1, source_target_pairs={{0,2},{1,3},{2,0},{3,1},{4,6},{5,7},{6,4},{7,5},{8,10},{9,11},{10,... | collective-permute-start | bytes 122888 | tf_op jit(solution)/shard_map/ppermute | solution.py:333
  8.0 2.9 %fetch.2 = (bf16[768,2048]{1,0:T(8,128)(2,1)S(1)}, bf16[768,2048]{1,0:T(8,128)(2,1)S(1)}) custom-call(bf16[16,176,2048]{2,1,0:T(8,128)(2,1)} %bitcast.5, bf16[16,176,2048]{2,1,0:T(8,128)(2,1)} %bitcast.8, bf16[4,8,640]{2,1,0:T(8,128)(2,1)S(1)} %get-tuple-element.31.refs_2_), custom_call_target="tpu_custom_call" | custom-call | bytes 6291456 | tf_op jit(solution)/shard_map/fetch/pallas_call | solution.py:342
  10.9 0.0 collective-permute-done.2.far
  10.9 0.7 %project.1 = (f32[8,512]{1,0:T(8,128)S(1)}, bf16[8,512]{1,0:T(8,128)(2,1)S(1)}, bf16[8,512]{1,0:T(8,128)(2,1)S(1)}, bf16[8,512]{1,0:T(8,128)(2,1)S(1)}) custom-call(f32[4,8,512]{2,1,0:T(8,128)S(1)} %get-tuple-element.29.own, f32[4,8,128]{2,1,0:T(8,128)S(1)} %get-tuple-element.30.own_lse, bf16[4,8,640]{2,1,0:T(8,128)(2,1)S(1)} %collective-permute-done.2.far, ...), custom_call_target="tpu_custom_call" | custom-call | tf_op jit(solution)/shard_map/project/pallas_call | solution.py:406
  11.6 1.1 %collective-permute-start.4 = (bf16[8,512]{1,0:T(8,128)(2,1)S(1)}, bf16[8,512]{1,0:T(8,128)(2,1)S(1)}, u32[]{:S(2)}, u32[]{:S(2)}) collective-permute-start(bf16[8,512]{1,0:T(8,128)(2,1)S(1)} %get-tuple-element.37), channel_id=1, source_target_pairs={{0,2},{1,3},{2,0},{3,1},{4,6},{5,7},{6,4},{7,5},{8,10},{9,11},{10,... | collective-permute-start | bytes 24584 | tf_op jit(solution)/shard_map/ppermute | solution.py:333
  12.7 0.0 collective-permute-start.5
  12.7 1.0 %collective-permute-start.3 = (bf16[8,512]{1,0:T(8,128)(2,1)S(1)}, bf16[8,512]{1,0:T(8,128)(2,1)S(1)}, u32[]{:S(2)}, u32[]{:S(2)}) collective-permute-start(bf16[8,512]{1,0:T(8,128)(2,1)S(1)} %get-tuple-element.36.refs_2_), channel_id=1, source_target_pairs={{0,1},{1,0},{2,3},{3,2},{4,5},{5,4},{6,7},{7,6},{8,9},{9,8},{10,11... | collective-permute-start | bytes 24584 | tf_op jit(solution)/shard_map/ppermute | solution.py:333
  13.7 2.9 %fetch.3 = (bf16[768,2048]{1,0:T(8,128)(2,1)S(1)}, bf16[768,2048]{1,0:T(8,128)(2,1)S(1)}) custom-call(bf16[16,176,2048]{2,1,0:T(8,128)(2,1)} %bitcast.6, bf16[16,176,2048]{2,1,0:T(8,128)(2,1)} %bitcast.9, bf16[8,512]{1,0:T(8,128)(2,1)S(1)} %get-tuple-element.36.refs_2_), custom_call_target="tpu_custom_call" | custom-call | bytes 6291456 | tf_op jit(solution)/shard_map/fetch/pallas_call | solution.py:342
  16.6 0.0 collective-permute-done.4.far_y
  16.6 0.0 collective-permute-done.5.far_both
  16.6 0.0 collective-permute-done.3.near
  16.7 15.9 %all_to_all.10.tokens = bf16[32,8,512]{2,1,0:T(8,128)(2,1)S(1)} all-to-all(bf16[32,8,512]{2,1,0:T(8,128)(2,1)S(1)} %get-tuple-element.42), channel_id=1, replica_groups=mesh['req'=8,'head'=4] {'req','head'}, dimensions={0} | all-to-all | bytes 524288 | tf_op jit(solution)/shard_map/all_to_all | solution.py:428
  32.5 10.7 %experts.1 = bf16[32,8,512]{2,1,0:T(8,128)(2,1)S(1)} custom-call(bf16[32,8,512]{2,1,0:T(8,128)(2,1)S(1)} %all_to_all.10.tokens, f32[1,2048]{1,0:T(1,128)S(1)} %get-tuple-element.43.gain, bf16[768,2048]{1,0:T(8,128)(2,1)S(1)} %get-tuple-element.34._.gate_a, bf16[768,2048]{1,0:T(8,128)(2,1)S(1)} %get-tuple-element.44.up_a, ...), custom_call_target="tpu_custom_call" | custom-call | tf_op jit(solution)/shard_map/experts/pallas_call | solution.py:429
  43.3 12.8 %all_to_all.11.parts = bf16[32,8,512]{2,1,0:T(8,128)(2,1)S(1)} all-to-all(bf16[32,8,512]{2,1,0:T(8,128)(2,1)S(1)} %experts.1), channel_id=1, replica_groups=mesh['req'=8,'head'=4] {'req','head'}, dimensions={0} | all-to-all | bytes 524288 | tf_op jit(solution)/shard_map/all_to_all | solution.py:447
  56.1 0.6 %final.1 = bf16[7,512]{1,0:T(8,128)(2,1)} custom-call(bf16[32,8,512]{2,1,0:T(8,128)(2,1)S(1)} %all_to_all.11.parts, f32[7,512]{1,0:T(8,128)S(1)} %get-tuple-element.46.mixed), custom_call_target="tpu_custom_call" | custom-call | tf_op jit(solution)/shard_map/final/pallas_call | solution.py:448
  (1 shorter events, 0.0 us)
Async XLA Ops:
  0.0 5.3 %collective-permute-start.1 = (bf16[2,576,128]{2,1,0:T(8,128)(2,1)}, bf16[2,576,128]{2,1,0:T(8,128)(2,1)S(1)}, u32[]{:S(2)}, u32[]{:S(2)}) collective-permute-start(bf16[2,576,128]{2,1,0:T(8,128)(2,1)} %bitcast.11), channel_id=1, source_target_pairs={{0,1},{1,0},{2,3},{3,2},{4,5},{5,4},{6,7},{7,6},{8,9},{9,8},{10,11... | collective-permute-start | bytes 884744 | tf_op jit(solution)/shard_map/ppermute | solution.py:333
  0.5 4.9 %collective-permute-start = (bf16[7,4,576]{2,1,0:T(4,128)(2,1)}, bf16[7,4,576]{2,1,0:T(4,128)(2,1)S(1)}, u32[]{:S(2)}, u32[]{:S(2)}) collective-permute-start(bf16[7,4,576]{2,1,0:T(4,128)(2,1)} %refs_4_.1), channel_id=1, source_target_pairs={{0,2},{1,3},{2,0},{3,1},{4,6},{5,7},{6,4},{7,5},{8,10},{9,11},{10,... | collective-permute-start | bytes 96776 | tf_op jit(solution)/shard_map/ppermute | solution.py:333
  6.1 4.8 %collective-permute-start.2 = (bf16[4,8,640]{2,1,0:T(8,128)(2,1)S(1)}, bf16[4,8,640]{2,1,0:T(8,128)(2,1)S(1)}, u32[]{:S(2)}, u32[]{:S(2)}) collective-permute-start(bf16[4,8,640]{2,1,0:T(8,128)(2,1)S(1)} %get-tuple-element.31.refs_2_), channel_id=1, source_target_pairs={{0,2},{1,3},{2,0},{3,1},{4,6},{5,7},{6,4},{7,5},{8,10},{9,11},{10,... | collective-permute-start | bytes 122888 | tf_op jit(solution)/shard_map/ppermute | solution.py:333
  11.6 5.0 %collective-permute-start.4 = (bf16[8,512]{1,0:T(8,128)(2,1)S(1)}, bf16[8,512]{1,0:T(8,128)(2,1)S(1)}, u32[]{:S(2)}, u32[]{:S(2)}) collective-permute-start(bf16[8,512]{1,0:T(8,128)(2,1)S(1)} %get-tuple-element.37), channel_id=1, source_target_pairs={{0,2},{1,3},{2,0},{3,1},{4,6},{5,7},{6,4},{7,5},{8,10},{9,11},{10,... | collective-permute-start | bytes 24584 | tf_op jit(solution)/shard_map/ppermute | solution.py:333
  12.7 3.9 %collective-permute-start.5 = (bf16[8,512]{1,0:T(8,128)(2,1)S(1)}, bf16[8,512]{1,0:T(8,128)(2,1)S(1)}, u32[]{:S(2)}, u32[]{:S(2)}) collective-permute-start(bf16[8,512]{1,0:T(8,128)(2,1)S(1)} %get-tuple-element.38), channel_id=1, source_target_pairs={{0,3},{1,2},{2,1},{3,0},{4,7},{5,6},{6,5},{7,4},{8,11},{9,10},{10,... | collective-permute-start | bytes 24584 | tf_op jit(solution)/shard_map/ppermute | solution.py:333
  12.7 3.9 %collective-permute-start.3 = (bf16[8,512]{1,0:T(8,128)(2,1)S(1)}, bf16[8,512]{1,0:T(8,128)(2,1)S(1)}, u32[]{:S(2)}, u32[]{:S(2)}) collective-permute-start(bf16[8,512]{1,0:T(8,128)(2,1)S(1)} %get-tuple-element.36.refs_2_), channel_id=1, source_target_pairs={{0,1},{1,0},{2,3},{3,2},{4,5},{5,4},{6,7},{7,6},{8,9},{9,8},{10,11... | collective-permute-start | bytes 24584 | tf_op jit(solution)/shard_map/ppermute | solution.py:333

commit v3 on v2

--- a/solution.py
+++ b/solution.py
@@ -192,18 +192,28 @@
         [residual, jnp.zeros((ROWS - requests, quarter), f32)], axis=0
     )
     block = jnp.where(row < requests, attn + padded, route[...]).astype(bf16)
+    half = spread_out.shape[2]
     for n in range(spread_out.shape[0]):
-        spread_out[n] = block
+        spread_out[n] = block[:, n % 2 * half : (n % 2 + 1) * half]
+
+
+def chunk_groups(first, last, chunk, count):
+    chunks = (last - first) // chunk
+    edges = [first + chunks * n // count * chunk for n in range(count + 1)]
+    return list(zip(edges, edges[1:]))
 
 
 def expert_kernel(
     chunk,
     tokens,
+    tokens_near,
     gain,
     gate_a,
     up_a,
     gate_b,
     up_b,
+    gate_c,
+    up_c,
     gate,
     up,
     down,
@@ -212,8 +222,8 @@
     mix_all,
     active_all,
     total,
-    gate_c,
-    up_c,
+    gate_d,
+    up_d,
     down_all,
     sems,
 ):
@@ -221,26 +231,30 @@
     head_count = lax.axis_size("head")
     req_at = lax.axis_index("req")
     slots, depth, model = down.shape
-    quarter = tokens.shape[2]
+    quarter = model // head_count
+    lower = lax.axis_index("head") % 2 == 0
     requests = ROWS - 1
     live = requests * req_count
     units = slots * depth
-    ready = gate_a.shape[0] + gate_b.shape[0]
+    ready = gate_a.shape[0] + gate_b.shape[0] + gate_c.shape[0]
     pairs = []
-    for first in range(ready, units, chunk):
-        for source, buffer in ((gate, gate_c), (up, up_c)):
+    halves = chunk_groups(ready, units, chunk, 2)
+    for first, last in halves:
+        for source, buffer in ((gate, gate_d), (up, up_d)):
             flat = source.reshape(units, model)
-            pairs.append((flat.at[pl.ds(first, chunk), :], buffer.at[pl.ds(first - ready, chunk), :]))
-    chunks = units // chunk
-    edges = [chunks * n // 3 * chunk for n in range(4)]
-    groups = list(zip(edges, edges[1:]))
+            pairs.append(
+                (flat.at[pl.ds(first, last - first), :], buffer.at[pl.ds(first - ready, last - first), :])
+            )
+    groups = chunk_groups(0, units, chunk, 2)
     for first, last in groups:
         span = pl.ds(first, last - first)
         pairs.append((down.reshape(units, model).at[span, :], down_all.at[span, :]))
     loads = start_all(tuple(pairs), sems)
     for i in range(req_count):
         for j in range(head_count):
-            block = tokens[i * head_count + j].astype(f32)
+            here, there = (part[i * head_count + j].astype(f32) for part in (tokens, tokens_near))
+            halves_of = (jnp.where(lower, here, there), jnp.where(lower, there, here))
+            block = jnp.concatenate(halves_of, axis=1)
             for c in range(quarter // LANES):
                 rows_all[j * quarter // LANES + c, pl.ds(i, ROWS, stride=req_count), :] = block[
                     :, c * LANES : (c + 1) * LANES
@@ -256,20 +270,21 @@
     spread = jnp.mean(mixed * mixed, axis=-1, keepdims=True)
     normed = (mixed * lax.rsqrt(spread + norm_eps) * gain[...]).astype(bf16)
     mix_rows = mix_all[...].astype(bf16)
-    split = gate_a.shape[0]
-    for first in range(0, units, chunk):
-        if first < split:
-            gate_at, up_at, offset = gate_a, up_a, first
-        elif first < ready:
-            gate_at, up_at, offset = gate_b, up_b, first - split
-        else:
-            gate_at, up_at, offset = gate_c, up_c, first - ready
-            for _ in range(2):
-                loads.pop(0).wait()
-        unit = first + lax.broadcasted_iota(jnp.int32, (chunk, 3 * EXPERTS), 0)
-        expert = lax.broadcasted_iota(jnp.int32, (chunk, 3 * EXPERTS), 1) % EXPERTS
-        here = jnp.where(expert == (req_at * slots + unit // depth) // 2, 1.0, 0.0).astype(bf16)
-        weight = lax.dot_general(here, mix_rows, NT, preferred_element_type=f32)
+    expert = lax.broadcasted_iota(jnp.int32, (max(slots, ROWS), 3 * EXPERTS), 1) % EXPERTS
+    slot_at = req_at * slots + lax.broadcasted_iota(jnp.int32, expert.shape, 0)
+    chosen = jnp.where(expert == slot_at // 2, 1.0, 0.0).astype(bf16)
+    by_slot = lax.dot_general(chosen, mix_rows, NT, preferred_element_type=f32)
+    homes = []
+    for gate_at, up_at in ((gate_a, up_a), (gate_b, up_b), (gate_c, up_c), (gate_d, up_d)):
+        homes += [(gate_at, up_at, offset) for offset in range(0, gate_at.shape[0], chunk)]
+    for first, (gate_at, up_at, offset) in zip(range(0, units, chunk), homes):
+        if first in [start for start, _ in halves]:
+            loads.pop(0).wait()
+            loads.pop(0).wait()
+        unit = first + lax.broadcasted_iota(jnp.int32, (chunk, live), 0)
+        weight = jnp.broadcast_to(by_slot[first // depth : first // depth + 1, :], (chunk, live))
+        for slot in range(first // depth + 1, (first + chunk - 1) // depth + 1):
+            weight = jnp.where(unit >= slot * depth, by_slot[slot : slot + 1, :], weight)
         gate_part = lax.dot_general(
             gate_at[offset : offset + chunk, :], normed, NT, preferred_element_type=f32
         )
@@ -326,6 +341,7 @@
     requests, heads, width = queries.shape
     model = hidden.shape[1]
     quarter = model // head_count
+    half = quarter // 2
     devices = req_count * head_count
     assert head_count == 4 and requests == ROWS - 1 and requests * EXPERTS <= quarter
 
@@ -353,7 +369,7 @@
     slots, _, depth = gate_weight.shape
     units = slots * depth
     chunk = units // 11
-    split_a, split_b = 3 * chunk, 6 * chunk
+    split_a, split_b, split_c = 2 * chunk, 5 * chunk, 6 * chunk
     gate = jnp.swapaxes(gate_weight, 1, 2)
     up = jnp.swapaxes(up_weight, 1, 2)
     cache = jnp.swapaxes(latent_cache, 1, 2)
@@ -418,7 +434,7 @@
         mix_kernel,
         out_shape=(
             jax.ShapeDtypeStruct((requests, quarter), f32),
-            jax.ShapeDtypeStruct((devices, ROWS, quarter), bf16),
+            jax.ShapeDtypeStruct((devices, ROWS, half), bf16),
         ),
         in_specs=[VMEM] * 7,
         out_specs=[VMEM] * 2,
@@ -426,24 +442,27 @@
         name="mix",
     )(mine, near, far_y, far_both, hidden, route, gate_b)
     tokens = lax.all_to_all(spread, both, split_axis=0, concat_axis=0, tiled=True)
+    gate_c, up_c = fetch(tokens, (gate, (split_b, split_c)), (up, (split_b, split_c)))
+    tokens_near = swap(tokens, 1)
+    ready = (gate_a, up_a, gate_b, up_b, gate_c, up_c)
     parts = pl.pallas_call(
         functools.partial(expert_kernel, chunk),
         out_shape=jax.ShapeDtypeStruct((devices, ROWS, quarter), bf16),
-        in_specs=[VMEM] * 6 + [ANY] * 3,
+        in_specs=[VMEM] * 9 + [ANY] * 3,
         out_specs=VMEM,
         scratch_shapes=[
             pltpu.VMEM((model // LANES, ROWS * req_count, LANES), f32),
             pltpu.VMEM((requests * req_count, 3 * EXPERTS), f32),
             pltpu.VMEM((requests * req_count, units), bf16),
             pltpu.VMEM((model // LANES, ROWS * req_count, LANES), f32),
-            pltpu.VMEM((units - split_b, model), bf16),
-            pltpu.VMEM((units - split_b, model), bf16),
+            pltpu.VMEM((units - split_c, model), bf16),
+            pltpu.VMEM((units - split_c, model), bf16),
             pltpu.VMEM((units, model), bf16),
-            pltpu.SemaphoreType.DMA((2 * (units - split_b) // chunk + 3,)),
+            pltpu.SemaphoreType.DMA((6,)),
         ],
         compiler_params=limit(32),
         name="experts",
-    )(tokens, gain, gate_a, up_a, gate_b, up_b, *on_hbm(gate, up, down_weight))
+    )(tokens, tokens_near, gain, *ready, *on_hbm(gate, up, down_weight))
     parts = lax.all_to_all(parts, both, split_axis=0, concat_axis=0, tiled=True)
     return pl.pallas_call(
         final_kernel,

time: 56.9 us -> 54.4 us (0.956)
  blocking collectives: 28.7 us -> 26.4 us
    all_to_all x1, blocking collectives: 15.9 us -> 14.1 us  [per_device(): lax.all_to_all(spread, both, split_axis=0, concat_axis=0, tiled=True)]
    pallas_call x1, Pallas kernels: 10.7 us -> 9.31 us  [per_device(): pl.pallas_call(functools.partial(expert_kernel, chunk), out_shape=jax.Sha...]
    pallas_call x2 -> x3, Pallas kernels: 5.72 us -> 6.66 us  [fetch(): pl.pallas_call(functools.partial(fetch_kernel, spans), out_shape=shapes,...]
    ppermute x6 -> x7, starting transfers between devices: 7.01 us -> 7.22 us  [swap(): lax.ppermute(value, 'head', [(n, n ^ flip) for n in range(head_count)])]
  transfers between devices with their start and end apart: 6 -> 7, of which waited for: 1 -> 1; matrix products, arithmetic and copies ran while one was open for 0% -> 0% of each run, Pallas kernels for 14% -> 16%
where the time goes in v3:
time: 54.4 us; the launch traced here: 54.2 us
  blocking collectives  26.4 us (49%)
  Pallas kernels  20.1 us (37%)
  starting transfers between devices  7.22 us (13%)
    all_to_all x1, blocking collectives, per_device(): lax.all_to_all(spread, both, split_axis=0, concat_axis=0, tiled=True)  14.1 us
    all_to_all x1, blocking collectives, per_device(): parts = lax.all_to_all(parts, both, split_axis=0, concat_axis=0, tiled=True)  12.3 us
    pallas_call x1, Pallas kernels, per_device(): pl.pallas_call(functools.partial(expert_kernel, chunk), out_shape=jax.Sha...  9.31 us
    ppermute x7, starting transfers between devices, swap(): lax.ppermute(value, 'head', [(n, n ^ flip) for n in range(head_count)])  7.22 us
    pallas_call x3, Pallas kernels, fetch(): pl.pallas_call(functools.partial(fetch_kernel, spans), out_shape=shapes,...  6.66 us
    pallas_call x1, Pallas kernels, per_device(): pl.pallas_call(stage_kernel, out_shape=(pltpu.VMEM((2 * pages_here, rows,...  1.97 us
  transfers between devices with their start and end apart: 7, of which 1 were waited for; matrix products, arithmetic and copies ran while one was open for 0% of the time, Pallas kernels for 16%

profile of v3, /device:TPU:0, one launch (start us, length us, event | category | flops | bytes accessed | tf_op | source)
XLA Modules:
  0.0 54.2 jit_solution(802240002318798467)
XLA Ops:
  0.0 0.5 collective-permute-start.1
  0.5 2.5 %collective-permute-start = (bf16[7,4,576]{2,1,0:T(4,128)(2,1)}, bf16[7,4,576]{2,1,0:T(4,128)(2,1)S(1)}, u32[]{:S(2)}, u32[]{:S(2)}) collective-permute-start(bf16[7,4,576]{2,1,0:T(4,128)(2,1)} %refs_4_.1), channel_id=1, source_target_pairs={{0,2},{1,3},{2,0},{3,1},{4,6},{5,7},{6,4},{7,5},{8,10},{9,11},{10,... | collective-permute-start | bytes 96776 | tf_op jit(solution)/shard_map/ppermute | solution.py:349
  3.0 2.0 %stage.1 = (f32[4,64,128]{2,1,0:T(8,128)S(1)}, f32[1,512]{1,0:T(1,128)S(1)}, bf16[7,4,576]{2,1,0:T(4,128)(2,1)S(1)}, bf16[2,576,128]{2,1,0:T(8,128)(2,1)S(1)}, b...) custom-call(s32[2,7]{1,0:T(2,128)} %bitcast.16, ...), custom_call_target="tpu_custom_call" | custom-call | bytes 3145728 | tf_op jit(solution)/shard_map/stage/pallas_call | solution.py:381
  4.9 0.4 collective-permute-done.q_far
  5.3 0.0 collective-permute-done.1.cache_near
  5.3 0.8 %attend.1 = (f32[4,8,512]{2,1,0:T(8,128)S(1)}, f32[4,8,128]{2,1,0:T(8,128)S(1)}, bf16[4,8,640]{2,1,0:T(8,128)(2,1)S(1)}) custom-call(f32[4,64,128]{2,1,0:T(8,128)S(1)} %get-tuple-element.28.usable, bf16[7,4,576]{2,1,0:T(4,128)(2,1)S(1)} %get-tuple-element.29.q_own, bf16[7,4,576]{2,1,0:T(4,128)(2,1)S(1)} %collective-permute-done.q_far, ...), custom_call_target="tpu_custom_call" | custom-call | tf_op jit(solution)/shard_map/attend/pallas_call | solution.py:402
  6.1 1.9 %collective-permute-start.2 = (bf16[4,8,640]{2,1,0:T(8,128)(2,1)S(1)}, bf16[4,8,640]{2,1,0:T(8,128)(2,1)S(1)}, u32[]{:S(2)}, u32[]{:S(2)}) collective-permute-start(bf16[4,8,640]{2,1,0:T(8,128)(2,1)S(1)} %get-tuple-element.33.refs_2_), channel_id=1, source_target_pairs={{0,2},{1,3},{2,0},{3,1},{4,6},{5,7},{6,4},{7,5},{8,10},{9,11},{10,... | collective-permute-start | bytes 122888 | tf_op jit(solution)/shard_map/ppermute | solution.py:349
  8.0 2.2 %fetch.3 = (bf16[512,2048]{1,0:T(8,128)(2,1)S(1)}, bf16[512,2048]{1,0:T(8,128)(2,1)S(1)}) custom-call(bf16[16,176,2048]{2,1,0:T(8,128)(2,1)} %bitcast.5, bf16[16,176,2048]{2,1,0:T(8,128)(2,1)} %bitcast.9, bf16[4,8,640]{2,1,0:T(8,128)(2,1)S(1)} %get-tuple-element.33.refs_2_), custom_call_target="tpu_custom_call" | custom-call | bytes 4194304 | tf_op jit(solution)/shard_map/fetch/pallas_call | solution.py:358
  10.3 0.0 collective-permute-done.2.far
  10.3 0.7 %project.1 = (f32[8,512]{1,0:T(8,128)S(1)}, bf16[8,512]{1,0:T(8,128)(2,1)S(1)}, bf16[8,512]{1,0:T(8,128)(2,1)S(1)}, bf16[8,512]{1,0:T(8,128)(2,1)S(1)}) custom-call(f32[4,8,512]{2,1,0:T(8,128)S(1)} %get-tuple-element.31.own, f32[4,8,128]{2,1,0:T(8,128)S(1)} %get-tuple-element.32.own_lse, bf16[4,8,640]{2,1,0:T(8,128)(2,1)S(1)} %collective-permute-done.2.far, ...), custom_call_target="tpu_custom_call" | custom-call | tf_op jit(solution)/shard_map/project/pallas_call | solution.py:422
  11.0 1.8 %collective-permute-start.4 = (bf16[8,512]{1,0:T(8,128)(2,1)S(1)}, bf16[8,512]{1,0:T(8,128)(2,1)S(1)}, u32[]{:S(2)}, u32[]{:S(2)}) collective-permute-start(bf16[8,512]{1,0:T(8,128)(2,1)S(1)} %get-tuple-element.39), channel_id=1, source_target_pairs={{0,2},{1,3},{2,0},{3,1},{4,6},{5,7},{6,4},{7,5},{8,10},{9,11},{10,... | collective-permute-start | bytes 24584 | tf_op jit(solution)/shard_map/ppermute | solution.py:349
  12.7 0.0 collective-permute-start.5
  12.7 0.4 collective-permute-start.3
  13.1 2.9 %fetch.4 = (bf16[768,2048]{1,0:T(8,128)(2,1)S(1)}, bf16[768,2048]{1,0:T(8,128)(2,1)S(1)}) custom-call(bf16[16,176,2048]{2,1,0:T(8,128)(2,1)} %bitcast.6, bf16[16,176,2048]{2,1,0:T(8,128)(2,1)} %bitcast.10, bf16[8,512]{1,0:T(8,128)(2,1)S(1)} %get-tuple-element.38.refs_2_), custom_call_target="tpu_custom_call" | custom-call | bytes 6291456 | tf_op jit(solution)/shard_map/fetch/pallas_call | solution.py:358
  16.0 0.0 collective-permute-done.4.far_y
  16.0 0.0 collective-permute-done.5.far_both
  16.0 0.0 collective-permute-done.3.near
  16.0 14.1 %all_to_all.10.refs_2_.tokens = bf16[32,8,256]{2,1,0:T(8,128)(2,1)S(1)} all-to-all(bf16[32,8,256]{2,1,0:T(8,128)(2,1)S(1)} %get-tuple-element.44), channel_id=1, replica_groups=mesh['req'=8,'head'=4] {'req','head'}, dimensions={0} | all-to-all | bytes 262144 | tf_op jit(solution)/shard_map/all_to_all | solution.py:444
  30.1 0.2 collective-permute-start.6
  30.4 1.6 %fetch.5 = (bf16[256,2048]{1,0:T(8,128)(2,1)S(1)}, bf16[256,2048]{1,0:T(8,128)(2,1)S(1)}) custom-call(bf16[16,176,2048]{2,1,0:T(8,128)(2,1)} %bitcast.7, bf16[16,176,2048]{2,1,0:T(8,128)(2,1)} %bitcast.11, bf16[32,8,256]{2,1,0:T(8,128)(2,1)S(1)} %all_to_all.10.refs_2_.tokens), custom_call_target="tpu_custom_call" | custom-call | bytes 2097152 | tf_op jit(solution)/shard_map/fetch/pallas_call | solution.py:358
  31.9 0.0 collective-permute-done.6.tokens_near
  31.9 9.3 %experts.1 = bf16[32,8,512]{2,1,0:T(8,128)(2,1)S(1)} custom-call(bf16[32,8,256]{2,1,0:T(8,128)(2,1)S(1)} %all_to_all.10.refs_2_.tokens, bf16[32,8,256]{2,1,0:T(8,128)(2,1)S(1)} %collective-permute-done.6.tokens_near, f32[1,2048]{1,0:T(1,128)S(1)} %get-tuple-element.45.gain, bf16[512,2048]{1,0:T(8,128)(2,1)S(1)} %get-tuple-element.36._.gate_a, ...), custom_call_target="tpu_custom_call" | custom-call | tf_op jit(solution)/shard_map/experts/pallas_call | solution.py:448
  41.3 12.3 %all_to_all.11.parts = bf16[32,8,512]{2,1,0:T(8,128)(2,1)S(1)} all-to-all(bf16[32,8,512]{2,1,0:T(8,128)(2,1)S(1)} %experts.1), channel_id=1, replica_groups=mesh['req'=8,'head'=4] {'req','head'}, dimensions={0} | all-to-all | bytes 524288 | tf_op jit(solution)/shard_map/all_to_all | solution.py:466
  53.6 0.6 %final.1 = bf16[7,512]{1,0:T(8,128)(2,1)} custom-call(bf16[32,8,512]{2,1,0:T(8,128)(2,1)S(1)} %all_to_all.11.parts, f32[7,512]{1,0:T(8,128)S(1)} %get-tuple-element.50.mixed), custom_call_target="tpu_custom_call" | custom-call | tf_op jit(solution)/shard_map/final/pallas_call | solution.py:467
  (1 shorter events, 0.0 us)
Async XLA Ops:
  0.0 5.3 %collective-permute-start.1 = (bf16[2,576,128]{2,1,0:T(8,128)(2,1)}, bf16[2,576,128]{2,1,0:T(8,128)(2,1)S(1)}, u32[]{:S(2)}, u32[]{:S(2)}) collective-permute-start(bf16[2,576,128]{2,1,0:T(8,128)(2,1)} %bitcast.13), channel_id=1, source_target_pairs={{0,1},{1,0},{2,3},{3,2},{4,5},{5,4},{6,7},{7,6},{8,9},{9,8},{10,11... | collective-permute-start | bytes 884744 | tf_op jit(solution)/shard_map/ppermute | solution.py:349
  0.5 4.9 %collective-permute-start = (bf16[7,4,576]{2,1,0:T(4,128)(2,1)}, bf16[7,4,576]{2,1,0:T(4,128)(2,1)S(1)}, u32[]{:S(2)}, u32[]{:S(2)}) collective-permute-start(bf16[7,4,576]{2,1,0:T(4,128)(2,1)} %refs_4_.1), channel_id=1, source_target_pairs={{0,2},{1,3},{2,0},{3,1},{4,6},{5,7},{6,4},{7,5},{8,10},{9,11},{10,... | collective-permute-start | bytes 96776 | tf_op jit(solution)/shard_map/ppermute | solution.py:349
  6.1 4.1 %collective-permute-start.2 = (bf16[4,8,640]{2,1,0:T(8,128)(2,1)S(1)}, bf16[4,8,640]{2,1,0:T(8,128)(2,1)S(1)}, u32[]{:S(2)}, u32[]{:S(2)}) collective-permute-start(bf16[4,8,640]{2,1,0:T(8,128)(2,1)S(1)} %get-tuple-element.33.refs_2_), channel_id=1, source_target_pairs={{0,2},{1,3},{2,0},{3,1},{4,6},{5,7},{6,4},{7,5},{8,10},{9,11},{10,... | collective-permute-start | bytes 122888 | tf_op jit(solution)/shard_map/ppermute | solution.py:349
  11.0 5.0 %collective-permute-start.4 = (bf16[8,512]{1,0:T(8,128)(2,1)S(1)}, bf16[8,512]{1,0:T(8,128)(2,1)S(1)}, u32[]{:S(2)}, u32[]{:S(2)}) collective-permute-start(bf16[8,512]{1,0:T(8,128)(2,1)S(1)} %get-tuple-element.39), channel_id=1, source_target_pairs={{0,2},{1,3},{2,0},{3,1},{4,6},{5,7},{6,4},{7,5},{8,10},{9,11},{10,... | collective-permute-start | bytes 24584 | tf_op jit(solution)/shard_map/ppermute | solution.py:349
  12.7 3.3 %collective-permute-start.5 = (bf16[8,512]{1,0:T(8,128)(2,1)S(1)}, bf16[8,512]{1,0:T(8,128)(2,1)S(1)}, u32[]{:S(2)}, u32[]{:S(2)}) collective-permute-start(bf16[8,512]{1,0:T(8,128)(2,1)S(1)} %get-tuple-element.40), channel_id=1, source_target_pairs={{0,3},{1,2},{2,1},{3,0},{4,7},{5,6},{6,5},{7,4},{8,11},{9,10},{10,... | collective-permute-start | bytes 24584 | tf_op jit(solution)/shard_map/ppermute | solution.py:349
  12.7 3.3 %collective-permute-start.3 = (bf16[8,512]{1,0:T(8,128)(2,1)S(1)}, bf16[8,512]{1,0:T(8,128)(2,1)S(1)}, u32[]{:S(2)}, u32[]{:S(2)}) collective-permute-start(bf16[8,512]{1,0:T(8,128)(2,1)S(1)} %get-tuple-element.38.refs_2_), channel_id=1, source_target_pairs={{0,1},{1,0},{2,3},{3,2},{4,5},{5,4},{6,7},{7,6},{8,9},{9,8},{10,11... | collective-permute-start | bytes 24584 | tf_op jit(solution)/shard_map/ppermute | solution.py:349
  30.1 1.8 %collective-permute-start.6 = (bf16[32,8,256]{2,1,0:T(8,128)(2,1)S(1)}, bf16[32,8,256]{2,1,0:T(8,128)(2,1)S(1)}, u32[]{:S(2)}, u32[]{:S(2)}) collective-permute-start(bf16[32,8,256]{2,1,0:T(8,128)(2,1)S(1)} %all_to_all.10.refs_2_.tokens), channel_id=1, source_target_pairs={{0,1},{1,0},{2,3},{3,2},{4,5},{5,4},{6,7},{7,6},{8,9},{9,8},{10,11... | collective-permute-start | bytes 393224 | tf_op jit(solution)/shard_map/ppermute | solution.py:349

commit v4 on v3

--- a/solution.py
+++ b/solution.py
@@ -217,14 +217,16 @@
     gate,
     up,
     down,
-    out,
+    theirs_out,
+    active_out,
+    down_own,
     rows_all,
     mix_all,
     active_all,
     total,
     gate_d,
     up_d,
-    down_all,
+    down_theirs,
     sems,
 ):
     req_count = lax.axis_size("req")
@@ -238,17 +240,19 @@
     units = slots * depth
     ready = gate_a.shape[0] + gate_b.shape[0] + gate_c.shape[0]
     pairs = []
-    halves = chunk_groups(ready, units, chunk, 2)
+    halves = chunk_groups(ready, units, chunk, 1)
     for first, last in halves:
         for source, buffer in ((gate, gate_d), (up, up_d)):
             flat = source.reshape(units, model)
             pairs.append(
                 (flat.at[pl.ds(first, last - first), :], buffer.at[pl.ds(first - ready, last - first), :])
             )
-    groups = chunk_groups(0, units, chunk, 2)
-    for first, last in groups:
-        span = pl.ds(first, last - first)
-        pairs.append((down.reshape(units, model).at[span, :], down_all.at[span, :]))
+    half = quarter // 2
+    flat = down.reshape(units, model)
+    for buffer, at in ((down_theirs, jnp.where(lower, 1, 0)), (down_own, jnp.where(lower, 0, 1))):
+        for j in range(head_count):
+            start = pl.multiple_of((2 * j + at) * half, half)
+            pairs.append((flat.at[:, pl.ds(start, half)], buffer.at[:, pl.ds(j * half, half)]))
     loads = start_all(tuple(pairs), sems)
     for i in range(req_count):
         for j in range(head_count):
@@ -293,26 +297,42 @@
         )
         active = gate_part / (1.0 + jnp.exp(-gate_part)) * up_part * weight
         active_all[:, first : first + chunk] = active.T.astype(bf16)
-    for c in range(model // LANES):
+    for _ in range(head_count):
+        loads.pop(0).wait()
+    active_out[...] = active_all[...]
+    down_half(active_all, down_theirs, theirs_out, total)
+    for load in loads:
+        load.wait()
+
+
+def down_half(active, weights, out, total):
+    groups, rows, _ = total.shape
+    live = active.shape[0]
+    req_count = rows // ROWS
+    head_count = out.shape[0] // req_count
+    product = jnp.dot(active[...], weights[...], preferred_element_type=f32)
+    for c in range(groups):
+        total[c, :live, :] = product[:, c * LANES : (c + 1) * LANES]
         total[c, live:, :] = jnp.zeros((req_count, LANES), f32)
-    for n, (first, last) in enumerate(groups):
-        loads.pop(0).wait()
-        product = jnp.dot(
-            active_all[:, first:last], down_all[first:last, :], preferred_element_type=f32
-        )
-        for c in range(model // LANES):
-            share = product[:, c * LANES : (c + 1) * LANES]
-            total[c, :live, :] = share if n == 0 else total[c, :live, :] + share
+    wide = groups // head_count
     for i in range(req_count):
         for j in range(head_count):
-            for c in range(quarter // LANES):
+            for c in range(wide):
                 out[i * head_count + j, :, c * LANES : (c + 1) * LANES] = total[
-                    j * quarter // LANES + c, pl.ds(i, ROWS, stride=req_count), :
-                ].astype(bf16)
+                    j * wide + c, pl.ds(i, ROWS, stride=req_count), :
+                ].astype(out.dtype)
+
+
+def join_kernel(mine, theirs, out):
+    out[...] = (mine[...] + theirs[...].astype(f32)).astype(bf16)
 
 
 def final_kernel(parts, mixed, out):
-    total = jnp.sum(parts[...].astype(f32), axis=0)
+    halves = []
+    for side in range(2):
+        sources = [parts[n].astype(f32) for n in range(side, parts.shape[0], 2)]
+        halves.append(functools.reduce(jnp.add, sources))
+    total = jnp.concatenate(halves, axis=1)
     out[...] = (mixed[...] + total[: mixed.shape[0]]).astype(bf16)
 
 
@@ -445,24 +465,48 @@
     gate_c, up_c = fetch(tokens, (gate, (split_b, split_c)), (up, (split_b, split_c)))
     tokens_near = swap(tokens, 1)
     ready = (gate_a, up_a, gate_b, up_b, gate_c, up_c)
-    parts = pl.pallas_call(
+    theirs, active, down_own = pl.pallas_call(
         functools.partial(expert_kernel, chunk),
-        out_shape=jax.ShapeDtypeStruct((devices, ROWS, quarter), bf16),
+        out_shape=(
+            jax.ShapeDtypeStruct((devices, ROWS, half), bf16),
+            pltpu.VMEM((requests * req_count, units), bf16),
+            pltpu.VMEM((units, model // 2), bf16),
+        ),
         in_specs=[VMEM] * 9 + [ANY] * 3,
-        out_specs=VMEM,
+        out_specs=[VMEM] * 3,
         scratch_shapes=[
             pltpu.VMEM((model // LANES, ROWS * req_count, LANES), f32),
             pltpu.VMEM((requests * req_count, 3 * EXPERTS), f32),
             pltpu.VMEM((requests * req_count, units), bf16),
-            pltpu.VMEM((model // LANES, ROWS * req_count, LANES), f32),
+            pltpu.VMEM((model // 2 // LANES, ROWS * req_count, LANES), f32),
             pltpu.VMEM((units - split_c, model), bf16),
             pltpu.VMEM((units - split_c, model), bf16),
-            pltpu.VMEM((units, model), bf16),
-            pltpu.SemaphoreType.DMA((6,)),
+            pltpu.VMEM((units, model // 2), bf16),
+            pltpu.SemaphoreType.DMA((2 + 2 * head_count,)),
         ],
         compiler_params=limit(32),
         name="experts",
     )(tokens, tokens_near, gain, *ready, *on_hbm(gate, up, down_weight))
+    mine_half = pl.pallas_call(
+        down_half,
+        out_shape=jax.ShapeDtypeStruct((devices, ROWS, half), f32),
+        in_specs=[VMEM] * 2,
+        out_specs=VMEM,
+        scratch_shapes=[pltpu.VMEM((model // 2 // LANES, ROWS * req_count, LANES), f32)],
+        compiler_params=limit(12),
+        cost_estimate=pl.CostEstimate(
+            flops=2 * requests * req_count * units * model, bytes_accessed=units * model, transcendentals=0
+        ),
+        name="down",
+    )(active, down_own)
+    parts = pl.pallas_call(
+        join_kernel,
+        out_shape=jax.ShapeDtypeStruct((devices, ROWS, half), bf16),
+        in_specs=[VMEM] * 2,
+        out_specs=VMEM,
+        compiler_params=limit(12),
+        name="join",
+    )(mine_half, swap(theirs, 1))
     parts = lax.all_to_all(parts, both, split_axis=0, concat_axis=0, tiled=True)
     return pl.pallas_call(
         final_kernel,

time: 54.4 us -> 52.8 us (0.971)
  blocking collectives: 26.4 us -> 24.1 us
    all_to_all x1, blocking collectives: 12.3 us -> 10 us  [per_device(): parts = lax.all_to_all(parts, both, split_axis=0, concat_axis=0, tiled=True)]
    ppermute x7 -> x8, starting transfers between devices: 7.22 us -> 7.58 us  [swap(): lax.ppermute(value, 'head', [(n, n ^ flip) for n in range(head_count)])]
    pallas_call x1 -> x3, Pallas kernels: 9.31 us -> 9.6 us  [the longest x1 8.41 us: per_device(): pl.pallas_call(functools.partial(expert_kernel, chunk), out_shape=(jax.Sh...]
  transfers between devices with their start and end apart: 7 -> 8, of which waited for: 1 -> 1; matrix products, arithmetic and copies ran while one was open for 0% -> 0% of each run, Pallas kernels for 16% -> 19%
where the time goes in v4:
time: 52.8 us; the launch traced here: 52.6 us
  blocking collectives  24.1 us (46%)
  Pallas kernels  20.4 us (39%)
  starting transfers between devices  7.58 us (14%)
    all_to_all x1, blocking collectives, per_device(): lax.all_to_all(spread, both, split_axis=0, concat_axis=0, tiled=True)  14.1 us
    all_to_all x1, blocking collectives, per_device(): parts = lax.all_to_all(parts, both, split_axis=0, concat_axis=0, tiled=True)  10 us
    pallas_call x1, Pallas kernels, per_device(): pl.pallas_call(functools.partial(expert_kernel, chunk), out_shape=(jax.Sh...  8.41 us
    ppermute x8, starting transfers between devices, swap(): lax.ppermute(value, 'head', [(n, n ^ flip) for n in range(head_count)])  7.58 us
    pallas_call x3, Pallas kernels, fetch(): pl.pallas_call(functools.partial(fetch_kernel, spans), out_shape=shapes,...  6.66 us
    pallas_call x1, Pallas kernels, per_device(): pl.pallas_call(stage_kernel, out_shape=(pltpu.VMEM((2 * pages_here, rows,...  1.97 us
    pallas_call x1, Pallas kernels, per_device(): pl.pallas_call(down_half, out_shape=jax.ShapeDtypeStruct((devices, ROWS,...  1.16 us
  transfers between devices with their start and end apart: 8, of which 1 were waited for; matrix products, arithmetic and copies ran while one was open for 0% of the time, Pallas kernels for 19%

profile of v4, /device:TPU:0, one launch (start us, length us, event | category | flops | bytes accessed | tf_op | source)
XLA Modules:
  0.0 52.6 jit_solution(9562257322671096127)
XLA Ops:
  0.0 0.5 collective-permute-start.1
  0.5 2.5 %collective-permute-start = (bf16[7,4,576]{2,1,0:T(4,128)(2,1)}, bf16[7,4,576]{2,1,0:T(4,128)(2,1)S(1)}, u32[]{:S(2)}, u32[]{:S(2)}) collective-permute-start(bf16[7,4,576]{2,1,0:T(4,128)(2,1)} %refs_4_.1), channel_id=1, source_target_pairs={{0,2},{1,3},{2,0},{3,1},{4,6},{5,7},{6,4},{7,5},{8,10},{9,11},{10,... | collective-permute-start | bytes 96776 | tf_op jit(solution)/shard_map/ppermute | solution.py:369
  3.0 2.0 %stage.1 = (f32[4,64,128]{2,1,0:T(8,128)S(1)}, f32[1,512]{1,0:T(1,128)S(1)}, bf16[7,4,576]{2,1,0:T(4,128)(2,1)S(1)}, bf16[2,576,128]{2,1,0:T(8,128)(2,1)S(1)}, b...) custom-call(s32[2,7]{1,0:T(2,128)} %bitcast.16, ...), custom_call_target="tpu_custom_call" | custom-call | bytes 3145728 | tf_op jit(solution)/shard_map/stage/pallas_call | solution.py:401
  4.9 0.4 collective-permute-done.q_far
  5.3 0.8 %attend.1 = (f32[4,8,512]{2,1,0:T(8,128)S(1)}, f32[4,8,128]{2,1,0:T(8,128)S(1)}, bf16[4,8,640]{2,1,0:T(8,128)(2,1)S(1)}) custom-call(f32[4,64,128]{2,1,0:T(8,128)S(1)} %get-tuple-element.31.usable, bf16[7,4,576]{2,1,0:T(4,128)(2,1)S(1)} %get-tuple-element.32.q_own, bf16[7,4,576]{2,1,0:T(4,128)(2,1)S(1)} %collective-permute-done.q_far, ...), custom_call_target="tpu_custom_call" | custom-call | tf_op jit(solution)/shard_map/attend/pallas_call | solution.py:422
  6.1 1.9 %collective-permute-start.2 = (bf16[4,8,640]{2,1,0:T(8,128)(2,1)S(1)}, bf16[4,8,640]{2,1,0:T(8,128)(2,1)S(1)}, u32[]{:S(2)}, u32[]{:S(2)}) collective-permute-start(bf16[4,8,640]{2,1,0:T(8,128)(2,1)S(1)} %get-tuple-element.36.refs_2_), channel_id=1, source_target_pairs={{0,2},{1,3},{2,0},{3,1},{4,6},{5,7},{6,4},{7,5},{8,10},{9,11},{10,... | collective-permute-start | bytes 122888 | tf_op jit(solution)/shard_map/ppermute | solution.py:369
  8.0 2.2 %fetch.3 = (bf16[512,2048]{1,0:T(8,128)(2,1)S(1)}, bf16[512,2048]{1,0:T(8,128)(2,1)S(1)}) custom-call(bf16[16,176,2048]{2,1,0:T(8,128)(2,1)} %bitcast.5, bf16[16,176,2048]{2,1,0:T(8,128)(2,1)} %bitcast.9, bf16[4,8,640]{2,1,0:T(8,128)(2,1)S(1)} %get-tuple-element.36.refs_2_), custom_call_target="tpu_custom_call" | custom-call | bytes 4194304 | tf_op jit(solution)/shard_map/fetch/pallas_call | solution.py:378
  10.3 0.0 collective-permute-done.2.far
  10.3 0.7 %project.1 = (f32[8,512]{1,0:T(8,128)S(1)}, bf16[8,512]{1,0:T(8,128)(2,1)S(1)}, bf16[8,512]{1,0:T(8,128)(2,1)S(1)}, bf16[8,512]{1,0:T(8,128)(2,1)S(1)}) custom-call(f32[4,8,512]{2,1,0:T(8,128)S(1)} %get-tuple-element.34.own, f32[4,8,128]{2,1,0:T(8,128)S(1)} %get-tuple-element.35.own_lse, bf16[4,8,640]{2,1,0:T(8,128)(2,1)S(1)} %collective-permute-done.2.far, ...), custom_call_target="tpu_custom_call" | custom-call | tf_op jit(solution)/shard_map/project/pallas_call | solution.py:442
  11.0 1.8 %collective-permute-start.4 = (bf16[8,512]{1,0:T(8,128)(2,1)S(1)}, bf16[8,512]{1,0:T(8,128)(2,1)S(1)}, u32[]{:S(2)}, u32[]{:S(2)}) collective-permute-start(bf16[8,512]{1,0:T(8,128)(2,1)S(1)} %get-tuple-element.42), channel_id=1, source_target_pairs={{0,2},{1,3},{2,0},{3,1},{4,6},{5,7},{6,4},{7,5},{8,10},{9,11},{10,... | collective-permute-start | bytes 24584 | tf_op jit(solution)/shard_map/ppermute | solution.py:369
  12.7 0.0 collective-permute-start.5
  12.7 0.4 collective-permute-start.3
  13.1 2.9 %fetch.4 = (bf16[768,2048]{1,0:T(8,128)(2,1)S(1)}, bf16[768,2048]{1,0:T(8,128)(2,1)S(1)}) custom-call(bf16[16,176,2048]{2,1,0:T(8,128)(2,1)} %bitcast.6, bf16[16,176,2048]{2,1,0:T(8,128)(2,1)} %bitcast.10, bf16[8,512]{1,0:T(8,128)(2,1)S(1)} %get-tuple-element.41.refs_2_), custom_call_target="tpu_custom_call" | custom-call | bytes 6291456 | tf_op jit(solution)/shard_map/fetch/pallas_call | solution.py:378
  16.0 0.0 collective-permute-done.5.far_both
  16.0 0.0 collective-permute-done.3.near
  16.0 14.1 %all_to_all.10.refs_2_.tokens = bf16[32,8,256]{2,1,0:T(8,128)(2,1)S(1)} all-to-all(bf16[32,8,256]{2,1,0:T(8,128)(2,1)S(1)} %get-tuple-element.47), channel_id=1, replica_groups=mesh['req'=8,'head'=4] {'req','head'}, dimensions={0} | all-to-all | bytes 262144 | tf_op jit(solution)/shard_map/all_to_all | solution.py:464
  30.1 0.2 collective-permute-start.6
  30.4 1.6 %fetch.5 = (bf16[256,2048]{1,0:T(8,128)(2,1)S(1)}, bf16[256,2048]{1,0:T(8,128)(2,1)S(1)}) custom-call(bf16[16,176,2048]{2,1,0:T(8,128)(2,1)} %bitcast.7, bf16[16,176,2048]{2,1,0:T(8,128)(2,1)} %bitcast.11, bf16[32,8,256]{2,1,0:T(8,128)(2,1)S(1)} %all_to_all.10.refs_2_.tokens), custom_call_target="tpu_custom_call" | custom-call | bytes 2097152 | tf_op jit(solution)/shard_map/fetch/pallas_call | solution.py:378
  31.9 0.0 collective-permute-done.6.tokens_near
  31.9 8.4 %experts.1 = (bf16[32,8,256]{2,1,0:T(8,128)(2,1)S(1)}, bf16[56,2816]{1,0:T(8,128)(2,1)S(1)}, bf16[2816,1024]{1,0:T(8,128)(2,1)S(1)}) custom-call(bf16[32,8,256]{2,1,0:T(8,128)(2,1)S(1)} %all_to_all.10.refs_2_.tokens, bf16[32,8,256]{2,1,0:T(8,128)(2,1)S(1)} %collective-permute-done.6.tokens_near, f32[1,2048]{1,0:T(1,128)S(1)} %get-tuple-element.48.gain, ...), custom_call_target="tpu_custom_call" | custom-call | tf_op jit(solution)/shard_map/experts/pallas_call | solution.py:468
  40.4 0.4 collective-permute-start.7
  40.7 1.2 %down.3.mine = f32[32,8,256]{2,1,0:T(8,128)S(1)} custom-call(bf16[56,2816]{1,0:T(8,128)(2,1)S(1)} %get-tuple-element.53.active, bf16[2816,1024]{1,0:T(8,128)(2,1)S(1)} %get-tuple-element.54.weights), custom_call_target="tpu_custom_call" | custom-call | flops 645922816 | bytes 5767168 | tf_op jit(solution)/shard_map/down/pallas_call | solution.py:490
  41.9 10.0 %all_to_all.11.parts = bf16[32,8,256]{2,1,0:T(8,128)(2,1)S(1)} all-to-all(bf16[32,8,256]{2,1,0:T(8,128)(2,1)S(1)} %join.1), channel_id=1, replica_groups=mesh['req'=8,'head'=4] {'req','head'}, dimensions={0} | all-to-all | bytes 262144 | tf_op jit(solution)/shard_map/all_to_all | solution.py:510
  51.9 0.6 %final.1 = bf16[7,512]{1,0:T(8,128)(2,1)} custom-call(bf16[32,8,256]{2,1,0:T(8,128)(2,1)S(1)} %all_to_all.11.parts, f32[7,512]{1,0:T(8,128)S(1)} %get-tuple-element.56.mixed), custom_call_target="tpu_custom_call" | custom-call | tf_op jit(solution)/shard_map/final/pallas_call | solution.py:511
  (5 shorter events, 0.1 us)
Async XLA Ops:
  0.0 5.3 %collective-permute-start.1 = (bf16[2,576,128]{2,1,0:T(8,128)(2,1)}, bf16[2,576,128]{2,1,0:T(8,128)(2,1)S(1)}, u32[]{:S(2)}, u32[]{:S(2)}) collective-permute-start(bf16[2,576,128]{2,1,0:T(8,128)(2,1)} %bitcast.13), channel_id=1, source_target_pairs={{0,1},{1,0},{2,3},{3,2},{4,5},{5,4},{6,7},{7,6},{8,9},{9,8},{10,11... | collective-permute-start | bytes 884744 | tf_op jit(solution)/shard_map/ppermute | solution.py:369
  0.5 4.9 %collective-permute-start = (bf16[7,4,576]{2,1,0:T(4,128)(2,1)}, bf16[7,4,576]{2,1,0:T(4,128)(2,1)S(1)}, u32[]{:S(2)}, u32[]{:S(2)}) collective-permute-start(bf16[7,4,576]{2,1,0:T(4,128)(2,1)} %refs_4_.1), channel_id=1, source_target_pairs={{0,2},{1,3},{2,0},{3,1},{4,6},{5,7},{6,4},{7,5},{8,10},{9,11},{10,... | collective-permute-start | bytes 96776 | tf_op jit(solution)/shard_map/ppermute | solution.py:369
  6.1 4.1 %collective-permute-start.2 = (bf16[4,8,640]{2,1,0:T(8,128)(2,1)S(1)}, bf16[4,8,640]{2,1,0:T(8,128)(2,1)S(1)}, u32[]{:S(2)}, u32[]{:S(2)}) collective-permute-start(bf16[4,8,640]{2,1,0:T(8,128)(2,1)S(1)} %get-tuple-element.36.refs_2_), channel_id=1, source_target_pairs={{0,2},{1,3},{2,0},{3,1},{4,6},{5,7},{6,4},{7,5},{8,10},{9,11},{10,... | collective-permute-start | bytes 122888 | tf_op jit(solution)/shard_map/ppermute | solution.py:369
  11.0 5.0 %collective-permute-start.4 = (bf16[8,512]{1,0:T(8,128)(2,1)S(1)}, bf16[8,512]{1,0:T(8,128)(2,1)S(1)}, u32[]{:S(2)}, u32[]{:S(2)}) collective-permute-start(bf16[8,512]{1,0:T(8,128)(2,1)S(1)} %get-tuple-element.42), channel_id=1, source_target_pairs={{0,2},{1,3},{2,0},{3,1},{4,6},{5,7},{6,4},{7,5},{8,10},{9,11},{10,... | collective-permute-start | bytes 24584 | tf_op jit(solution)/shard_map/ppermute | solution.py:369
  12.7 3.3 %collective-permute-start.5 = (bf16[8,512]{1,0:T(8,128)(2,1)S(1)}, bf16[8,512]{1,0:T(8,128)(2,1)S(1)}, u32[]{:S(2)}, u32[]{:S(2)}) collective-permute-start(bf16[8,512]{1,0:T(8,128)(2,1)S(1)} %get-tuple-element.43), channel_id=1, source_target_pairs={{0,3},{1,2},{2,1},{3,0},{4,7},{5,6},{6,5},{7,4},{8,11},{9,10},{10,... | collective-permute-start | bytes 24584 | tf_op jit(solution)/shard_map/ppermute | solution.py:369
  12.7 3.3 %collective-permute-start.3 = (bf16[8,512]{1,0:T(8,128)(2,1)S(1)}, bf16[8,512]{1,0:T(8,128)(2,1)S(1)}, u32[]{:S(2)}, u32[]{:S(2)}) collective-permute-start(bf16[8,512]{1,0:T(8,128)(2,1)S(1)} %get-tuple-element.41.refs_2_), channel_id=1, source_target_pairs={{0,1},{1,0},{2,3},{3,2},{4,5},{5,4},{6,7},{7,6},{8,9},{9,8},{10,11... | collective-permute-start | bytes 24584 | tf_op jit(solution)/shard_map/ppermute | solution.py:369
  30.1 1.8 %collective-permute-start.6 = (bf16[32,8,256]{2,1,0:T(8,128)(2,1)S(1)}, bf16[32,8,256]{2,1,0:T(8,128)(2,1)S(1)}, u32[]{:S(2)}, u32[]{:S(2)}) collective-permute-start(bf16[32,8,256]{2,1,0:T(8,128)(2,1)S(1)} %all_to_all.10.refs_2_.tokens), channel_id=1, source_target_pairs={{0,1},{1,0},{2,3},{3,2},{4,5},{5,4},{6,7},{7,6},{8,9},{9,8},{10,11... | collective-permute-start | bytes 393224 | tf_op jit(solution)/shard_map/ppermute | solution.py:369
  40.4 1.5 %collective-permute-start.7 = (bf16[32,8,256]{2,1,0:T(8,128)(2,1)S(1)}, bf16[32,8,256]{2,1,0:T(8,128)(2,1)S(1)}, u32[]{:S(2)}, u32[]{:S(2)}) collective-permute-start(bf16[32,8,256]{2,1,0:T(8,128)(2,1)S(1)} %get-tuple-element.55), channel_id=1, source_target_pairs={{0,1},{1,0},{2,3},{3,2},{4,5},{5,4},{6,7},{7,6},{8,9},{9,8},{10,11... | collective-permute-start | bytes 393224 | tf_op jit(solution)/shard_map/ppermute | solution.py:369

commit v5 on v4

--- a/solution.py
+++ b/solution.py
@@ -175,7 +175,7 @@
     quarter = mine.shape[1]
     mine[...] = whole[:, pl.ds(pl.multiple_of(head_at * quarter, quarter), quarter)]
     for out, flip in ((near, 1), (far_y, 2), (far_both, 3)):
-        start = pl.multiple_of((head_at ^ flip) * quarter, quarter)
+        start = pl.multiple_of((head_at + flip) % 4 * quarter, quarter)
         out[...] = whole[:, pl.ds(start, quarter)].astype(bf16)
 
 
@@ -449,7 +449,10 @@
         name="project",
     )(own, own_lse, far, value_up, out_proj, gate_a)
     gate_b, up_b = fetch(near, (gate, (split_a, split_b)), (up, (split_a, split_b)))
-    near, far_y, far_both = swap(near, 1), swap(far_y, 2), swap(far_both, 3)
+    near, far_y, far_both = (
+        lax.ppermute(piece, "head", [(n, (n + step) % head_count) for n in range(head_count)])
+        for step, piece in ((1, near), (2, far_y), (3, far_both))
+    )
     mixed, spread = pl.pallas_call(
         mix_kernel,
         out_shape=(

time: 52.8 us -> 52.4 us (level)
    ppermute x0 -> x3, starting transfers between devices: none -> 2.26 us  [per_device(): lax.ppermute(piece, 'head', [(n, (n + step) % head_count) for n in range(...]
    ppermute x8 -> x5, starting transfers between devices: 7.58 us -> 5.43 us  [swap(): lax.ppermute(value, 'head', [(n, n ^ flip) for n in range(head_count)])]
where the time goes in v5:
time: 52.4 us; the launch traced here: 52.2 us
  blocking collectives  23.6 us (45%)
  Pallas kernels  20.3 us (39%)
  starting transfers between devices  7.69 us (15%)
    all_to_all x1, blocking collectives, per_device(): lax.all_to_all(spread, both, split_axis=0, concat_axis=0, tiled=True)  13.6 us
    all_to_all x1, blocking collectives, per_device(): parts = lax.all_to_all(parts, both, split_axis=0, concat_axis=0, tiled=True)  10 us
    pallas_call x1, Pallas kernels, per_device(): pl.pallas_call(functools.partial(expert_kernel, chunk), out_shape=(jax.Sh...  8.4 us
    pallas_call x3, Pallas kernels, fetch(): pl.pallas_call(functools.partial(fetch_kernel, spans), out_shape=shapes,...  6.66 us
    ppermute x5, starting transfers between devices, swap(): lax.ppermute(value, 'head', [(n, n ^ flip) for n in range(head_count)])  5.43 us
    ppermute x3, starting transfers between devices, per_device(): lax.ppermute(piece, 'head', [(n, (n + step) % head_count) for n in range(...  2.26 us
    pallas_call x1, Pallas kernels, per_device(): pl.pallas_call(stage_kernel, out_shape=(pltpu.VMEM((2 * pages_here, rows,...  1.97 us
    pallas_call x1, Pallas kernels, per_device(): pl.pallas_call(down_half, out_shape=jax.ShapeDtypeStruct((devices, ROWS,...  1.16 us
  transfers between devices with their start and end apart: 8, of which 1 were waited for; matrix products, arithmetic and copies ran while one was open for 0% of the time, Pallas kernels for 19%

profile of v5, /device:TPU:0, one launch (start us, length us, event | category | flops | bytes accessed | tf_op | source)
XLA Modules:
  0.0 52.2 jit_solution(16705437416975060604)
XLA Ops:
  0.0 0.5 collective-permute-start.1
  0.5 2.5 %collective-permute-start = (bf16[7,4,576]{2,1,0:T(4,128)(2,1)}, bf16[7,4,576]{2,1,0:T(4,128)(2,1)S(1)}, u32[]{:S(2)}, u32[]{:S(2)}) collective-permute-start(bf16[7,4,576]{2,1,0:T(4,128)(2,1)} %refs_4_.1), channel_id=1, source_target_pairs={{0,2},{1,3},{2,0},{3,1},{4,6},{5,7},{6,4},{7,5},{8,10},{9,11},{10,... | collective-permute-start | bytes 96776 | tf_op jit(solution)/shard_map/ppermute | solution.py:369
  3.0 2.0 %stage.1 = (f32[4,64,128]{2,1,0:T(8,128)S(1)}, f32[1,512]{1,0:T(1,128)S(1)}, bf16[7,4,576]{2,1,0:T(4,128)(2,1)S(1)}, bf16[2,576,128]{2,1,0:T(8,128)(2,1)S(1)}, b...) custom-call(s32[2,7]{1,0:T(2,128)} %bitcast.16, ...), custom_call_target="tpu_custom_call" | custom-call | bytes 3145728 | tf_op jit(solution)/shard_map/stage/pallas_call | solution.py:401
  4.9 0.4 collective-permute-done.q_far
  5.3 0.8 %attend.1 = (f32[4,8,512]{2,1,0:T(8,128)S(1)}, f32[4,8,128]{2,1,0:T(8,128)S(1)}, bf16[4,8,640]{2,1,0:T(8,128)(2,1)S(1)}) custom-call(f32[4,64,128]{2,1,0:T(8,128)S(1)} %get-tuple-element.31.usable, bf16[7,4,576]{2,1,0:T(4,128)(2,1)S(1)} %get-tuple-element.32.q_own, bf16[7,4,576]{2,1,0:T(4,128)(2,1)S(1)} %collective-permute-done.q_far, ...), custom_call_target="tpu_custom_call" | custom-call | tf_op jit(solution)/shard_map/attend/pallas_call | solution.py:422
  6.1 1.9 %collective-permute-start.2 = (bf16[4,8,640]{2,1,0:T(8,128)(2,1)S(1)}, bf16[4,8,640]{2,1,0:T(8,128)(2,1)S(1)}, u32[]{:S(2)}, u32[]{:S(2)}) collective-permute-start(bf16[4,8,640]{2,1,0:T(8,128)(2,1)S(1)} %get-tuple-element.36.refs_2_), channel_id=1, source_target_pairs={{0,2},{1,3},{2,0},{3,1},{4,6},{5,7},{6,4},{7,5},{8,10},{9,11},{10,... | collective-permute-start | bytes 122888 | tf_op jit(solution)/shard_map/ppermute | solution.py:369
  8.0 2.2 %fetch.3 = (bf16[512,2048]{1,0:T(8,128)(2,1)S(1)}, bf16[512,2048]{1,0:T(8,128)(2,1)S(1)}) custom-call(bf16[16,176,2048]{2,1,0:T(8,128)(2,1)} %bitcast.5, bf16[16,176,2048]{2,1,0:T(8,128)(2,1)} %bitcast.9, bf16[4,8,640]{2,1,0:T(8,128)(2,1)S(1)} %get-tuple-element.36.refs_2_), custom_call_target="tpu_custom_call" | custom-call | bytes 4194304 | tf_op jit(solution)/shard_map/fetch/pallas_call | solution.py:378
  10.3 0.0 collective-permute-done.2.far
  10.3 0.7 %project.1 = (f32[8,512]{1,0:T(8,128)S(1)}, bf16[8,512]{1,0:T(8,128)(2,1)S(1)}, bf16[8,512]{1,0:T(8,128)(2,1)S(1)}, bf16[8,512]{1,0:T(8,128)(2,1)S(1)}) custom-call(f32[4,8,512]{2,1,0:T(8,128)S(1)} %get-tuple-element.34.own, f32[4,8,128]{2,1,0:T(8,128)S(1)} %get-tuple-element.35.own_lse, bf16[4,8,640]{2,1,0:T(8,128)(2,1)S(1)} %collective-permute-done.2.far, ...), custom_call_target="tpu_custom_call" | custom-call | tf_op jit(solution)/shard_map/project/pallas_call | solution.py:442
  11.0 1.8 %collective-permute-start.4 = (bf16[8,512]{1,0:T(8,128)(2,1)S(1)}, bf16[8,512]{1,0:T(8,128)(2,1)S(1)}, u32[]{:S(2)}, u32[]{:S(2)}) collective-permute-start(bf16[8,512]{1,0:T(8,128)(2,1)S(1)} %get-tuple-element.42), channel_id=1, source_target_pairs={{0,2},{1,3},{2,0},{3,1},{4,6},{5,7},{6,4},{7,5},{8,10},{9,11},{10,... | collective-permute-start | bytes 24584 | tf_op jit(solution)/shard_map/ppermute | solution.py:453
  12.7 0.0 collective-permute-start.5
  12.7 0.5 collective-permute-start.3
  13.2 2.9 %fetch.4 = (bf16[768,2048]{1,0:T(8,128)(2,1)S(1)}, bf16[768,2048]{1,0:T(8,128)(2,1)S(1)}) custom-call(bf16[16,176,2048]{2,1,0:T(8,128)(2,1)} %bitcast.6, bf16[16,176,2048]{2,1,0:T(8,128)(2,1)} %bitcast.10, bf16[8,512]{1,0:T(8,128)(2,1)S(1)} %get-tuple-element.41.refs_2_), custom_call_target="tpu_custom_call" | custom-call | bytes 6291456 | tf_op jit(solution)/shard_map/fetch/pallas_call | solution.py:378
  16.1 0.0 collective-permute-done.4.far_y
  16.1 0.0 collective-permute-done.3.near
  16.1 13.6 %all_to_all.10.refs_2_.tokens = bf16[32,8,256]{2,1,0:T(8,128)(2,1)S(1)} all-to-all(bf16[32,8,256]{2,1,0:T(8,128)(2,1)S(1)} %get-tuple-element.47), channel_id=1, replica_groups=mesh['req'=8,'head'=4] {'req','head'}, dimensions={0} | all-to-all | bytes 262144 | tf_op jit(solution)/shard_map/all_to_all | solution.py:467
  29.8 0.2 collective-permute-start.6
  30.0 1.6 %fetch.5 = (bf16[256,2048]{1,0:T(8,128)(2,1)S(1)}, bf16[256,2048]{1,0:T(8,128)(2,1)S(1)}) custom-call(bf16[16,176,2048]{2,1,0:T(8,128)(2,1)} %bitcast.7, bf16[16,176,2048]{2,1,0:T(8,128)(2,1)} %bitcast.11, bf16[32,8,256]{2,1,0:T(8,128)(2,1)S(1)} %all_to_all.10.refs_2_.tokens), custom_call_target="tpu_custom_call" | custom-call | bytes 2097152 | tf_op jit(solution)/shard_map/fetch/pallas_call | solution.py:378
  31.5 8.4 %experts.1 = (bf16[32,8,256]{2,1,0:T(8,128)(2,1)S(1)}, bf16[56,2816]{1,0:T(8,128)(2,1)S(1)}, bf16[2816,1024]{1,0:T(8,128)(2,1)S(1)}) custom-call(bf16[32,8,256]{2,1,0:T(8,128)(2,1)S(1)} %all_to_all.10.refs_2_.tokens, bf16[32,8,256]{2,1,0:T(8,128)(2,1)S(1)} %collective-permute-done.6.tokens_near, f32[1,2048]{1,0:T(1,128)S(1)} %get-tuple-element.48.gain, ...), custom_call_target="tpu_custom_call" | custom-call | tf_op jit(solution)/shard_map/experts/pallas_call | solution.py:471
  40.0 0.4 collective-permute-start.7
  40.3 1.2 %down.3.mine = f32[32,8,256]{2,1,0:T(8,128)S(1)} custom-call(bf16[56,2816]{1,0:T(8,128)(2,1)S(1)} %get-tuple-element.53.active, bf16[2816,1024]{1,0:T(8,128)(2,1)S(1)} %get-tuple-element.54.weights), custom_call_target="tpu_custom_call" | custom-call | flops 645922816 | bytes 5767168 | tf_op jit(solution)/shard_map/down/pallas_call | solution.py:493
  41.5 0.0 collective-permute-done.7.theirs
  41.5 10.0 %all_to_all.11.parts = bf16[32,8,256]{2,1,0:T(8,128)(2,1)S(1)} all-to-all(bf16[32,8,256]{2,1,0:T(8,128)(2,1)S(1)} %join.1), channel_id=1, replica_groups=mesh['req'=8,'head'=4] {'req','head'}, dimensions={0} | all-to-all | bytes 262144 | tf_op jit(solution)/shard_map/all_to_all | solution.py:513
  51.5 0.6 %final.1 = bf16[7,512]{1,0:T(8,128)(2,1)} custom-call(bf16[32,8,256]{2,1,0:T(8,128)(2,1)S(1)} %all_to_all.11.parts, f32[7,512]{1,0:T(8,128)S(1)} %get-tuple-element.56.mixed), custom_call_target="tpu_custom_call" | custom-call | tf_op jit(solution)/shard_map/final/pallas_call | solution.py:514
  (5 shorter events, 0.1 us)
Async XLA Ops:
  0.0 5.3 %collective-permute-start.1 = (bf16[2,576,128]{2,1,0:T(8,128)(2,1)}, bf16[2,576,128]{2,1,0:T(8,128)(2,1)S(1)}, u32[]{:S(2)}, u32[]{:S(2)}) collective-permute-start(bf16[2,576,128]{2,1,0:T(8,128)(2,1)} %bitcast.13), channel_id=1, source_target_pairs={{0,1},{1,0},{2,3},{3,2},{4,5},{5,4},{6,7},{7,6},{8,9},{9,8},{10,11... | collective-permute-start | bytes 884744 | tf_op jit(solution)/shard_map/ppermute | solution.py:369
  0.5 4.9 %collective-permute-start = (bf16[7,4,576]{2,1,0:T(4,128)(2,1)}, bf16[7,4,576]{2,1,0:T(4,128)(2,1)S(1)}, u32[]{:S(2)}, u32[]{:S(2)}) collective-permute-start(bf16[7,4,576]{2,1,0:T(4,128)(2,1)} %refs_4_.1), channel_id=1, source_target_pairs={{0,2},{1,3},{2,0},{3,1},{4,6},{5,7},{6,4},{7,5},{8,10},{9,11},{10,... | collective-permute-start | bytes 96776 | tf_op jit(solution)/shard_map/ppermute | solution.py:369
  6.1 4.1 %collective-permute-start.2 = (bf16[4,8,640]{2,1,0:T(8,128)(2,1)S(1)}, bf16[4,8,640]{2,1,0:T(8,128)(2,1)S(1)}, u32[]{:S(2)}, u32[]{:S(2)}) collective-permute-start(bf16[4,8,640]{2,1,0:T(8,128)(2,1)S(1)} %get-tuple-element.36.refs_2_), channel_id=1, source_target_pairs={{0,2},{1,3},{2,0},{3,1},{4,6},{5,7},{6,4},{7,5},{8,10},{9,11},{10,... | collective-permute-start | bytes 122888 | tf_op jit(solution)/shard_map/ppermute | solution.py:369
  11.0 5.1 %collective-permute-start.4 = (bf16[8,512]{1,0:T(8,128)(2,1)S(1)}, bf16[8,512]{1,0:T(8,128)(2,1)S(1)}, u32[]{:S(2)}, u32[]{:S(2)}) collective-permute-start(bf16[8,512]{1,0:T(8,128)(2,1)S(1)} %get-tuple-element.42), channel_id=1, source_target_pairs={{0,2},{1,3},{2,0},{3,1},{4,6},{5,7},{6,4},{7,5},{8,10},{9,11},{10,... | collective-permute-start | bytes 24584 | tf_op jit(solution)/shard_map/ppermute | solution.py:453
  12.7 3.4 %collective-permute-start.5 = (bf16[8,512]{1,0:T(8,128)(2,1)S(1)}, bf16[8,512]{1,0:T(8,128)(2,1)S(1)}, u32[]{:S(2)}, u32[]{:S(2)}) collective-permute-start(bf16[8,512]{1,0:T(8,128)(2,1)S(1)} %get-tuple-element.43), channel_id=1, source_target_pairs={{0,3},{1,0},{2,1},{3,2},{4,7},{5,4},{6,5},{7,6},{8,11},{9,8},{10,9... | collective-permute-start | bytes 24584 | tf_op jit(solution)/shard_map/ppermute | solution.py:453
  12.7 3.4 %collective-permute-start.3 = (bf16[8,512]{1,0:T(8,128)(2,1)S(1)}, bf16[8,512]{1,0:T(8,128)(2,1)S(1)}, u32[]{:S(2)}, u32[]{:S(2)}) collective-permute-start(bf16[8,512]{1,0:T(8,128)(2,1)S(1)} %get-tuple-element.41.refs_2_), channel_id=1, source_target_pairs={{0,1},{1,2},{2,3},{3,0},{4,5},{5,6},{6,7},{7,4},{8,9},{9,10},{10,1... | collective-permute-start | bytes 24584 | tf_op jit(solution)/shard_map/ppermute | solution.py:453
  29.8 1.8 %collective-permute-start.6 = (bf16[32,8,256]{2,1,0:T(8,128)(2,1)S(1)}, bf16[32,8,256]{2,1,0:T(8,128)(2,1)S(1)}, u32[]{:S(2)}, u32[]{:S(2)}) collective-permute-start(bf16[32,8,256]{2,1,0:T(8,128)(2,1)S(1)} %all_to_all.10.refs_2_.tokens), channel_id=1, source_target_pairs={{0,1},{1,0},{2,3},{3,2},{4,5},{5,4},{6,7},{7,6},{8,9},{9,8},{10,11... | collective-permute-start | bytes 393224 | tf_op jit(solution)/shard_map/ppermute | solution.py:369
  40.0 1.5 %collective-permute-start.7 = (bf16[32,8,256]{2,1,0:T(8,128)(2,1)S(1)}, bf16[32,8,256]{2,1,0:T(8,128)(2,1)S(1)}, u32[]{:S(2)}, u32[]{:S(2)}) collective-permute-start(bf16[32,8,256]{2,1,0:T(8,128)(2,1)S(1)} %get-tuple-element.55), channel_id=1, source_target_pairs={{0,1},{1,0},{2,3},{3,2},{4,5},{5,4},{6,7},{7,6},{8,9},{9,8},{10,11... | collective-permute-start | bytes 393224 | tf_op jit(solution)/shard_map/ppermute | solution.py:369

commit v6 on v5

--- a/solution.py
+++ b/solution.py
@@ -47,12 +47,15 @@
 
 def stage_kernel(*refs):
     table_in, lens_in, ids_in, mix_in = refs[:4]
-    bias_out, route_out = refs[10:12]
-    table, lens, ids, mix, small_sems, sems = refs[18:]
+    bias_out, route_out = refs[11:13]
+    weight, first_out = refs[10], refs[19]
+    table, lens, ids, mix, small_sems, sems = refs[20:]
     small = start_all(
         ((table_in, table), (lens_in, lens), (ids_in, ids), (mix_in, mix)), small_sems
     )
-    large = start_all(tuple(zip(refs[4:10], refs[12:18])), sems)
+    flat = weight.reshape(weight.shape[0] * weight.shape[1], weight.shape[2])
+    first = (flat.at[pl.ds(0, first_out.shape[0]), :], first_out)
+    large = start_all((*zip(refs[4:10], refs[13:19]), first), sems)
     for copy in small:
         copy.wait()
     head_at = lax.axis_index("head")
@@ -208,6 +211,7 @@
     tokens,
     tokens_near,
     gain,
+    gate_z,
     gate_a,
     up_a,
     gate_b,
@@ -238,7 +242,7 @@
     requests = ROWS - 1
     live = requests * req_count
     units = slots * depth
-    ready = gate_a.shape[0] + gate_b.shape[0] + gate_c.shape[0]
+    ready = up_a.shape[0] + up_b.shape[0] + up_c.shape[0]
     pairs = []
     halves = chunk_groups(ready, units, chunk, 1)
     for first, last in halves:
@@ -278,10 +282,11 @@
     slot_at = req_at * slots + lax.broadcasted_iota(jnp.int32, expert.shape, 0)
     chosen = jnp.where(expert == slot_at // 2, 1.0, 0.0).astype(bf16)
     by_slot = lax.dot_general(chosen, mix_rows, NT, preferred_element_type=f32)
-    homes = []
-    for gate_at, up_at in ((gate_a, up_a), (gate_b, up_b), (gate_c, up_c), (gate_d, up_d)):
-        homes += [(gate_at, up_at, offset) for offset in range(0, gate_at.shape[0], chunk)]
-    for first, (gate_at, up_at, offset) in zip(range(0, units, chunk), homes):
+    gates, ups = (
+        [(part, offset) for part in parts for offset in range(0, part.shape[0], chunk)]
+        for parts in ((gate_z, gate_a, gate_b, gate_c, gate_d), (up_a, up_b, up_c, up_d))
+    )
+    for first, (gate_at, gate_from), (up_at, up_from) in zip(range(0, units, chunk), gates, ups):
         if first in [start for start, _ in halves]:
             loads.pop(0).wait()
             loads.pop(0).wait()
@@ -290,10 +295,10 @@
         for slot in range(first // depth + 1, (first + chunk - 1) // depth + 1):
             weight = jnp.where(unit >= slot * depth, by_slot[slot : slot + 1, :], weight)
         gate_part = lax.dot_general(
-            gate_at[offset : offset + chunk, :], normed, NT, preferred_element_type=f32
+            gate_at[gate_from : gate_from + chunk, :], normed, NT, preferred_element_type=f32
         )
         up_part = lax.dot_general(
-            up_at[offset : offset + chunk, :], normed, NT, preferred_element_type=f32
+            up_at[up_from : up_from + chunk, :], normed, NT, preferred_element_type=f32
         )
         active = gate_part / (1.0 + jnp.exp(-gate_part)) * up_part * weight
         active_all[:, first : first + chunk] = active.T.astype(bf16)
@@ -389,7 +394,8 @@
     slots, _, depth = gate_weight.shape
     units = slots * depth
     chunk = units // 11
-    split_a, split_b, split_c = 2 * chunk, 5 * chunk, 6 * chunk
+    split_z, up_a_end = chunk, 2 * chunk
+    split_a, split_b, split_c = 3 * chunk, 5 * chunk, 6 * chunk
     gate = jnp.swapaxes(gate_weight, 1, 2)
     up = jnp.swapaxes(up_weight, 1, 2)
     cache = jnp.swapaxes(latent_cache, 1, 2)
@@ -398,27 +404,28 @@
     q_far = swap(queries, 2)
     cache_near = swap(cache, 1)
     large = (queries, cache, value_up, out_proj, hidden, norm_gain.reshape(1, model))
-    usable, route, q_own, cache_own, value_up, out_proj, hidden, gain = pl.pallas_call(
+    usable, route, q_own, cache_own, value_up, out_proj, hidden, gain, gate_z = pl.pallas_call(
         stage_kernel,
         out_shape=(
             pltpu.VMEM((2 * pages_here, rows, PAGE), f32),
             pltpu.VMEM((1, quarter), f32),
             *(pltpu.VMEM(value.shape, value.dtype) for value in large),
+            pltpu.VMEM((split_z, model), bf16),
         ),
-        in_specs=[ANY] * 10,
-        out_specs=[VMEM] * 8,
+        in_specs=[ANY] * 11,
+        out_specs=[VMEM] * 9,
         scratch_shapes=[
             pltpu.SMEM(page_table.shape[::-1], jnp.int32),
             pltpu.SMEM(seq_lens.shape, jnp.int32),
             pltpu.SMEM(expert_ids.shape, jnp.int32),
             pltpu.SMEM(expert_mix.shape, f32),
             pltpu.SemaphoreType.DMA((4,)),
-            pltpu.SemaphoreType.DMA((6,)),
+            pltpu.SemaphoreType.DMA((7,)),
         ],
         compiler_params=limit(4),
         cost_estimate=pl.CostEstimate(flops=0, bytes_accessed=3 * 2**20, transcendentals=0),
         name="stage",
-    )(*on_hbm(page_table.T, seq_lens, expert_ids, expert_mix, *large))
+    )(*on_hbm(page_table.T, seq_lens, expert_ids, expert_mix, *large, gate))
     own, own_lse, far = pl.pallas_call(
         attend_kernel,
         out_shape=(
@@ -436,7 +443,7 @@
         compiler_params=limit(8),
         name="attend",
     )(usable, q_own, q_far, cache_own, cache_near)
-    gate_a, up_a = fetch(far, (gate, (0, split_a)), (up, (0, split_a)))
+    gate_a, up_a = fetch(far, (gate, (split_z, split_a)), (up, (0, up_a_end)))
     far = swap(far, 2)
     piece = jax.ShapeDtypeStruct((ROWS, quarter), bf16)
     mine, near, far_y, far_both = pl.pallas_call(
@@ -448,7 +455,7 @@
         compiler_params=limit(8),
         name="project",
     )(own, own_lse, far, value_up, out_proj, gate_a)
-    gate_b, up_b = fetch(near, (gate, (split_a, split_b)), (up, (split_a, split_b)))
+    gate_b, up_b = fetch(near, (gate, (split_a, split_b)), (up, (up_a_end, split_b)))
     near, far_y, far_both = (
         lax.ppermute(piece, "head", [(n, (n + step) % head_count) for n in range(head_count)])
         for step, piece in ((1, near), (2, far_y), (3, far_both))
@@ -467,7 +474,7 @@
     tokens = lax.all_to_all(spread, both, split_axis=0, concat_axis=0, tiled=True)
     gate_c, up_c = fetch(tokens, (gate, (split_b, split_c)), (up, (split_b, split_c)))
     tokens_near = swap(tokens, 1)
-    ready = (gate_a, up_a, gate_b, up_b, gate_c, up_c)
+    ready = (gate_z, gate_a, up_a, gate_b, up_b, gate_c, up_c)
     theirs, active, down_own = pl.pallas_call(
         functools.partial(expert_kernel, chunk),
         out_shape=(
@@ -475,7 +482,7 @@
             pltpu.VMEM((requests * req_count, units), bf16),
             pltpu.VMEM((units, model // 2), bf16),
         ),
-        in_specs=[VMEM] * 9 + [ANY] * 3,
+        in_specs=[VMEM] * 10 + [ANY] * 3,
         out_specs=[VMEM] * 3,
         scratch_shapes=[
             pltpu.VMEM((model // LANES, ROWS * req_count, LANES), f32),

time: 52.4 us -> 52.3 us (level)
  no operation moved by 1% of the time
where the time goes in v6:
time: 52.3 us; the launch traced here: 52.1 us
  blocking collectives  23.6 us (45%)
  Pallas kernels  20.5 us (39%)
  starting transfers between devices  7.7 us (15%)
    all_to_all x1, blocking collectives, per_device(): lax.all_to_all(spread, both, split_axis=0, concat_axis=0, tiled=True)  13.6 us
    all_to_all x1, blocking collectives, per_device(): parts = lax.all_to_all(parts, both, split_axis=0, concat_axis=0, tiled=True)  10 us
    pallas_call x1, Pallas kernels, per_device(): pl.pallas_call(functools.partial(expert_kernel, chunk), out_shape=(jax.Sh...  8.63 us
    pallas_call x3, Pallas kernels, fetch(): pl.pallas_call(functools.partial(fetch_kernel, spans), out_shape=shapes,...  6.33 us
    ppermute x5, starting transfers between devices, swap(): lax.ppermute(value, 'head', [(n, n ^ flip) for n in range(head_count)])  5.44 us
    ppermute x3, starting transfers between devices, per_device(): lax.ppermute(piece, 'head', [(n, (n + step) % head_count) for n in range(...  2.26 us
    pallas_call x1, Pallas kernels, per_device(): pl.pallas_call(stage_kernel, out_shape=(pltpu.VMEM((2 * pages_here, rows,...  2.26 us
    pallas_call x1, Pallas kernels, per_device(): pl.pallas_call(down_half, out_shape=jax.ShapeDtypeStruct((devices, ROWS,...  1.16 us
  transfers between devices with their start and end apart: 8, of which 1 were waited for; matrix products, arithmetic and copies ran while one was open for 0% of the time, Pallas kernels for 19%

profile of v6, /device:TPU:0, one launch (start us, length us, event | category | flops | bytes accessed | tf_op | source)
XLA Modules:
  0.0 52.1 jit_solution(2885852494403659114)
XLA Ops:
  0.0 0.5 collective-permute-start.1
  0.5 2.5 %collective-permute-start = (bf16[7,4,576]{2,1,0:T(4,128)(2,1)}, bf16[7,4,576]{2,1,0:T(4,128)(2,1)S(1)}, u32[]{:S(2)}, u32[]{:S(2)}) collective-permute-start(bf16[7,4,576]{2,1,0:T(4,128)(2,1)} %refs_4_.1), channel_id=1, source_target_pairs={{0,2},{1,3},{2,0},{3,1},{4,6},{5,7},{6,4},{7,5},{8,10},{9,11},{10,... | collective-permute-start | bytes 96776 | tf_op jit(solution)/shard_map/ppermute | solution.py:374
  3.0 2.3 %stage.1 = (f32[4,64,128]{2,1,0:T(8,128)S(1)}, f32[1,512]{1,0:T(1,128)S(1)}, bf16[7,4,576]{2,1,0:T(4,128)(2,1)S(1)}, bf16[2,576,128]{2,1,0:T(8,128)(2,1)S(1)}, b...) custom-call(s32[2,7]{1,0:T(2,128)} %bitcast.17, ...), custom_call_target="tpu_custom_call" | custom-call | bytes 3145728 | tf_op jit(solution)/shard_map/stage/pallas_call | solution.py:407
  5.2 0.1 collective-permute-done.q_far
  5.3 0.0 collective-permute-done.1.cache_near
  5.3 0.8 %attend.1 = (f32[4,8,512]{2,1,0:T(8,128)S(1)}, f32[4,8,128]{2,1,0:T(8,128)S(1)}, bf16[4,8,640]{2,1,0:T(8,128)(2,1)S(1)}) custom-call(f32[4,64,128]{2,1,0:T(8,128)S(1)} %get-tuple-element.32.usable, bf16[7,4,576]{2,1,0:T(4,128)(2,1)S(1)} %get-tuple-element.33.q_own, bf16[7,4,576]{2,1,0:T(4,128)(2,1)S(1)} %collective-permute-done.q_far, ...), custom_call_target="tpu_custom_call" | custom-call | tf_op jit(solution)/shard_map/attend/pallas_call | solution.py:429
  6.1 1.9 %collective-permute-start.2 = (bf16[4,8,640]{2,1,0:T(8,128)(2,1)S(1)}, bf16[4,8,640]{2,1,0:T(8,128)(2,1)S(1)}, u32[]{:S(2)}, u32[]{:S(2)}) collective-permute-start(bf16[4,8,640]{2,1,0:T(8,128)(2,1)S(1)} %get-tuple-element.37.refs_2_), channel_id=1, source_target_pairs={{0,2},{1,3},{2,0},{3,1},{4,6},{5,7},{6,4},{7,5},{8,10},{9,11},{10,... | collective-permute-start | bytes 122888 | tf_op jit(solution)/shard_map/ppermute | solution.py:374
  8.0 2.2 %fetch.3 = (bf16[512,2048]{1,0:T(8,128)(2,1)S(1)}, bf16[512,2048]{1,0:T(8,128)(2,1)S(1)}) custom-call(bf16[16,176,2048]{2,1,0:T(8,128)(2,1)} %bitcast.6, bf16[16,176,2048]{2,1,0:T(8,128)(2,1)} %bitcast.10, bf16[4,8,640]{2,1,0:T(8,128)(2,1)S(1)} %get-tuple-element.37.refs_2_), custom_call_target="tpu_custom_call" | custom-call | bytes 4194304 | tf_op jit(solution)/shard_map/fetch/pallas_call | solution.py:383
  10.3 0.0 collective-permute-done.2.far
  10.3 0.7 %project.1 = (f32[8,512]{1,0:T(8,128)S(1)}, bf16[8,512]{1,0:T(8,128)(2,1)S(1)}, bf16[8,512]{1,0:T(8,128)(2,1)S(1)}, bf16[8,512]{1,0:T(8,128)(2,1)S(1)}) custom-call(f32[4,8,512]{2,1,0:T(8,128)S(1)} %get-tuple-element.35.own, f32[4,8,128]{2,1,0:T(8,128)S(1)} %get-tuple-element.36.own_lse, bf16[4,8,640]{2,1,0:T(8,128)(2,1)S(1)} %collective-permute-done.2.far, ...), custom_call_target="tpu_custom_call" | custom-call | tf_op jit(solution)/shard_map/project/pallas_call | solution.py:449
  11.0 1.8 %collective-permute-start.4 = (bf16[8,512]{1,0:T(8,128)(2,1)S(1)}, bf16[8,512]{1,0:T(8,128)(2,1)S(1)}, u32[]{:S(2)}, u32[]{:S(2)}) collective-permute-start(bf16[8,512]{1,0:T(8,128)(2,1)S(1)} %get-tuple-element.43), channel_id=1, source_target_pairs={{0,2},{1,3},{2,0},{3,1},{4,6},{5,7},{6,4},{7,5},{8,10},{9,11},{10,... | collective-permute-start | bytes 24584 | tf_op jit(solution)/shard_map/ppermute | solution.py:460
  12.7 0.0 collective-permute-start.5
  12.7 0.5 collective-permute-start.3
  13.2 2.5 %fetch.4 = (bf16[512,2048]{1,0:T(8,128)(2,1)S(1)}, bf16[768,2048]{1,0:T(8,128)(2,1)S(1)}) custom-call(bf16[16,176,2048]{2,1,0:T(8,128)(2,1)} %bitcast.7, bf16[16,176,2048]{2,1,0:T(8,128)(2,1)} %bitcast.11, bf16[8,512]{1,0:T(8,128)(2,1)S(1)} %get-tuple-element.42.refs_2_), custom_call_target="tpu_custom_call" | custom-call | bytes 5242880 | tf_op jit(solution)/shard_map/fetch/pallas_call | solution.py:383
  15.8 0.0 collective-permute-done.4.far_y
  15.8 0.0 collective-permute-done.3.near
  15.8 13.6 %all_to_all.10.refs_2_.tokens = bf16[32,8,256]{2,1,0:T(8,128)(2,1)S(1)} all-to-all(bf16[32,8,256]{2,1,0:T(8,128)(2,1)S(1)} %get-tuple-element.48), channel_id=1, replica_groups=mesh['req'=8,'head'=4] {'req','head'}, dimensions={0} | all-to-all | bytes 262144 | tf_op jit(solution)/shard_map/all_to_all | solution.py:474
  29.4 0.2 collective-permute-start.6
  29.6 1.6 %fetch.5 = (bf16[256,2048]{1,0:T(8,128)(2,1)S(1)}, bf16[256,2048]{1,0:T(8,128)(2,1)S(1)}) custom-call(bf16[16,176,2048]{2,1,0:T(8,128)(2,1)} %bitcast.8, bf16[16,176,2048]{2,1,0:T(8,128)(2,1)} %bitcast.12, bf16[32,8,256]{2,1,0:T(8,128)(2,1)S(1)} %all_to_all.10.refs_2_.tokens), custom_call_target="tpu_custom_call" | custom-call | bytes 2097152 | tf_op jit(solution)/shard_map/fetch/pallas_call | solution.py:383
  31.2 8.6 %experts.1 = (bf16[32,8,256]{2,1,0:T(8,128)(2,1)S(1)}, bf16[56,2816]{1,0:T(8,128)(2,1)S(1)}, bf16[2816,1024]{1,0:T(8,128)(2,1)S(1)}) custom-call(bf16[32,8,256]{2,1,0:T(8,128)(2,1)S(1)} %all_to_all.10.refs_2_.tokens, bf16[32,8,256]{2,1,0:T(8,128)(2,1)S(1)} %collective-permute-done.6.tokens_near, f32[1,2048]{1,0:T(1,128)S(1)} %get-tuple-element.49.gain, ...), custom_call_target="tpu_custom_call" | custom-call | tf_op jit(solution)/shard_map/experts/pallas_call | solution.py:478
  39.9 0.4 collective-permute-start.7
  40.2 1.2 %down.3.mine = f32[32,8,256]{2,1,0:T(8,128)S(1)} custom-call(bf16[56,2816]{1,0:T(8,128)(2,1)S(1)} %get-tuple-element.55.active, bf16[2816,1024]{1,0:T(8,128)(2,1)S(1)} %get-tuple-element.56.weights), custom_call_target="tpu_custom_call" | custom-call | flops 645922816 | bytes 5767168 | tf_op jit(solution)/shard_map/down/pallas_call | solution.py:500
  41.4 10.0 %all_to_all.11.parts = bf16[32,8,256]{2,1,0:T(8,128)(2,1)S(1)} all-to-all(bf16[32,8,256]{2,1,0:T(8,128)(2,1)S(1)} %join.1), channel_id=1, replica_groups=mesh['req'=8,'head'=4] {'req','head'}, dimensions={0} | all-to-all | bytes 262144 | tf_op jit(solution)/shard_map/all_to_all | solution.py:520
  51.4 0.6 %final.1 = bf16[7,512]{1,0:T(8,128)(2,1)} custom-call(bf16[32,8,256]{2,1,0:T(8,128)(2,1)S(1)} %all_to_all.11.parts, f32[7,512]{1,0:T(8,128)S(1)} %get-tuple-element.58.mixed), custom_call_target="tpu_custom_call" | custom-call | tf_op jit(solution)/shard_map/final/pallas_call | solution.py:521
  (5 shorter events, 0.1 us)
Async XLA Ops:
  0.0 5.3 %collective-permute-start.1 = (bf16[2,576,128]{2,1,0:T(8,128)(2,1)}, bf16[2,576,128]{2,1,0:T(8,128)(2,1)S(1)}, u32[]{:S(2)}, u32[]{:S(2)}) collective-permute-start(bf16[2,576,128]{2,1,0:T(8,128)(2,1)} %bitcast.14), channel_id=1, source_target_pairs={{0,1},{1,0},{2,3},{3,2},{4,5},{5,4},{6,7},{7,6},{8,9},{9,8},{10,11... | collective-permute-start | bytes 884744 | tf_op jit(solution)/shard_map/ppermute | solution.py:374
  0.5 4.9 %collective-permute-start = (bf16[7,4,576]{2,1,0:T(4,128)(2,1)}, bf16[7,4,576]{2,1,0:T(4,128)(2,1)S(1)}, u32[]{:S(2)}, u32[]{:S(2)}) collective-permute-start(bf16[7,4,576]{2,1,0:T(4,128)(2,1)} %refs_4_.1), channel_id=1, source_target_pairs={{0,2},{1,3},{2,0},{3,1},{4,6},{5,7},{6,4},{7,5},{8,10},{9,11},{10,... | collective-permute-start | bytes 96776 | tf_op jit(solution)/shard_map/ppermute | solution.py:374
  6.1 4.1 %collective-permute-start.2 = (bf16[4,8,640]{2,1,0:T(8,128)(2,1)S(1)}, bf16[4,8,640]{2,1,0:T(8,128)(2,1)S(1)}, u32[]{:S(2)}, u32[]{:S(2)}) collective-permute-start(bf16[4,8,640]{2,1,0:T(8,128)(2,1)S(1)} %get-tuple-element.37.refs_2_), channel_id=1, source_target_pairs={{0,2},{1,3},{2,0},{3,1},{4,6},{5,7},{6,4},{7,5},{8,10},{9,11},{10,... | collective-permute-start | bytes 122888 | tf_op jit(solution)/shard_map/ppermute | solution.py:374
  11.0 4.8 %collective-permute-start.4 = (bf16[8,512]{1,0:T(8,128)(2,1)S(1)}, bf16[8,512]{1,0:T(8,128)(2,1)S(1)}, u32[]{:S(2)}, u32[]{:S(2)}) collective-permute-start(bf16[8,512]{1,0:T(8,128)(2,1)S(1)} %get-tuple-element.43), channel_id=1, source_target_pairs={{0,2},{1,3},{2,0},{3,1},{4,6},{5,7},{6,4},{7,5},{8,10},{9,11},{10,... | collective-permute-start | bytes 24584 | tf_op jit(solution)/shard_map/ppermute | solution.py:460
  12.7 3.1 %collective-permute-start.5 = (bf16[8,512]{1,0:T(8,128)(2,1)S(1)}, bf16[8,512]{1,0:T(8,128)(2,1)S(1)}, u32[]{:S(2)}, u32[]{:S(2)}) collective-permute-start(bf16[8,512]{1,0:T(8,128)(2,1)S(1)} %get-tuple-element.44), channel_id=1, source_target_pairs={{0,3},{1,0},{2,1},{3,2},{4,7},{5,4},{6,5},{7,6},{8,11},{9,8},{10,9... | collective-permute-start | bytes 24584 | tf_op jit(solution)/shard_map/ppermute | solution.py:460
  12.7 3.1 %collective-permute-start.3 = (bf16[8,512]{1,0:T(8,128)(2,1)S(1)}, bf16[8,512]{1,0:T(8,128)(2,1)S(1)}, u32[]{:S(2)}, u32[]{:S(2)}) collective-permute-start(bf16[8,512]{1,0:T(8,128)(2,1)S(1)} %get-tuple-element.42.refs_2_), channel_id=1, source_target_pairs={{0,1},{1,2},{2,3},{3,0},{4,5},{5,6},{6,7},{7,4},{8,9},{9,10},{10,1... | collective-permute-start | bytes 24584 | tf_op jit(solution)/shard_map/ppermute | solution.py:460
  29.4 1.8 %collective-permute-start.6 = (bf16[32,8,256]{2,1,0:T(8,128)(2,1)S(1)}, bf16[32,8,256]{2,1,0:T(8,128)(2,1)S(1)}, u32[]{:S(2)}, u32[]{:S(2)}) collective-permute-start(bf16[32,8,256]{2,1,0:T(8,128)(2,1)S(1)} %all_to_all.10.refs_2_.tokens), channel_id=1, source_target_pairs={{0,1},{1,0},{2,3},{3,2},{4,5},{5,4},{6,7},{7,6},{8,9},{9,8},{10,11... | collective-permute-start | bytes 393224 | tf_op jit(solution)/shard_map/ppermute | solution.py:374
  39.9 1.5 %collective-permute-start.7 = (bf16[32,8,256]{2,1,0:T(8,128)(2,1)S(1)}, bf16[32,8,256]{2,1,0:T(8,128)(2,1)S(1)}, u32[]{:S(2)}, u32[]{:S(2)}) collective-permute-start(bf16[32,8,256]{2,1,0:T(8,128)(2,1)S(1)} %get-tuple-element.57), channel_id=1, source_target_pairs={{0,1},{1,0},{2,3},{3,2},{4,5},{5,4},{6,7},{7,6},{8,9},{9,8},{10,11... | collective-permute-start | bytes 393224 | tf_op jit(solution)/shard_map/ppermute | solution.py:374

commit v7 on v6

--- a/solution.py
+++ b/solution.py
@@ -197,7 +197,8 @@
     block = jnp.where(row < requests, attn + padded, route[...]).astype(bf16)
     half = spread_out.shape[2]
     for n in range(spread_out.shape[0]):
-        spread_out[n] = block[:, n % 2 * half : (n % 2 + 1) * half]
+        side = n // lax.axis_size("req") % 2
+        spread_out[n] = block[:, side * half : (side + 1) * half]
 
 
 def chunk_groups(first, last, chunk, count):
@@ -260,7 +261,7 @@
     loads = start_all(tuple(pairs), sems)
     for i in range(req_count):
         for j in range(head_count):
-            here, there = (part[i * head_count + j].astype(f32) for part in (tokens, tokens_near))
+            here, there = (part[j * req_count + i].astype(f32) for part in (tokens, tokens_near))
             halves_of = (jnp.where(lower, here, there), jnp.where(lower, there, here))
             block = jnp.concatenate(halves_of, axis=1)
             for c in range(quarter // LANES):
@@ -323,7 +324,7 @@
     for i in range(req_count):
         for j in range(head_count):
             for c in range(wide):
-                out[i * head_count + j, :, c * LANES : (c + 1) * LANES] = total[
+                out[j * req_count + i, :, c * LANES : (c + 1) * LANES] = total[
                     j * wide + c, pl.ds(i, ROWS, stride=req_count), :
                 ].astype(out.dtype)
 
@@ -335,7 +336,8 @@
 def final_kernel(parts, mixed, out):
     halves = []
     for side in range(2):
-        sources = [parts[n].astype(f32) for n in range(side, parts.shape[0], 2)]
+        places = [n for n in range(parts.shape[0]) if n // lax.axis_size("req") % 2 == side]
+        sources = [parts[n].astype(f32) for n in places]
         halves.append(functools.reduce(jnp.add, sources))
     total = jnp.concatenate(halves, axis=1)
     out[...] = (mixed[...] + total[: mixed.shape[0]]).astype(bf16)
@@ -362,7 +364,7 @@
 ):
     head_count = lax.axis_size("head")
     req_count = lax.axis_size("req")
-    both = ("req", "head")
+    both = ("head", "req")
     requests, heads, width = queries.shape
     model = hidden.shape[1]
     quarter = model // head_count

time: 52.3 us -> 51.8 us (level)
  no operation moved by 1% of the time
where the time goes in v7:
time: 51.8 us; the launch traced here: 51.6 us
  blocking collectives  23.1 us (45%)
  Pallas kernels  20.6 us (40%)
  starting transfers between devices  7.69 us (15%)
    all_to_all x1, blocking collectives, per_device(): lax.all_to_all(spread, both, split_axis=0, concat_axis=0, tiled=True)  13.1 us
    all_to_all x1, blocking collectives, per_device(): parts = lax.all_to_all(parts, both, split_axis=0, concat_axis=0, tiled=True)  10 us
    pallas_call x1, Pallas kernels, per_device(): pl.pallas_call(functools.partial(expert_kernel, chunk), out_shape=(jax.Sh...  8.64 us
    pallas_call x3, Pallas kernels, fetch(): pl.pallas_call(functools.partial(fetch_kernel, spans), out_shape=shapes,...  6.33 us
    ppermute x5, starting transfers between devices, swap(): lax.ppermute(value, 'head', [(n, n ^ flip) for n in range(head_count)])  5.43 us
    ppermute x3, starting transfers between devices, per_device(): lax.ppermute(piece, 'head', [(n, (n + step) % head_count) for n in range(...  2.26 us
    pallas_call x1, Pallas kernels, per_device(): pl.pallas_call(stage_kernel, out_shape=(pltpu.VMEM((2 * pages_here, rows,...  2.26 us
    pallas_call x1, Pallas kernels, per_device(): pl.pallas_call(down_half, out_shape=jax.ShapeDtypeStruct((devices, ROWS,...  1.16 us
  transfers between devices with their start and end apart: 8, of which 1 were waited for; matrix products, arithmetic and copies ran while one was open for 0% of the time, Pallas kernels for 19%

profile of v7, /device:TPU:0, one launch (start us, length us, event | category | flops | bytes accessed | tf_op | source)
XLA Modules:
  0.0 51.6 jit_solution(3702086870447950315)
XLA Ops:
  0.0 0.5 collective-permute-start.1
  0.5 2.5 %collective-permute-start = (bf16[7,4,576]{2,1,0:T(4,128)(2,1)}, bf16[7,4,576]{2,1,0:T(4,128)(2,1)S(1)}, u32[]{:S(2)}, u32[]{:S(2)}) collective-permute-start(bf16[7,4,576]{2,1,0:T(4,128)(2,1)} %refs_4_.1), channel_id=1, source_target_pairs={{0,2},{1,3},{2,0},{3,1},{4,6},{5,7},{6,4},{7,5},{8,10},{9,11},{10,... | collective-permute-start | bytes 96776 | tf_op jit(solution)/shard_map/ppermute | solution.py:376
  3.0 2.3 %stage.1 = (f32[4,64,128]{2,1,0:T(8,128)S(1)}, f32[1,512]{1,0:T(1,128)S(1)}, bf16[7,4,576]{2,1,0:T(4,128)(2,1)S(1)}, bf16[2,576,128]{2,1,0:T(8,128)(2,1)S(1)}, b...) custom-call(s32[2,7]{1,0:T(2,128)} %bitcast.17, ...), custom_call_target="tpu_custom_call" | custom-call | bytes 3145728 | tf_op jit(solution)/shard_map/stage/pallas_call | solution.py:409
  5.2 0.1 collective-permute-done.q_far
  5.3 0.8 %attend.1 = (f32[4,8,512]{2,1,0:T(8,128)S(1)}, f32[4,8,128]{2,1,0:T(8,128)S(1)}, bf16[4,8,640]{2,1,0:T(8,128)(2,1)S(1)}) custom-call(f32[4,64,128]{2,1,0:T(8,128)S(1)} %get-tuple-element.32.usable, bf16[7,4,576]{2,1,0:T(4,128)(2,1)S(1)} %get-tuple-element.33.q_own, bf16[7,4,576]{2,1,0:T(4,128)(2,1)S(1)} %collective-permute-done.q_far, ...), custom_call_target="tpu_custom_call" | custom-call | tf_op jit(solution)/shard_map/attend/pallas_call | solution.py:431
  6.1 1.9 %collective-permute-start.2 = (bf16[4,8,640]{2,1,0:T(8,128)(2,1)S(1)}, bf16[4,8,640]{2,1,0:T(8,128)(2,1)S(1)}, u32[]{:S(2)}, u32[]{:S(2)}) collective-permute-start(bf16[4,8,640]{2,1,0:T(8,128)(2,1)S(1)} %get-tuple-element.37.refs_2_), channel_id=1, source_target_pairs={{0,2},{1,3},{2,0},{3,1},{4,6},{5,7},{6,4},{7,5},{8,10},{9,11},{10,... | collective-permute-start | bytes 122888 | tf_op jit(solution)/shard_map/ppermute | solution.py:376
  8.0 2.2 %fetch.3 = (bf16[512,2048]{1,0:T(8,128)(2,1)S(1)}, bf16[512,2048]{1,0:T(8,128)(2,1)S(1)}) custom-call(bf16[16,176,2048]{2,1,0:T(8,128)(2,1)} %bitcast.6, bf16[16,176,2048]{2,1,0:T(8,128)(2,1)} %bitcast.10, bf16[4,8,640]{2,1,0:T(8,128)(2,1)S(1)} %get-tuple-element.37.refs_2_), custom_call_target="tpu_custom_call" | custom-call | bytes 4194304 | tf_op jit(solution)/shard_map/fetch/pallas_call | solution.py:385
  10.3 0.0 collective-permute-done.2.far
  10.3 0.7 %project.1 = (f32[8,512]{1,0:T(8,128)S(1)}, bf16[8,512]{1,0:T(8,128)(2,1)S(1)}, bf16[8,512]{1,0:T(8,128)(2,1)S(1)}, bf16[8,512]{1,0:T(8,128)(2,1)S(1)}) custom-call(f32[4,8,512]{2,1,0:T(8,128)S(1)} %get-tuple-element.35.own, f32[4,8,128]{2,1,0:T(8,128)S(1)} %get-tuple-element.36.own_lse, bf16[4,8,640]{2,1,0:T(8,128)(2,1)S(1)} %collective-permute-done.2.far, ...), custom_call_target="tpu_custom_call" | custom-call | tf_op jit(solution)/shard_map/project/pallas_call | solution.py:451
  11.0 1.8 %collective-permute-start.4 = (bf16[8,512]{1,0:T(8,128)(2,1)S(1)}, bf16[8,512]{1,0:T(8,128)(2,1)S(1)}, u32[]{:S(2)}, u32[]{:S(2)}) collective-permute-start(bf16[8,512]{1,0:T(8,128)(2,1)S(1)} %get-tuple-element.43), channel_id=1, source_target_pairs={{0,2},{1,3},{2,0},{3,1},{4,6},{5,7},{6,4},{7,5},{8,10},{9,11},{10,... | collective-permute-start | bytes 24584 | tf_op jit(solution)/shard_map/ppermute | solution.py:462
  12.7 0.5 collective-permute-start.3
  13.2 2.5 %fetch.4 = (bf16[512,2048]{1,0:T(8,128)(2,1)S(1)}, bf16[768,2048]{1,0:T(8,128)(2,1)S(1)}) custom-call(bf16[16,176,2048]{2,1,0:T(8,128)(2,1)} %bitcast.7, bf16[16,176,2048]{2,1,0:T(8,128)(2,1)} %bitcast.11, bf16[8,512]{1,0:T(8,128)(2,1)S(1)} %get-tuple-element.42.refs_2_), custom_call_target="tpu_custom_call" | custom-call | bytes 5242880 | tf_op jit(solution)/shard_map/fetch/pallas_call | solution.py:385
  15.8 0.0 collective-permute-done.5.far_both
  15.8 0.0 collective-permute-done.3.near
  15.8 13.1 %all_to_all.10.refs_2_.tokens = bf16[32,8,256]{2,1,0:T(8,128)(2,1)S(1)} all-to-all(bf16[32,8,256]{2,1,0:T(8,128)(2,1)S(1)} %get-tuple-element.48), channel_id=1, replica_groups=mesh['req'=8,'head'=4] {'head','req'}, dimensions={0} | all-to-all | bytes 262144 | tf_op jit(solution)/shard_map/all_to_all | solution.py:476
  28.9 0.1 collective-permute-start.6
  29.1 1.6 %fetch.5 = (bf16[256,2048]{1,0:T(8,128)(2,1)S(1)}, bf16[256,2048]{1,0:T(8,128)(2,1)S(1)}) custom-call(bf16[16,176,2048]{2,1,0:T(8,128)(2,1)} %bitcast.8, bf16[16,176,2048]{2,1,0:T(8,128)(2,1)} %bitcast.12, bf16[32,8,256]{2,1,0:T(8,128)(2,1)S(1)} %all_to_all.10.refs_2_.tokens), custom_call_target="tpu_custom_call" | custom-call | bytes 2097152 | tf_op jit(solution)/shard_map/fetch/pallas_call | solution.py:385
  30.6 0.0 collective-permute-done.6.tokens_near
  30.6 8.6 %experts.1 = (bf16[32,8,256]{2,1,0:T(8,128)(2,1)S(1)}, bf16[56,2816]{1,0:T(8,128)(2,1)S(1)}, bf16[2816,1024]{1,0:T(8,128)(2,1)S(1)}) custom-call(bf16[32,8,256]{2,1,0:T(8,128)(2,1)S(1)} %all_to_all.10.refs_2_.tokens, bf16[32,8,256]{2,1,0:T(8,128)(2,1)S(1)} %collective-permute-done.6.tokens_near, f32[1,2048]{1,0:T(1,128)S(1)} %get-tuple-element.49.gain, ...), custom_call_target="tpu_custom_call" | custom-call | tf_op jit(solution)/shard_map/experts/pallas_call | solution.py:480
  39.3 0.5 collective-permute-start.7
  39.7 1.2 %down.3.mine = f32[32,8,256]{2,1,0:T(8,128)S(1)} custom-call(bf16[56,2816]{1,0:T(8,128)(2,1)S(1)} %get-tuple-element.55.active, bf16[2816,1024]{1,0:T(8,128)(2,1)S(1)} %get-tuple-element.56.weights), custom_call_target="tpu_custom_call" | custom-call | flops 645922816 | bytes 5767168 | tf_op jit(solution)/shard_map/down/pallas_call | solution.py:502
  40.9 0.0 collective-permute-done.7.theirs
  41.0 10.0 %all_to_all.11.parts = bf16[32,8,256]{2,1,0:T(8,128)(2,1)S(1)} all-to-all(bf16[32,8,256]{2,1,0:T(8,128)(2,1)S(1)} %join.1), channel_id=1, replica_groups=mesh['req'=8,'head'=4] {'head','req'}, dimensions={0} | all-to-all | bytes 262144 | tf_op jit(solution)/shard_map/all_to_all | solution.py:522
  51.0 0.6 %final.1 = bf16[7,512]{1,0:T(8,128)(2,1)} custom-call(bf16[32,8,256]{2,1,0:T(8,128)(2,1)S(1)} %all_to_all.11.parts, f32[7,512]{1,0:T(8,128)S(1)} %get-tuple-element.58.mixed), custom_call_target="tpu_custom_call" | custom-call | tf_op jit(solution)/shard_map/final/pallas_call | solution.py:523
  (5 shorter events, 0.1 us)
Async XLA Ops:
  0.0 5.3 %collective-permute-start.1 = (bf16[2,576,128]{2,1,0:T(8,128)(2,1)}, bf16[2,576,128]{2,1,0:T(8,128)(2,1)S(1)}, u32[]{:S(2)}, u32[]{:S(2)}) collective-permute-start(bf16[2,576,128]{2,1,0:T(8,128)(2,1)} %bitcast.14), channel_id=1, source_target_pairs={{0,1},{1,0},{2,3},{3,2},{4,5},{5,4},{6,7},{7,6},{8,9},{9,8},{10,11... | collective-permute-start | bytes 884744 | tf_op jit(solution)/shard_map/ppermute | solution.py:376
  0.5 4.9 %collective-permute-start = (bf16[7,4,576]{2,1,0:T(4,128)(2,1)}, bf16[7,4,576]{2,1,0:T(4,128)(2,1)S(1)}, u32[]{:S(2)}, u32[]{:S(2)}) collective-permute-start(bf16[7,4,576]{2,1,0:T(4,128)(2,1)} %refs_4_.1), channel_id=1, source_target_pairs={{0,2},{1,3},{2,0},{3,1},{4,6},{5,7},{6,4},{7,5},{8,10},{9,11},{10,... | collective-permute-start | bytes 96776 | tf_op jit(solution)/shard_map/ppermute | solution.py:376
  6.1 4.1 %collective-permute-start.2 = (bf16[4,8,640]{2,1,0:T(8,128)(2,1)S(1)}, bf16[4,8,640]{2,1,0:T(8,128)(2,1)S(1)}, u32[]{:S(2)}, u32[]{:S(2)}) collective-permute-start(bf16[4,8,640]{2,1,0:T(8,128)(2,1)S(1)} %get-tuple-element.37.refs_2_), channel_id=1, source_target_pairs={{0,2},{1,3},{2,0},{3,1},{4,6},{5,7},{6,4},{7,5},{8,10},{9,11},{10,... | collective-permute-start | bytes 122888 | tf_op jit(solution)/shard_map/ppermute | solution.py:376
  11.0 4.8 %collective-permute-start.4 = (bf16[8,512]{1,0:T(8,128)(2,1)S(1)}, bf16[8,512]{1,0:T(8,128)(2,1)S(1)}, u32[]{:S(2)}, u32[]{:S(2)}) collective-permute-start(bf16[8,512]{1,0:T(8,128)(2,1)S(1)} %get-tuple-element.43), channel_id=1, source_target_pairs={{0,2},{1,3},{2,0},{3,1},{4,6},{5,7},{6,4},{7,5},{8,10},{9,11},{10,... | collective-permute-start | bytes 24584 | tf_op jit(solution)/shard_map/ppermute | solution.py:462
  12.7 3.1 %collective-permute-start.5 = (bf16[8,512]{1,0:T(8,128)(2,1)S(1)}, bf16[8,512]{1,0:T(8,128)(2,1)S(1)}, u32[]{:S(2)}, u32[]{:S(2)}) collective-permute-start(bf16[8,512]{1,0:T(8,128)(2,1)S(1)} %get-tuple-element.44), channel_id=1, source_target_pairs={{0,3},{1,0},{2,1},{3,2},{4,7},{5,4},{6,5},{7,6},{8,11},{9,8},{10,9... | collective-permute-start | bytes 24584 | tf_op jit(solution)/shard_map/ppermute | solution.py:462
  12.7 3.1 %collective-permute-start.3 = (bf16[8,512]{1,0:T(8,128)(2,1)S(1)}, bf16[8,512]{1,0:T(8,128)(2,1)S(1)}, u32[]{:S(2)}, u32[]{:S(2)}) collective-permute-start(bf16[8,512]{1,0:T(8,128)(2,1)S(1)} %get-tuple-element.42.refs_2_), channel_id=1, source_target_pairs={{0,1},{1,2},{2,3},{3,0},{4,5},{5,6},{6,7},{7,4},{8,9},{9,10},{10,1... | collective-permute-start | bytes 24584 | tf_op jit(solution)/shard_map/ppermute | solution.py:462
  28.9 1.7 %collective-permute-start.6 = (bf16[32,8,256]{2,1,0:T(8,128)(2,1)S(1)}, bf16[32,8,256]{2,1,0:T(8,128)(2,1)S(1)}, u32[]{:S(2)}, u32[]{:S(2)}) collective-permute-start(bf16[32,8,256]{2,1,0:T(8,128)(2,1)S(1)} %all_to_all.10.refs_2_.tokens), channel_id=1, source_target_pairs={{0,1},{1,0},{2,3},{3,2},{4,5},{5,4},{6,7},{7,6},{8,9},{9,8},{10,11... | collective-permute-start | bytes 393224 | tf_op jit(solution)/shard_map/ppermute | solution.py:376
  39.3 1.6 %collective-permute-start.7 = (bf16[32,8,256]{2,1,0:T(8,128)(2,1)S(1)}, bf16[32,8,256]{2,1,0:T(8,128)(2,1)S(1)}, u32[]{:S(2)}, u32[]{:S(2)}) collective-permute-start(bf16[32,8,256]{2,1,0:T(8,128)(2,1)S(1)} %get-tuple-element.57), channel_id=1, source_target_pairs={{0,1},{1,0},{2,3},{3,2},{4,5},{5,4},{6,7},{7,6},{8,9},{9,8},{10,11... | collective-permute-start | bytes 393224 | tf_op jit(solution)/shard_map/ppermute | solution.py:376

commit v8 on v7

--- a/solution.py
+++ b/solution.py
@@ -397,7 +397,7 @@
     units = slots * depth
     chunk = units // 11
     split_z, up_a_end = chunk, 2 * chunk
-    split_a, split_b, split_c = 3 * chunk, 5 * chunk, 6 * chunk
+    split_a, split_b, split_c = 3 * chunk, 5 * chunk, 7 * chunk
     gate = jnp.swapaxes(gate_weight, 1, 2)
     up = jnp.swapaxes(up_weight, 1, 2)
     cache = jnp.swapaxes(latent_cache, 1, 2)

time: 51.8 us -> 51.7 us (level)
    pallas_call x1, Pallas kernels: 8.64 us -> 7.9 us  [per_device(): pl.pallas_call(functools.partial(expert_kernel, chunk), out_shape=(jax.Sh...]
    pallas_call x3, Pallas kernels: 6.33 us -> 7.01 us  [fetch(): pl.pallas_call(functools.partial(fetch_kernel, spans), out_shape=shapes,...]
  transfers between devices with their start and end apart: 8 -> 8, of which waited for: 1 -> 1; matrix products, arithmetic and copies ran while one was open for 0% -> 0% of each run, Pallas kernels for 19% -> 20%
where the time goes in v8:
time: 51.7 us; the launch traced here: 51.5 us
  blocking collectives  23.1 us (45%)
  Pallas kernels  20.5 us (40%)
  starting transfers between devices  7.69 us (15%)
    all_to_all x1, blocking collectives, per_device(): lax.all_to_all(spread, both, split_axis=0, concat_axis=0, tiled=True)  13.1 us
    all_to_all x1, blocking collectives, per_device(): parts = lax.all_to_all(parts, both, split_axis=0, concat_axis=0, tiled=True)  10 us
    pallas_call x1, Pallas kernels, per_device(): pl.pallas_call(functools.partial(expert_kernel, chunk), out_shape=(jax.Sh...  7.9 us
    pallas_call x3, Pallas kernels, fetch(): pl.pallas_call(functools.partial(fetch_kernel, spans), out_shape=shapes,...  7.01 us
    ppermute x5, starting transfers between devices, swap(): lax.ppermute(value, 'head', [(n, n ^ flip) for n in range(head_count)])  5.43 us
    ppermute x3, starting transfers between devices, per_device(): lax.ppermute(piece, 'head', [(n, (n + step) % head_count) for n in range(...  2.26 us
    pallas_call x1, Pallas kernels, per_device(): pl.pallas_call(stage_kernel, out_shape=(pltpu.VMEM((2 * pages_here, rows,...  2.26 us
    pallas_call x1, Pallas kernels, per_device(): pl.pallas_call(down_half, out_shape=jax.ShapeDtypeStruct((devices, ROWS,...  1.16 us
  transfers between devices with their start and end apart: 8, of which 1 were waited for; matrix products, arithmetic and copies ran while one was open for 0% of the time, Pallas kernels for 20%

profile of v8, /device:TPU:0, one launch (start us, length us, event | category | flops | bytes accessed | tf_op | source)
XLA Modules:
  0.0 51.5 jit_solution(17157513166406571055)
XLA Ops:
  0.0 0.5 collective-permute-start.1
  0.5 2.5 %collective-permute-start = (bf16[7,4,576]{2,1,0:T(4,128)(2,1)}, bf16[7,4,576]{2,1,0:T(4,128)(2,1)S(1)}, u32[]{:S(2)}, u32[]{:S(2)}) collective-permute-start(bf16[7,4,576]{2,1,0:T(4,128)(2,1)} %refs_4_.1), channel_id=1, source_target_pairs={{0,2},{1,3},{2,0},{3,1},{4,6},{5,7},{6,4},{7,5},{8,10},{9,11},{10,... | collective-permute-start | bytes 96776 | tf_op jit(solution)/shard_map/ppermute | solution.py:376
  3.0 2.3 %stage.1 = (f32[4,64,128]{2,1,0:T(8,128)S(1)}, f32[1,512]{1,0:T(1,128)S(1)}, bf16[7,4,576]{2,1,0:T(4,128)(2,1)S(1)}, bf16[2,576,128]{2,1,0:T(8,128)(2,1)S(1)}, b...) custom-call(s32[2,7]{1,0:T(2,128)} %bitcast.17, ...), custom_call_target="tpu_custom_call" | custom-call | bytes 3145728 | tf_op jit(solution)/shard_map/stage/pallas_call | solution.py:409
  5.2 0.1 collective-permute-done.q_far
  5.3 0.0 collective-permute-done.1.cache_near
  5.3 0.8 %attend.1 = (f32[4,8,512]{2,1,0:T(8,128)S(1)}, f32[4,8,128]{2,1,0:T(8,128)S(1)}, bf16[4,8,640]{2,1,0:T(8,128)(2,1)S(1)}) custom-call(f32[4,64,128]{2,1,0:T(8,128)S(1)} %get-tuple-element.32.usable, bf16[7,4,576]{2,1,0:T(4,128)(2,1)S(1)} %get-tuple-element.33.q_own, bf16[7,4,576]{2,1,0:T(4,128)(2,1)S(1)} %collective-permute-done.q_far, ...), custom_call_target="tpu_custom_call" | custom-call | tf_op jit(solution)/shard_map/attend/pallas_call | solution.py:431
  6.1 1.9 %collective-permute-start.2 = (bf16[4,8,640]{2,1,0:T(8,128)(2,1)S(1)}, bf16[4,8,640]{2,1,0:T(8,128)(2,1)S(1)}, u32[]{:S(2)}, u32[]{:S(2)}) collective-permute-start(bf16[4,8,640]{2,1,0:T(8,128)(2,1)S(1)} %get-tuple-element.37.refs_2_), channel_id=1, source_target_pairs={{0,2},{1,3},{2,0},{3,1},{4,6},{5,7},{6,4},{7,5},{8,10},{9,11},{10,... | collective-permute-start | bytes 122888 | tf_op jit(solution)/shard_map/ppermute | solution.py:376
  8.0 2.2 %fetch.3 = (bf16[512,2048]{1,0:T(8,128)(2,1)S(1)}, bf16[512,2048]{1,0:T(8,128)(2,1)S(1)}) custom-call(bf16[16,176,2048]{2,1,0:T(8,128)(2,1)} %bitcast.6, bf16[16,176,2048]{2,1,0:T(8,128)(2,1)} %bitcast.10, bf16[4,8,640]{2,1,0:T(8,128)(2,1)S(1)} %get-tuple-element.37.refs_2_), custom_call_target="tpu_custom_call" | custom-call | bytes 4194304 | tf_op jit(solution)/shard_map/fetch/pallas_call | solution.py:385
  10.3 0.0 collective-permute-done.2.far
  10.3 0.7 %project.1 = (f32[8,512]{1,0:T(8,128)S(1)}, bf16[8,512]{1,0:T(8,128)(2,1)S(1)}, bf16[8,512]{1,0:T(8,128)(2,1)S(1)}, bf16[8,512]{1,0:T(8,128)(2,1)S(1)}) custom-call(f32[4,8,512]{2,1,0:T(8,128)S(1)} %get-tuple-element.35.own, f32[4,8,128]{2,1,0:T(8,128)S(1)} %get-tuple-element.36.own_lse, bf16[4,8,640]{2,1,0:T(8,128)(2,1)S(1)} %collective-permute-done.2.far, ...), custom_call_target="tpu_custom_call" | custom-call | tf_op jit(solution)/shard_map/project/pallas_call | solution.py:451
  11.0 1.8 %collective-permute-start.4 = (bf16[8,512]{1,0:T(8,128)(2,1)S(1)}, bf16[8,512]{1,0:T(8,128)(2,1)S(1)}, u32[]{:S(2)}, u32[]{:S(2)}) collective-permute-start(bf16[8,512]{1,0:T(8,128)(2,1)S(1)} %get-tuple-element.43), channel_id=1, source_target_pairs={{0,2},{1,3},{2,0},{3,1},{4,6},{5,7},{6,4},{7,5},{8,10},{9,11},{10,... | collective-permute-start | bytes 24584 | tf_op jit(solution)/shard_map/ppermute | solution.py:462
  12.7 0.5 collective-permute-start.3
  13.2 2.5 %fetch.4 = (bf16[512,2048]{1,0:T(8,128)(2,1)S(1)}, bf16[768,2048]{1,0:T(8,128)(2,1)S(1)}) custom-call(bf16[16,176,2048]{2,1,0:T(8,128)(2,1)} %bitcast.7, bf16[16,176,2048]{2,1,0:T(8,128)(2,1)} %bitcast.11, bf16[8,512]{1,0:T(8,128)(2,1)S(1)} %get-tuple-element.42.refs_2_), custom_call_target="tpu_custom_call" | custom-call | bytes 5242880 | tf_op jit(solution)/shard_map/fetch/pallas_call | solution.py:385
  15.8 0.0 collective-permute-done.5.far_both
  15.8 0.0 collective-permute-done.3.near
  15.8 13.1 %all_to_all.10.refs_2_.tokens = bf16[32,8,256]{2,1,0:T(8,128)(2,1)S(1)} all-to-all(bf16[32,8,256]{2,1,0:T(8,128)(2,1)S(1)} %get-tuple-element.48), channel_id=1, replica_groups=mesh['req'=8,'head'=4] {'head','req'}, dimensions={0} | all-to-all | bytes 262144 | tf_op jit(solution)/shard_map/all_to_all | solution.py:476
  28.9 0.1 collective-permute-start.6
  29.1 2.2 %fetch.5 = (bf16[512,2048]{1,0:T(8,128)(2,1)S(1)}, bf16[512,2048]{1,0:T(8,128)(2,1)S(1)}) custom-call(bf16[16,176,2048]{2,1,0:T(8,128)(2,1)} %bitcast.8, bf16[16,176,2048]{2,1,0:T(8,128)(2,1)} %bitcast.12, bf16[32,8,256]{2,1,0:T(8,128)(2,1)S(1)} %all_to_all.10.refs_2_.tokens), custom_call_target="tpu_custom_call" | custom-call | bytes 4194304 | tf_op jit(solution)/shard_map/fetch/pallas_call | solution.py:385
  31.3 0.0 collective-permute-done.6.tokens_near
  31.3 7.9 %experts.1 = (bf16[32,8,256]{2,1,0:T(8,128)(2,1)S(1)}, bf16[56,2816]{1,0:T(8,128)(2,1)S(1)}, bf16[2816,1024]{1,0:T(8,128)(2,1)S(1)}) custom-call(bf16[32,8,256]{2,1,0:T(8,128)(2,1)S(1)} %all_to_all.10.refs_2_.tokens, bf16[32,8,256]{2,1,0:T(8,128)(2,1)S(1)} %collective-permute-done.6.tokens_near, f32[1,2048]{1,0:T(1,128)S(1)} %get-tuple-element.49.gain, ...), custom_call_target="tpu_custom_call" | custom-call | tf_op jit(solution)/shard_map/experts/pallas_call | solution.py:480
  39.2 0.5 collective-permute-start.7
  39.7 1.2 %down.3.mine = f32[32,8,256]{2,1,0:T(8,128)S(1)} custom-call(bf16[56,2816]{1,0:T(8,128)(2,1)S(1)} %get-tuple-element.55.active, bf16[2816,1024]{1,0:T(8,128)(2,1)S(1)} %get-tuple-element.56.weights), custom_call_target="tpu_custom_call" | custom-call | flops 645922816 | bytes 5767168 | tf_op jit(solution)/shard_map/down/pallas_call | solution.py:502
  40.9 10.0 %all_to_all.11.parts = bf16[32,8,256]{2,1,0:T(8,128)(2,1)S(1)} all-to-all(bf16[32,8,256]{2,1,0:T(8,128)(2,1)S(1)} %join.1), channel_id=1, replica_groups=mesh['req'=8,'head'=4] {'head','req'}, dimensions={0} | all-to-all | bytes 262144 | tf_op jit(solution)/shard_map/all_to_all | solution.py:522
  50.9 0.6 %final.1 = bf16[7,512]{1,0:T(8,128)(2,1)} custom-call(bf16[32,8,256]{2,1,0:T(8,128)(2,1)S(1)} %all_to_all.11.parts, f32[7,512]{1,0:T(8,128)S(1)} %get-tuple-element.58.mixed), custom_call_target="tpu_custom_call" | custom-call | tf_op jit(solution)/shard_map/final/pallas_call | solution.py:523
  (5 shorter events, 0.1 us)
Async XLA Ops:
  0.0 5.3 %collective-permute-start.1 = (bf16[2,576,128]{2,1,0:T(8,128)(2,1)}, bf16[2,576,128]{2,1,0:T(8,128)(2,1)S(1)}, u32[]{:S(2)}, u32[]{:S(2)}) collective-permute-start(bf16[2,576,128]{2,1,0:T(8,128)(2,1)} %bitcast.14), channel_id=1, source_target_pairs={{0,1},{1,0},{2,3},{3,2},{4,5},{5,4},{6,7},{7,6},{8,9},{9,8},{10,11... | collective-permute-start | bytes 884744 | tf_op jit(solution)/shard_map/ppermute | solution.py:376
  0.5 4.9 %collective-permute-start = (bf16[7,4,576]{2,1,0:T(4,128)(2,1)}, bf16[7,4,576]{2,1,0:T(4,128)(2,1)S(1)}, u32[]{:S(2)}, u32[]{:S(2)}) collective-permute-start(bf16[7,4,576]{2,1,0:T(4,128)(2,1)} %refs_4_.1), channel_id=1, source_target_pairs={{0,2},{1,3},{2,0},{3,1},{4,6},{5,7},{6,4},{7,5},{8,10},{9,11},{10,... | collective-permute-start | bytes 96776 | tf_op jit(solution)/shard_map/ppermute | solution.py:376
  6.1 4.1 %collective-permute-start.2 = (bf16[4,8,640]{2,1,0:T(8,128)(2,1)S(1)}, bf16[4,8,640]{2,1,0:T(8,128)(2,1)S(1)}, u32[]{:S(2)}, u32[]{:S(2)}) collective-permute-start(bf16[4,8,640]{2,1,0:T(8,128)(2,1)S(1)} %get-tuple-element.37.refs_2_), channel_id=1, source_target_pairs={{0,2},{1,3},{2,0},{3,1},{4,6},{5,7},{6,4},{7,5},{8,10},{9,11},{10,... | collective-permute-start | bytes 122888 | tf_op jit(solution)/shard_map/ppermute | solution.py:376
  11.0 4.8 %collective-permute-start.4 = (bf16[8,512]{1,0:T(8,128)(2,1)S(1)}, bf16[8,512]{1,0:T(8,128)(2,1)S(1)}, u32[]{:S(2)}, u32[]{:S(2)}) collective-permute-start(bf16[8,512]{1,0:T(8,128)(2,1)S(1)} %get-tuple-element.43), channel_id=1, source_target_pairs={{0,2},{1,3},{2,0},{3,1},{4,6},{5,7},{6,4},{7,5},{8,10},{9,11},{10,... | collective-permute-start | bytes 24584 | tf_op jit(solution)/shard_map/ppermute | solution.py:462
  12.7 3.1 %collective-permute-start.5 = (bf16[8,512]{1,0:T(8,128)(2,1)S(1)}, bf16[8,512]{1,0:T(8,128)(2,1)S(1)}, u32[]{:S(2)}, u32[]{:S(2)}) collective-permute-start(bf16[8,512]{1,0:T(8,128)(2,1)S(1)} %get-tuple-element.44), channel_id=1, source_target_pairs={{0,3},{1,0},{2,1},{3,2},{4,7},{5,4},{6,5},{7,6},{8,11},{9,8},{10,9... | collective-permute-start | bytes 24584 | tf_op jit(solution)/shard_map/ppermute | solution.py:462
  12.7 3.1 %collective-permute-start.3 = (bf16[8,512]{1,0:T(8,128)(2,1)S(1)}, bf16[8,512]{1,0:T(8,128)(2,1)S(1)}, u32[]{:S(2)}, u32[]{:S(2)}) collective-permute-start(bf16[8,512]{1,0:T(8,128)(2,1)S(1)} %get-tuple-element.42.refs_2_), channel_id=1, source_target_pairs={{0,1},{1,2},{2,3},{3,0},{4,5},{5,6},{6,7},{7,4},{8,9},{9,10},{10,1... | collective-permute-start | bytes 24584 | tf_op jit(solution)/shard_map/ppermute | solution.py:462
  28.9 2.4 %collective-permute-start.6 = (bf16[32,8,256]{2,1,0:T(8,128)(2,1)S(1)}, bf16[32,8,256]{2,1,0:T(8,128)(2,1)S(1)}, u32[]{:S(2)}, u32[]{:S(2)}) collective-permute-start(bf16[32,8,256]{2,1,0:T(8,128)(2,1)S(1)} %all_to_all.10.refs_2_.tokens), channel_id=1, source_target_pairs={{0,1},{1,0},{2,3},{3,2},{4,5},{5,4},{6,7},{7,6},{8,9},{9,8},{10,11... | collective-permute-start | bytes 393224 | tf_op jit(solution)/shard_map/ppermute | solution.py:376
  39.2 1.6 %collective-permute-start.7 = (bf16[32,8,256]{2,1,0:T(8,128)(2,1)S(1)}, bf16[32,8,256]{2,1,0:T(8,128)(2,1)S(1)}, u32[]{:S(2)}, u32[]{:S(2)}) collective-permute-start(bf16[32,8,256]{2,1,0:T(8,128)(2,1)S(1)} %get-tuple-element.57), channel_id=1, source_target_pairs={{0,1},{1,0},{2,3},{3,2},{4,5},{5,4},{6,7},{7,6},{8,9},{9,8},{10,11... | collective-permute-start | bytes 393224 | tf_op jit(solution)/shard_map/ppermute | solution.py:376
